TPU v7x, 32 devices: a whole 2x2x4 slice. The times are simulated.
32 devices in a mesh: dp: 1, context: 16 (over z, y, x), tensor: 2 (over core).
Axes of the slice: x: 2, y: 2, z: 4, core: 2. Of those that a mesh axis runs over, the one named last changes fastest.
Arguments:
- queries: bfloat16 [1, 2048, 4096], P('dp', 'context', 'tensor'), may hold values from -30 to 30
- keys: bfloat16 [1, 2048, 256], P('dp', 'context', 'tensor'), may hold values from -4 to 4
- values: bfloat16 [1, 2048, 256], P('dp', 'context', 'tensor'), may hold values from -6 to 6
- outputs: bfloat16 [1, 2048, 4096], P('dp', 'context', 'tensor'), may hold values from -6 to 6
- grad_out: bfloat16 [1, 2048, 4096], P('dp', 'context', 'tensor'), may hold values from -24 to 24
- inputs: bfloat16 [1, 2048, 16384], P('dp', ('context', 'tensor')), may hold values from -1.5 to 1.5
- block_doc: int32 [1, 16], P('dp'), may hold values from 0 to 3, never falling along the last dimension, each value on 1 to 8 neighbouring positions
- span_slots: int32 [32], replicated, may hold values from 0 to 31, as said below
Outputs:
- grad_queries: bfloat16 [1, 2048, 4096], P('dp', 'context', 'tensor')
- grad_key_weight: float32 [16384, 256], P('context', 'tensor')
- grad_value_weight: float32 [16384, 256], P('context', 'tensor')
Inputs may be any that keep to these rules, and one draw needn't show every extreme that they name: span_slots is a permutation; slots 2 d and 2 d + 1 hold two spans c and 31 - c.
All inputs are finite; a program needn't handle non-finite values.
Results may differ from a plain program's by a relative error of at most 0.0065.
Values may be sent and summed in bfloat16 or wider, within the bound.
No kernel may reach another device: no remote copies, remote signals or barrier semaphores. Data moves between devices by JAX's collectives and lax.ppermute only.
A program may use at most 64 MiB of HBM per device.

v0:
```python
import math

import jax
import jax.numpy as jnp
from jax import lax
from jax.sharding import PartitionSpec as P


def table_lookup(entries, positions):
    matches = positions[..., None] == jnp.arange(entries.shape[-1], dtype=jnp.int32)
    return jnp.sum(jnp.where(matches, entries, 0), axis=-1)


def on_device(queries, keys, values, outputs, grad_out, inputs, block_doc, span_slots):
    batch_count, row_count, query_width = queries.shape
    head_size = keys.shape[2]
    group_size = query_width // head_size
    slot_count = span_slots.shape[0]
    span_rows = row_count // 2
    total_rows = span_rows * slot_count
    block_tokens = total_rows // block_doc.shape[1]
    key_block = min(512, total_rows)
    block_count = total_rows // key_block
    scaling = 1.0 / math.sqrt(head_size)
    my_index = lax.axis_index("context")
    offsets = jnp.arange(row_count, dtype=jnp.int32)
    query_position = (
        table_lookup(span_slots, 2 * my_index + offsets // span_rows) * span_rows
        + offsets % span_rows
    )
    query_document = table_lookup(block_doc[:, None, :], (query_position // block_tokens)[None, :])
    key_document = jnp.repeat(block_doc, block_tokens, axis=1)
    slot_index = jnp.arange(slot_count, dtype=jnp.int32)
    inverse = jnp.sum(
        jnp.where(span_slots[None, :] == slot_index[:, None], slot_index[None, :], 0), axis=1
    )
    gathered_keys, gathered_values = (
        lax.all_gather(keys, "context", axis=1, tiled=True),
        lax.all_gather(values, "context", axis=1, tiled=True),
    )
    key_rows = gathered_keys.reshape(batch_count, slot_count, span_rows, head_size)[
        :, inverse
    ].reshape(batch_count, total_rows, head_size)
    value_rows = gathered_values.reshape(batch_count, slot_count, span_rows, head_size)[
        :, inverse
    ].reshape(batch_count, total_rows, head_size)
    query_head_rows = queries.reshape(batch_count, row_count, group_size, head_size)
    gradient_heads = grad_out.reshape(batch_count, row_count, group_size, head_size)
    output_heads = outputs.reshape(batch_count, row_count, group_size, head_size)
    row_delta = jnp.einsum(
        "bqgd,bqgd->bgq", gradient_heads, output_heads, preferred_element_type=jnp.float32
    )[..., None]

    def block_mask(block_start):
        key_position = block_start + jnp.arange(key_block, dtype=jnp.int32)
        key_portion = lax.dynamic_slice_in_dim(key_document, block_start, key_block, 1)
        causal = key_position[None, None, :] <= query_position[None, :, None]
        same_document = key_portion[:, None, :] == query_document[:, :, None]
        return (causal & same_document)[:, None]

    def block_scores(key_portion):
        return (
            jnp.einsum(
                "xztw,xjw->xtzj", query_head_rows, key_portion, preferred_element_type=jnp.float32
            )
            * scaling
        )

    def first_pass(state, block_number):
        block_start = block_number * key_block
        allowed = block_mask(block_start)
        running_max, running_sum = state
        key_portion = lax.dynamic_slice_in_dim(key_rows, block_start, key_block, 1)
        scores = block_scores(key_portion)
        new_max = jnp.maximum(running_max, jnp.max(jnp.where(allowed, scores, -1e30), axis=3))
        weights = jnp.where(allowed, jnp.exp(scores - new_max[..., None]), 0.0)
        return (
            (new_max, running_sum * jnp.exp(running_max - new_max) + jnp.sum(weights, axis=3)),
            None,
        )

    start_max = jnp.full((batch_count, group_size, row_count), -1e30, jnp.float32)
    (running_max, running_sum), unused = lax.scan(
        first_pass, (start_max, jnp.zeros_like(start_max)), jnp.arange(block_count)
    )
    log_norm = (running_max + jnp.log(running_sum))[..., None]

    def second_pass(query_grad, block_number):
        block_start = block_number * key_block
        allowed = block_mask(block_start)
        carried = query_grad
        key_portion = lax.dynamic_slice_in_dim(key_rows, block_start, key_block, 1)
        value_portion = lax.dynamic_slice_in_dim(value_rows, block_start, key_block, 1)
        scores = block_scores(key_portion)
        attention = jnp.where(allowed, jnp.exp(scores - log_norm), 0.0)
        attention_lowered = attention.astype(jnp.bfloat16)
        value_grad = jnp.einsum(
            "elcj,ecla->eja", attention_lowered, gradient_heads, preferred_element_type=jnp.float32
        )
        attention_grad = jnp.einsum(
            "xztw,xjw->xtzj", gradient_heads, value_portion, preferred_element_type=jnp.float32
        )
        score_gradient = (attention * (attention_grad - row_delta)).astype(jnp.bfloat16)
        carried = carried + jnp.einsum(
            "lseu,luv->lesv", score_gradient, key_portion, preferred_element_type=jnp.float32
        )
        key_grad = (
            jnp.einsum(
                "elcj,ecla->eja",
                score_gradient,
                query_head_rows,
                preferred_element_type=jnp.float32,
            )
            * scaling
        )
        return (carried, jnp.concatenate([key_grad, value_grad], axis=2))

    start_grad = jnp.zeros((batch_count, row_count, group_size, head_size), jnp.float32)
    query_grad, block_grads = lax.scan(second_pass, start_grad, jnp.arange(block_count))
    grad_queries = (
        (query_grad * scaling).astype(jnp.bfloat16).reshape(batch_count, row_count, query_width)
    )
    position_grads = jnp.moveaxis(block_grads, 0, 1).reshape(
        batch_count, slot_count, span_rows, 2 * head_size
    )
    stored_grads = position_grads[:, span_slots].reshape(batch_count, total_rows, 2 * head_size)
    local_grads = lax.psum_scatter(stored_grads, "context", scatter_dimension=1, tiled=True)
    grads_low = local_grads.astype(jnp.bfloat16)
    token_rows = lax.all_gather(inputs, "tensor", axis=1, tiled=True)
    shares = lax.psum_scatter(
        jnp.einsum("bnd,bne->de", token_rows, grads_low, preferred_element_type=jnp.float32),
        "context",
        scatter_dimension=0,
        tiled=True,
    )
    summed = lax.psum(shares, "dp")
    return (grad_queries, summed[:, :head_size], summed[:, head_size:])


def solution(mesh):
    in_specs = (
        P("dp", "context", "tensor"),
        P("dp", "context", "tensor"),
        P("dp", "context", "tensor"),
        P("dp", "context", "tensor"),
        P("dp", "context", "tensor"),
        P("dp", ("context", "tensor"), None),
        P("dp", None),
        P(),
    )
    out_specs = (P("dp", "context", "tensor"), P("context", "tensor"), P("context", "tensor"))
    return jax.shard_map(
        on_device, mesh=mesh, in_specs=in_specs, out_specs=out_specs, check_vma=False
    )
```

profile of v0, /device:TPU:0, one launch (start us, length us, event | category | flops | bytes accessed | tf_op | source)
XLA Modules:
  0.0 592.2 jit_solution(16975515604377176983)
XLA Ops:
  10.4 1.3 copy.42
  12.0 45.3 %all_gather.9 = bf16[1,2048,128]{2,1,0:T(8,128)(2,1)S(1)} all-gather(bf16[1,128,128]{2,1,0:T(8,128)(2,1)S(1)} %copy-done.2), channel_id=1, replica_groups=mesh['dp'=1,'context'=16,'tensor'=2] {'context'}, dimensions={1}, use_global_device_ids=true | all-gather | bytes 557056 | tf_op jit(solution)/shard_map/all_gather | solution.py:38
  58.2 12.6 %while.26 = (s32[]{:T(128)}, f32[1,16,128]{2,1,0:T(8,128)S(1)}, f32[1,16,128]{2,1,0:T(8,128)S(1)}, s32[4]{0:T(128)S(1)}, s32[128]{0:T(128)S(1)}, /*index=5*/s32[...) while((s32[]{:T(128)}, f32[1,16,128]{2,1,0:T(8,128)S(1)}, ...), condition=%wide.region_6.7_spmd.clone, body=%wide.region_3.6_spmd.clone.sunk | while | flops 275982848 | bytes 9358550 | solution.py:83
  60.4 0.8 fusion.83
  63.6 0.8 fusion.83
  66.7 0.8 fusion.83
  69.9 0.8 fusion.83
  70.8 38.5 %all_gather.10 = bf16[1,2048,128]{2,1,0:T(8,128)(2,1)S(1)} all-gather(bf16[1,128,128]{2,1,0:T(8,128)(2,1)S(1)} %copy-done.3), channel_id=1, replica_groups=mesh['dp'=1,'context'=16,'tensor'=2] {'context'}, dimensions={1}, use_global_device_ids=true | all-gather | bytes 557056 | tf_op jit(solution)/shard_map/all_gather | solution.py:39
  109.3 1.4 gather_fusion.1
  110.7 1.1 copy.68
  111.8 1.0 copy.44
  113.4 32.2 %while.27 = (s32[]{:T(128)}, f32[1,128,16,128]{1,3,2,0:T(8,128)S(1)}, f32[4,1,512,256]{3,2,0,1:T(8,128)}, s32[4]{0:T(128)S(1)}, bf16[1,2048,128]{2,1,0:T(8,128)(...) while((s32[]{:T(128)}, ...), condition=%wide.region_8.9_spmd.clone, body=%wide.region_7.8_spmd.clone.sunk | while | flops 1353581056 | bytes 29461788 | solution.py:119
  115.8 0.9 fusion.97
  116.7 2.2 fusion.95
  120.6 0.8 constant_dynamic-update-slice_fusion.2
  123.8 1.0 fusion.97
  124.7 2.2 fusion.95
  128.7 0.9 constant_dynamic-update-slice_fusion.2
  131.8 0.9 fusion.97
  132.8 2.2 fusion.95
  136.7 0.8 constant_dynamic-update-slice_fusion.2
  139.8 1.0 fusion.97
  140.8 2.2 fusion.95
  144.7 0.9 constant_dynamic-update-slice_fusion.2
  145.6 3.6 gather_fusion.2
  149.3 78.2 %reduce-scatter.3.cloned.1.call-done = f32[1,128,256]{2,1,0:T(8,128)} async-done(((f32[1,2048,256]{2,1,0:T(8,128)}), f32[1,128,256]{2,1,0:T(8,128)}) %reduce-scatter.3.cloned.1.call-update) | async-done | bytes 131088 | tf_op jit(solution)/shard_map/reduce_scatter | solution.py:127
  227.6 10.3 %convolution_bitcast_fusion = f32[16384,256]{0,1:T(8,128)} fusion(bf16[1,128,16384]{2,1,0:T(8,128)(2,1)} %all-gather.2.cloned.1.call-done, f32[1,128,256]{2,1,0:T(8,128)} %reduce-scatter.3.cloned.1.call-done), kind=kOutput, calls=%fused_computation.61 | convolution fusion | flops 1073774592 | bytes 21102592 | tf_op jit(solution)/shard_map/bnd,bne->de/dot_general | solution.py:131
  238.1 1.0 copy.63
  239.1 342.4 %reduce-scatter.5.cloned.1.call-done = f32[1024,256]{0,1:T(8,128)} async-done(((f32[16384,256]{0,1:T(8,128)}), f32[1024,256]{0,1:T(8,128)}) %reduce-scatter.5.cloned.1.call-update) | async-done | bytes 1048592 | tf_op jit(solution)/shard_map/reduce_scatter | solution.py:130
  581.5 1.3 fusion.64
  582.8 1.0 copy.48
  583.8 1.0 copy.47
  (116 shorter events, 23.4 us)
Async XLA Ops:
  8.0 4.0 copy-start.2
  8.0 49.4 %copy-start.4 = (s32[1,16]{1,0:T(1,128)S(1)}, s32[1,16]{1,0:T(1,128)}, u32[]{:S(2)}) copy-start(s32[1,16]{1,0:T(1,128)} %param.18) | copy-start | bytes 196
  8.0 141.3 %all-gather.2.cloned.1.call-start = ((), (), s32[]{:S(2)}) async-start(), calls=%async_computation.3 | async-start | bytes 6291456 | tf_op jit(solution)/shard_map/all_gather | solution.py:129
  8.8 218.8 %reduce-scatter.3.cloned.1.call-start = ((), (), s32[]{:S(2)}) async-start(), calls=%async_computation.2 | async-start | bytes 2228224 | tf_op jit(solution)/shard_map/reduce_scatter | solution.py:127
  58.2 12.6 %copy-start.3 = (bf16[1,128,128]{2,1,0:T(8,128)(2,1)S(1)}, bf16[1,128,128]{2,1,0:T(8,128)(2,1)}, u32[]{:S(2)}) copy-start(bf16[1,128,128]{2,1,0:T(8,128)(2,1)} %param.14) | copy-start | bytes 98308
  58.2 53.6 %copy-start = (bf16[1,128,2048]{2,1,0:T(8,128)(2,1)S(1)}, bf16[1,128,2048]{2,1,0:T(8,128)(2,1)}, u32[]{:S(2)}) copy-start(bf16[1,128,2048]{2,1,0:T(8,128)(2,1)} %param.16) | copy-start | bytes 1572868
  113.4 32.2 %copy-start.5 = (s32[32]{0:T(128)S(1)}, s32[32]{0:T(128)}, u32[]{:S(2)}) copy-start(s32[32]{0:T(128)} %param.19) | copy-start | bytes 388
  113.4 2.3 copy-start.1
  121.5 2.3 copy-start.1
  129.5 2.3 copy-start.1
  137.5 2.3 copy-start.1
  149.2 432.3 %reduce-scatter.5.cloned.1.call-start = ((), (), s32[]{:S(2)}) async-start(), calls=%async_computation.4 | async-start | bytes 17825792 | tf_op jit(solution)/shard_map/reduce_scatter | solution.py:130
Sparse Core Ops, SparseCore 0:
  10.4 16.3 all-gather.1
Sparse Core Ops, SparseCore 1:
  149.3 78.2 reduce-scatter.2
  238.0 343.5 reduce-scatter.4
where the time goes:
time: 597 us; the launch traced here: 592 us
  waiting for transfers between devices  421 us (71%)
  blocking collectives  83.8 us (14%)
  matrix products  34.5 us (6%)
  local copies, waits for them, and re-layouts  23.2 us (4%)
  between operations  15.7 us (3%)
  other arithmetic  7.41 us (1%)
  loops' own time  6.04 us (1%)
    reduce_scatter x1, waiting for transfers between devices, on_device(): lax.psum_scatter(jnp.einsum('bnd,bne->de', token_rows, grads_low, preferr...  342 us
    reduce_scatter x1, waiting for transfers between devices, on_device(): lax.psum_scatter(stored_grads, 'context', scatter_dimension=1, tiled=True)  78.2 us
    all_gather x1, blocking collectives, on_device(): lax.all_gather(keys, 'context', axis=1, tiled=True)  45.3 us
    all_gather x1, blocking collectives, on_device(): lax.all_gather(values, 'context', axis=1, tiled=True)  38.5 us
  transfers between devices with their start and end apart: 3, of which 2 were waited for; matrix products, arithmetic and copies ran while one was open for 9% of the time, Pallas kernels for 0%

commit v1 on v0

v1 whole, which is shorter than its diff:
```python
import functools
import math

import jax
import jax.numpy as jnp
from jax import lax
from jax.experimental import pallas as pl
from jax.experimental.pallas import tpu as pltpu
from jax.sharding import PartitionSpec as P

NT = (((1,), (1,)), ((), ()))
NN = (((1,), (0,)), ((), ()))
TN = (((0,), (0,)), ((), ()))

LOW = 4


def dot(left, right, dims):
    return lax.dot_general(left, right, dims, preferred_element_type=jnp.float32)


def swap(value, offset, count):
    return lax.ppermute(value, "context", [(i, i ^ offset) for i in range(count)])


def attention_kernel(
    me, slots, docs, q_ref, do_ref, delta_ref, *refs, low, span_rows, block_tokens, chunk, heads, head,
):
    kv_refs, (dq_ref, *dkv_refs), scratch = refs[:low], refs[low : 2 * low + 1], refs[2 * low + 1 :]
    k_pos, v_pos, q_rows, do_rows, scores, grads, query_grad = scratch
    slot_count = slots.shape[0]
    block_count = docs.shape[0]
    total = span_rows * slot_count
    lanes = heads * span_rows
    scaling = 1.0 / math.sqrt(head)
    log2e = 1.4426950408889634
    own = me[0]

    def spans_of_pieces():
        for r in range(slot_count // 2):
            for half in range(2):
                span = slots[2 * (own ^ r) + half]
                place = pl.ds(pl.multiple_of(span * span_rows, span_rows), span_rows)
                yield r % low, pl.ds((2 * (r // low) + half) * span_rows, span_rows), place

    for piece, rows, place in spans_of_pieces():
        k_pos[place, :] = kv_refs[piece][rows, :head]
        v_pos[place, :] = kv_refs[piece][rows, head:]
    k_pos[total:, :] = jnp.zeros((chunk, head), k_pos.dtype)
    v_pos[total:, :] = jnp.zeros((chunk, head), v_pos.dtype)
    grads[...] = jnp.zeros_like(grads)

    for local in range(2):
        span = slots[2 * own + local]
        document = docs[span * span_rows // block_tokens]
        first_block = lax.fori_loop(
            0, block_count, lambda b, n: n + (docs[b] < document).astype(jnp.int32), jnp.int32(0)
        )
        first = first_block * block_tokens
        chunks = ((span + 1) * span_rows - first + chunk - 1) // chunk
        for h in range(heads):
            source = (slice(local * span_rows, (local + 1) * span_rows), slice(h * head, (h + 1) * head))
            q_rows[h * span_rows : (h + 1) * span_rows, :] = q_ref[source]
            do_rows[h * span_rows : (h + 1) * span_rows, :] = do_ref[source]

        def key_place(i):
            return pl.ds(pl.multiple_of(first + i * chunk, span_rows), chunk)

        def score_place(i):
            return pl.ds(pl.multiple_of(i * chunk, chunk), chunk)

        row_in_span = lax.broadcasted_iota(jnp.int32, (chunk, lanes), 1) % span_rows
        key_in_chunk = lax.broadcasted_iota(jnp.int32, (chunk, lanes), 0)
        ahead = key_in_chunk - row_in_span

        def raw_scores(i, largest):
            found = dot(k_pos[key_place(i), :], q_rows[...], NT)
            found = jnp.where(ahead <= span * span_rows - first - i * chunk, found, -1e30)
            scores[score_place(i), :] = found
            return jnp.maximum(largest, jnp.max(found.reshape(chunk // 8, 8, lanes), axis=0))

        largest = lax.fori_loop(0, chunks, raw_scores, jnp.full((8, lanes), -1e30, jnp.float32))
        largest = jnp.max(largest, axis=0, keepdims=True)

        def weigh(i, total_weight):
            weight = jnp.exp2((scores[score_place(i), :] - largest) * (scaling * log2e))
            scores[score_place(i), :] = weight
            return total_weight + jnp.sum(weight.reshape(chunk // 8, 8, lanes), axis=0)

        weight_sum = lax.fori_loop(0, chunks, weigh, jnp.zeros((8, lanes), jnp.float32))
        inverse = 1.0 / jnp.sum(weight_sum, axis=0, keepdims=True)
        delta = delta_ref[local]

        query_grad[...] = jnp.zeros_like(query_grad)

        def gradients(i, carry):
            attention = scores[score_place(i), :] * inverse
            attention_grad = dot(v_pos[key_place(i), :], do_rows[...], NT)
            score_grad = (attention * (attention_grad - delta)).astype(jnp.bfloat16)
            keys = k_pos[key_place(i), :]
            grads[key_place(i), :head] += dot(score_grad, q_rows[...], NN)
            grads[key_place(i), head:] += dot(attention.astype(jnp.bfloat16), do_rows[...], NN)
            query_grad[...] += dot(keys, score_grad, TN)
            return carry

        lax.fori_loop(0, chunks, gradients, 0)
        turned = (query_grad[...] * scaling).T.astype(dq_ref.dtype)
        for h in range(heads):
            dq_ref[local * span_rows : (local + 1) * span_rows, h * head : (h + 1) * head] = turned[
                h * span_rows : (h + 1) * span_rows, :
            ]

    for piece, rows, place in spans_of_pieces():
        dkv_refs[piece][rows, :head] = (grads[place, :head] * scaling).astype(jnp.bfloat16)
        dkv_refs[piece][rows, head:] = grads[place, head:].astype(jnp.bfloat16)


def attention_grads(me, slots, docs, queries, grad_out, delta, key_values, head, block_tokens):
    rows, width = queries.shape
    low = len(key_values)
    total = low * key_values[0].shape[0]
    heads = width // head
    span_rows = rows // 2
    chunk = min(256, total)
    vmem = pl.BlockSpec(memory_space=pltpu.VMEM)
    smem = pl.BlockSpec(memory_space=pltpu.SMEM)
    lanes = heads * span_rows
    body = functools.partial(
        attention_kernel, low=low, span_rows=span_rows, block_tokens=block_tokens, chunk=chunk, heads=heads, head=head
    )
    return pl.pallas_call(
        body,
        out_shape=(
            jax.ShapeDtypeStruct((rows, width), jnp.bfloat16),
            *(jax.ShapeDtypeStruct((total // low, 2 * head), jnp.bfloat16) for _ in range(low)),
        ),
        in_specs=[smem, smem, smem, vmem, vmem, vmem] + [vmem] * low,
        out_specs=(vmem,) * (low + 1),
        scratch_shapes=[
            pltpu.VMEM((total + chunk, head), jnp.bfloat16),
            pltpu.VMEM((total + chunk, head), jnp.bfloat16),
            pltpu.VMEM((lanes, head), jnp.bfloat16),
            pltpu.VMEM((lanes, head), jnp.bfloat16),
            pltpu.VMEM((total + chunk, lanes), jnp.float32),
            pltpu.VMEM((total + chunk, 2 * head), jnp.float32),
            pltpu.VMEM((head, lanes), jnp.float32),
        ],
        compiler_params=pltpu.CompilerParams(vmem_limit_bytes=48 << 20),
        name="attention_grads",
    )(me, slots, docs, queries, grad_out, delta, *key_values)


def turned_columns(me, halves, rows, column_count):
    count = halves[0].shape[0]
    spec = pl.BlockSpec((1, rows, column_count), lambda r, me: (me[0] ^ r, 0, 0))
    tensor_count = len(halves)

    def body(me, *refs):
        both = jnp.concatenate([ref[0] for ref in refs[:-1]], axis=0)
        refs[-1][...] = both.T

    return pl.pallas_call(
        body,
        out_shape=jax.ShapeDtypeStruct((column_count, count * tensor_count * rows), jnp.bfloat16),
        grid_spec=pltpu.PrefetchScalarGridSpec(
            num_scalar_prefetch=1,
            grid=(count,),
            in_specs=[spec] * tensor_count,
            out_specs=pl.BlockSpec((column_count, tensor_count * rows), lambda r, me: (0, r)),
        ),
        name="turned_columns",
    )(me, *halves)


def on_device(queries, keys, values, outputs, grad_out, inputs, block_doc, span_slots):
    batch_count, row_count, query_width = queries.shape
    head = keys.shape[2]
    heads = query_width // head
    span_rows = row_count // 2
    total = span_rows * span_slots.shape[0]
    block_tokens = total // block_doc.shape[1]
    count = total // row_count
    low = min(LOW, count)
    high = count // low
    token_rows = inputs.shape[1]
    tensor_count = row_count // token_rows
    column_count = inputs.shape[2] // count
    me = lax.axis_index("context").astype(jnp.int32).reshape(1)

    sent = inputs.reshape(batch_count, token_rows, count, column_count)
    sent = jnp.moveaxis(sent, 2, 0).reshape(count, batch_count * token_rows, column_count)
    mine = lax.all_to_all(sent, "context", split_axis=0, concat_axis=0, tiled=True)
    tensor_index = lax.axis_index("tensor")
    if tensor_count == 2:
        other = lax.ppermute(mine, "tensor", [(0, 1), (1, 0)])
        halves = [jnp.where(tensor_index == 0, mine, other), jnp.where(tensor_index == 0, other, mine)]
    else:
        every = lax.all_gather(mine, "tensor", axis=0)
        halves = [every[t] for t in range(tensor_count)]

    own = jnp.concatenate([keys, values], axis=2)
    column = jnp.concatenate([own] + [swap(own, k * low, count) for k in range(1, high)], axis=1)
    key_values = [column] + [swap(column, k, count) for k in range(1, low)]

    delta = jnp.einsum(
        "bqgd,bqgd->bgq",
        grad_out.reshape(batch_count, row_count, heads, head),
        outputs.reshape(batch_count, row_count, heads, head),
        preferred_element_type=jnp.float32,
    )
    delta = delta.reshape(batch_count, heads, 2, span_rows).swapaxes(1, 2).reshape(batch_count, 2, 1, heads * span_rows)

    query_grads, weight_grads = [], []
    for b in range(batch_count):
        query_grad, *partials = attention_grads(
            me, span_slots, block_doc[b], queries[b], grad_out[b], delta[b], [kv[b] for kv in key_values], head, block_tokens
        )
        query_grads.append(query_grad)
        arrived = [partials[0]] + [swap(partials[k], k, count) for k in range(1, low)]
        sums = sum(p.astype(jnp.float32) for p in arrived)
        pieces = [sums[k * row_count : (k + 1) * row_count] for k in range(high)]
        arrived = [pieces[0]] + [swap(pieces[k].astype(jnp.bfloat16), k * low, count) for k in range(1, high)]
        own_grads = sum(p.astype(jnp.float32) for p in arrived).astype(jnp.bfloat16)
        column = jnp.concatenate([own_grads] + [swap(own_grads, k * low, count) for k in range(1, high)], axis=0)
        columns = [column] + [swap(column, k, count) for k in range(1, low)]
        all_grads = jnp.stack([c.reshape(high, row_count, 2 * head) for c in columns], axis=1).reshape(total, 2 * head)
        own_halves = [h[:, b * token_rows : (b + 1) * token_rows] for h in halves]
        turned = turned_columns(me, own_halves, token_rows, column_count)
        weight_grads.append(dot(turned, all_grads, NN))
    summed = lax.psum(sum(weight_grads), "dp")
    return jnp.stack(query_grads), summed[:, :head], summed[:, head:]


def solution(mesh):
    in_specs = (
        P("dp", "context", "tensor"),
        P("dp", "context", "tensor"),
        P("dp", "context", "tensor"),
        P("dp", "context", "tensor"),
        P("dp", "context", "tensor"),
        P("dp", ("context", "tensor"), None),
        P("dp", None),
        P(),
    )
    out_specs = (P("dp", "context", "tensor"), P("context", "tensor"), P("context", "tensor"))
    return jax.shard_map(on_device, mesh=mesh, in_specs=in_specs, out_specs=out_specs, check_vma=False)
```

time: 597 us -> 155 us (0.26)
  waiting for transfers between devices: 421 us -> 83.9 us
  blocking collectives: 83.8 us -> 0 us
  starting transfers between devices: 0.12 us -> 36.3 us
  matrix products: 34.5 us -> 3.44 us
  Pallas kernels: 0 us -> 19.4 us
  local copies, waits for them, and re-layouts: 23.2 us -> 4.63 us
  between operations: 15.7 us -> 0.79 us
  loops' own time: 6.04 us -> 0 us
    reduce_scatter x2 -> x0, waiting for transfers between devices: 421 us -> none  [the longest x1 342 us: on_device(): lax.psum_scatter(jnp.einsum('bnd,bne->de', token_rows, grads_low, preferr...]
    all_gather x2 -> x0, blocking collectives: 83.8 us -> none  [the longest x1 45.3 us: on_device(): lax.all_gather(keys, 'context', axis=1, tiled=True)]
    all_to_all x0 -> x1, waiting for transfers between devices: none -> 43.1 us  [on_device(): lax.all_to_all(sent, 'context', split_axis=0, concat_axis=0, tiled=True)]
    ppermute x0 -> x19, waiting for transfers between devices: none -> 40.9 us  [the longest x18 40.9 us: swap(): lax.ppermute(value, 'context', [(i, i ^ offset) for i in range(count)])]
    dot_general x25 -> x1, matrix products: 34.5 us -> 3.44 us  [dot(): lax.dot_general(left, right, dims, preferred_element_type=jnp.float32)]
    ppermute x0 -> x19, starting transfers between devices: none -> 27.7 us  [the longest x18 27.7 us: swap(): lax.ppermute(value, 'context', [(i, i ^ offset) for i in range(count)])]
    pallas_call x0 -> x2, Pallas kernels: none -> 19.4 us  [the longest x1 11.2 us: turned_columns(): pl.pallas_call(body, out_shape=jax.ShapeDtypeStruct((column_count, count...]
    all_to_all x0 -> x1, starting transfers between devices: none -> 8.51 us  [on_device(): lax.all_to_all(sent, 'context', split_axis=0, concat_axis=0, tiled=True)]
  transfers between devices with their start and end apart: 3 -> 20, of which waited for: 2 -> 16; matrix products, arithmetic and copies ran while one was open for 9% -> 1% of each run, Pallas kernels for 0% -> 5%
where the time goes in v1:
time: 155 us; the launch traced here: 154 us
  waiting for transfers between devices  83.9 us (54%)
  starting transfers between devices  36.3 us (23%)
  Pallas kernels  19.4 us (13%)
  other arithmetic  5.24 us (3%)
  local copies, waits for them, and re-layouts  4.63 us (3%)
  matrix products  3.44 us (2%)
    all_to_all x1, waiting for transfers between devices, on_device(): lax.all_to_all(sent, 'context', split_axis=0, concat_axis=0, tiled=True)  43.1 us
    ppermute x18, waiting for transfers between devices, swap(): lax.ppermute(value, 'context', [(i, i ^ offset) for i in range(count)])  40.9 us
    ppermute x18, starting transfers between devices, swap(): lax.ppermute(value, 'context', [(i, i ^ offset) for i in range(count)])  27.7 us
    pallas_call x1, Pallas kernels, turned_columns(): pl.pallas_call(body, out_shape=jax.ShapeDtypeStruct((column_count, count...  11.2 us
    all_to_all x1, starting transfers between devices, on_device(): lax.all_to_all(sent, 'context', split_axis=0, concat_axis=0, tiled=True)  8.51 us
    pallas_call x1, Pallas kernels, attention_grads(): pl.pallas_call(body, out_shape=(jax.ShapeDtypeStruct((rows, width), jnp.b...  8.24 us
    select_n x1, other arithmetic, on_device(): jnp.where(tensor_index == 0, other, mine)  4.52 us
    dot_general x1, matrix products, dot(): lax.dot_general(left, right, dims, preferred_element_type=jnp.float32)  3.44 us
  transfers between devices with their start and end apart: 20, of which 16 were waited for; matrix products, arithmetic and copies ran while one was open for 1% of the time, Pallas kernels for 5%

profile of v1, /device:TPU:0, one launch (start us, length us, event | category | flops | bytes accessed | tf_op | source)
XLA Modules:
  0.0 153.7 jit_solution(3715368005328854571)
XLA Ops:
  0.6 3.1 %copy.30 = bf16[1,8,16,8,1024]{4,3,1,2,0:T(8,128)(2,1)} copy(bf16[1,8,16,8,1024]{4,3,2,1,0:T(8,128)(2,1)} %bitcast.55) | data formatting | bytes 4194304 | tf_op jit(solution)/shard_map/reshape | solution.py:190
  3.8 8.5 %all-to-all-start = ((bf16[16,64,1024]{2,1,0:T(8,128)(2,1)}), bf16[16,64,1024]{2,1,0:T(8,128)(2,1)}, u32[]{:S(2)}, u32[]{:S(2)}) async-start(bf16[16,64,1024]{2,1,0:T(8,128)(2,1)} %bitcast.47), calls=%async_computation | async-start | bytes 4194304 | tf_op jit(solution)/shard_map/all_to_all | solution.py:192
  12.3 43.1 %all-to-all-done = bf16[16,64,1024]{2,1,0:T(8,128)(2,1)} async-done(((bf16[16,64,1024]{2,1,0:T(8,128)(2,1)}), bf16[16,64,1024]{2,1,0:T(8,128)(2,1)}, u32[]{:S(2)}, u32[]{:S(2)}) %all-to-all-start) | async-done | bytes 2097184 | tf_op jit(solution)/shard_map/all_to_all | solution.py:192
  55.5 6.2 %collective-permute-start.2 = (bf16[1,128,256]{2,1,0:T(8,128)(2,1)S(1)}, bf16[1,128,256]{2,1,0:T(8,128)(2,1)S(1)}, u32[]{:S(2)}, u32[]{:S(2)}) collective-permute-start(bf16[1,128,256]{2,1,0:T(8,128)(2,1)S(1)} %constant_dynamic-update-slice_fusion), channel_id=1, source_target_pairs={{0,24},{2,26},{4,28},{6,30},{8,16},{10,18},{12,20},{14,22},{16,8},... | collective-permute-start | bytes 196616 | tf_op jit(solution)/shard_map/ppermute | solution.py:23
  61.7 1.7 %collective-permute-start.1 = (bf16[1,128,256]{2,1,0:T(8,128)(2,1)S(1)}, bf16[1,128,256]{2,1,0:T(8,128)(2,1)S(1)}, u32[]{:S(2)}, u32[]{:S(2)}) collective-permute-start(bf16[1,128,256]{2,1,0:T(8,128)(2,1)S(1)} %constant_dynamic-update-slice_fusion), channel_id=1, source_target_pairs={{0,16},{2,18},{4,20},{6,22},{8,24},{10,26},{12,28},{14,30},{16,0},... | collective-permute-start | bytes 196616 | tf_op jit(solution)/shard_map/ppermute | solution.py:23
  64.5 4.2 %collective-permute-done.1 = bf16[1,128,256]{2,1,0:T(8,128)(2,1)S(1)} collective-permute-done((bf16[1,128,256]{2,1,0:T(8,128)(2,1)S(1)}, bf16[1,128,256]{2,1,0:T(8,128)(2,1)S(1)}, u32[]{:S(2)}, u32[]{:S(2)}) %collective-permute-start.1) | collective-permute-done | bytes 65568 | tf_op jit(solution)/shard_map/ppermute | solution.py:23
  68.9 2.8 %collective-permute-start.4 = (bf16[1,512,256]{2,1,0:T(8,128)(2,1)S(1)}, bf16[1,512,256]{2,1,0:T(8,128)(2,1)S(1)}, u32[]{:S(2)}, u32[]{:S(2)}) collective-permute-start(bf16[1,512,256]{2,1,0:T(8,128)(2,1)S(1)} %get-tuple-element.22), channel_id=1, source_target_pairs={{0,4},{2,6},{4,0},{6,2},{8,12},{10,14},{12,8},{14,10},{16,20},{18,... | collective-permute-start | bytes 786440 | tf_op jit(solution)/shard_map/ppermute | solution.py:23
  71.7 0.8 collective-permute-start.3
  74.0 4.2 %collective-permute-done.4 = bf16[1,512,256]{2,1,0:T(8,128)(2,1)S(1)} collective-permute-done((bf16[1,512,256]{2,1,0:T(8,128)(2,1)S(1)}, bf16[1,512,256]{2,1,0:T(8,128)(2,1)S(1)}, u32[]{:S(2)}, u32[]{:S(2)}) %collective-permute-start.4) | collective-permute-done | bytes 262176 | tf_op jit(solution)/shard_map/ppermute | solution.py:23
  78.2 2.7 %collective-permute-done.3 = bf16[1,512,256]{2,1,0:T(8,128)(2,1)S(1)} collective-permute-done((bf16[1,512,256]{2,1,0:T(8,128)(2,1)S(1)}, bf16[1,512,256]{2,1,0:T(8,128)(2,1)S(1)}, u32[]{:S(2)}, u32[]{:S(2)}) %collective-permute-start.3) | collective-permute-done | bytes 262176 | tf_op jit(solution)/shard_map/ppermute | solution.py:23
  80.9 4.2 %collective-permute-done.5 = bf16[1,512,256]{2,1,0:T(8,128)(2,1)S(1)} collective-permute-done((bf16[1,512,256]{2,1,0:T(8,128)(2,1)S(1)}, bf16[1,512,256]{2,1,0:T(8,128)(2,1)S(1)}, u32[]{:S(2)}, u32[]{:S(2)}) %collective-permute-start.5) | collective-permute-done | bytes 262176 | tf_op jit(solution)/shard_map/ppermute | solution.py:23
  85.1 8.2 %attention_grads.1 = (bf16[128,2048]{1,0:T(8,128)(2,1)}, bf16[512,256]{1,0:T(8,128)(2,1)S(1)}, bf16[512,256]{1,0:T(8,128)(2,1)S(1)}, bf16[512,256]{1,0:T(8,128)(2,1)S(1)}, bf16[512,256]{1,0:T(8,128)(2,1)S(1)}) custom-call(s32[1]{0:T(128)} %bitcast.2.me, s32[32]{0:T(128)S(1)} %copy-done.2, s32[16]{0:T(128)S(1)} %bitcast.54, bf16[128,2048]{1,0:T(8,128)(2,1)S(1)} %bitcast.50, ...), custom_call_target="tpu_custom_call" | custom-call | tf_op jit(solution)/shard_map/attention_grads/pallas_call | solution.py:131
  93.3 1.7 %collective-permute-start.8 = (bf16[512,256]{1,0:T(8,128)(2,1)S(1)}, bf16[512,256]{1,0:T(8,128)(2,1)S(1)}, u32[]{:S(2)}, u32[]{:S(2)}) collective-permute-start(bf16[512,256]{1,0:T(8,128)(2,1)S(1)} %get-tuple-element.11), channel_id=1, source_target_pairs={{0,4},{2,6},{4,0},{6,2},{8,12},{10,14},{12,8},{14,10},{16,20},{18,... | collective-permute-start | bytes 786440 | tf_op jit(solution)/shard_map/ppermute | solution.py:23
  95.0 1.8 %collective-permute-start.9 = (bf16[512,256]{1,0:T(8,128)(2,1)S(1)}, bf16[512,256]{1,0:T(8,128)(2,1)S(1)}, u32[]{:S(2)}, u32[]{:S(2)}) collective-permute-start(bf16[512,256]{1,0:T(8,128)(2,1)S(1)} %get-tuple-element.12), channel_id=1, source_target_pairs={{0,6},{2,4},{4,2},{6,0},{8,14},{10,12},{12,10},{14,8},{16,22},{18,... | collective-permute-start | bytes 786440 | tf_op jit(solution)/shard_map/ppermute | solution.py:23
  96.8 5.8 %collective-permute-done.7 = bf16[512,256]{1,0:T(8,128)(2,1)S(1)} collective-permute-done((bf16[512,256]{1,0:T(8,128)(2,1)S(1)}, bf16[512,256]{1,0:T(8,128)(2,1)S(1)}, u32[]{:S(2)}, u32[]{:S(2)}) %collective-permute-start.7) | collective-permute-done | bytes 262176 | tf_op jit(solution)/shard_map/ppermute | solution.py:23
  102.6 4.6 %collective-permute-done.9 = bf16[512,256]{1,0:T(8,128)(2,1)S(1)} collective-permute-done((bf16[512,256]{1,0:T(8,128)(2,1)S(1)}, bf16[512,256]{1,0:T(8,128)(2,1)S(1)}, u32[]{:S(2)}, u32[]{:S(2)}) %collective-permute-start.9) | collective-permute-done | bytes 262176 | tf_op jit(solution)/shard_map/ppermute | solution.py:23
  107.4 1.7 %collective-permute-start.12 = (bf16[128,256]{1,0:T(8,128)(2,1)S(1)}, bf16[128,256]{1,0:T(8,128)(2,1)S(1)}, u32[]{:S(2)}, u32[]{:S(2)}) collective-permute-start(bf16[128,256]{1,0:T(8,128)(2,1)S(1)} %get-tuple-element.20), channel_id=1, source_target_pairs={{0,24},{2,26},{4,28},{6,30},{8,16},{10,18},{12,20},{14,22},{16,8},... | collective-permute-start | bytes 196616 | tf_op jit(solution)/shard_map/ppermute | solution.py:23
  109.1 1.8 %collective-permute-start.11 = (bf16[128,256]{1,0:T(8,128)(2,1)S(1)}, bf16[128,256]{1,0:T(8,128)(2,1)S(1)}, u32[]{:S(2)}, u32[]{:S(2)}) collective-permute-start(bf16[128,256]{1,0:T(8,128)(2,1)S(1)} %get-tuple-element.21), channel_id=1, source_target_pairs={{0,16},{2,18},{4,20},{6,22},{8,24},{10,26},{12,28},{14,30},{16,0},... | collective-permute-start | bytes 196616 | tf_op jit(solution)/shard_map/ppermute | solution.py:23
  110.9 1.3 collective-permute-done.10
  112.2 1.5 collective-permute-done.12
  113.7 2.0 %collective-permute-done.11 = bf16[128,256]{1,0:T(8,128)(2,1)S(1)} collective-permute-done((bf16[128,256]{1,0:T(8,128)(2,1)S(1)}, bf16[128,256]{1,0:T(8,128)(2,1)S(1)}, u32[]{:S(2)}, u32[]{:S(2)}) %collective-permute-start.11) | collective-permute-done | bytes 65568 | tf_op jit(solution)/shard_map/ppermute | solution.py:23
  115.7 1.7 %collective-permute-start.15 = (bf16[128,256]{1,0:T(8,128)(2,1)S(1)}, bf16[128,256]{1,0:T(8,128)(2,1)S(1)}, u32[]{:S(2)}, u32[]{:S(2)}) collective-permute-start(bf16[128,256]{1,0:T(8,128)(2,1)S(1)} %fusion.3), channel_id=1, source_target_pairs={{0,24},{2,26},{4,28},{6,30},{8,16},{10,18},{12,20},{14,22},{16,8},... | collective-permute-start | bytes 196616 | tf_op jit(solution)/shard_map/ppermute | solution.py:23
  117.4 2.7 %collective-permute-start.13 = (bf16[128,256]{1,0:T(8,128)(2,1)S(1)}, bf16[128,256]{1,0:T(8,128)(2,1)S(1)}, u32[]{:S(2)}, u32[]{:S(2)}) collective-permute-start(bf16[128,256]{1,0:T(8,128)(2,1)S(1)} %fusion.3), channel_id=1, source_target_pairs={{0,8},{2,10},{4,12},{6,14},{8,0},{10,2},{12,4},{14,6},{16,24},{18,... | collective-permute-start | bytes 196616 | tf_op jit(solution)/shard_map/ppermute | solution.py:23
  120.1 1.7 %collective-permute-done.15 = bf16[128,256]{1,0:T(8,128)(2,1)S(1)} collective-permute-done((bf16[128,256]{1,0:T(8,128)(2,1)S(1)}, bf16[128,256]{1,0:T(8,128)(2,1)S(1)}, u32[]{:S(2)}, u32[]{:S(2)}) %collective-permute-start.15) | collective-permute-done | bytes 65568 | tf_op jit(solution)/shard_map/ppermute | solution.py:23
  121.8 1.4 collective-permute-done.14
  123.2 2.9 %collective-permute-start.18 = (bf16[512,256]{1,0:T(8,128)(2,1)S(1)}, bf16[512,256]{1,0:T(8,128)(2,1)S(1)}, u32[]{:S(2)}, u32[]{:S(2)}) collective-permute-start(bf16[512,256]{1,0:T(8,128)(2,1)S(1)} %pad_maximum_fusion.2), channel_id=1, source_target_pairs={{0,6},{2,4},{4,2},{6,0},{8,14},{10,12},{12,10},{14,8},{16,22},{18,... | collective-permute-start | bytes 786440 | tf_op jit(solution)/shard_map/ppermute | solution.py:23
  126.8 3.9 %collective-permute-done.18 = bf16[512,256]{1,0:T(8,128)(2,1)S(1)} collective-permute-done((bf16[512,256]{1,0:T(8,128)(2,1)S(1)}, bf16[512,256]{1,0:T(8,128)(2,1)S(1)}, u32[]{:S(2)}, u32[]{:S(2)}) %collective-permute-start.18) | collective-permute-done | bytes 262176 | tf_op jit(solution)/shard_map/ppermute | solution.py:23
  130.7 2.7 %collective-permute-done.17 = bf16[512,256]{1,0:T(8,128)(2,1)S(1)} collective-permute-done((bf16[512,256]{1,0:T(8,128)(2,1)S(1)}, bf16[512,256]{1,0:T(8,128)(2,1)S(1)}, u32[]{:S(2)}, u32[]{:S(2)}) %collective-permute-start.17) | collective-permute-done | bytes 262176 | tf_op jit(solution)/shard_map/ppermute | solution.py:23
  133.5 4.5 %broadcast_select_fusion = (bf16[16,64,1024]{2,1,0:T(8,128)(2,1)}, bf16[16,64,1024]{2,1,0:T(8,128)(2,1)}) fusion(bf16[16,64,1024]{2,1,0:T(8,128)(2,1)} %collective-permute-done.6, bf16[16,64,1024]{2,1,0:T(8,128)(2,1)} %all-to-all-done, pred[]{:T(512)S(6)} %eq.4), kind=kLoop, calls=%fused_computation.1 | loop fusion | flops 2097152 | bytes 8388609 | tf_op jit(solution)/shard_map/jit(_where)/select_n | solution.py:196
  138.1 11.2 %turned_columns.1 = bf16[1024,2048]{1,0:T(8,128)(2,1)} custom-call(s32[1]{0:T(128)} %bitcast.2.me, bf16[16,64,1024]{2,1,0:T(8,128)(2,1)} %get-tuple-element.16.refs_0_, bf16[16,64,1024]{2,1,0:T(8,128)(2,1)} %get-tuple-element.15.refs_1_), custom_call_target="tpu_custom_call" | custom-call | tf_op jit(solution)/shard_map/turned_columns/pallas_call | solution.py:162
  149.2 3.4 %fusion.8 = f32[1024,256]{1,0:T(8,128)S(1)} fusion(bf16[1024,2048]{1,0:T(8,128)(2,1)} %turned_columns.1, bf16[2048,256]{1,0:T(8,128)(2,1)S(1)} %bitcast.58), kind=kOutput, calls=%fused_computation.19 | convolution fusion | flops 1073741824 | bytes 6291456 | tf_op jit(solution)/shard_map/dot_general | solution.py:19
  152.7 1.0 fusion.6
  (42 shorter events, 4.0 us)
Async XLA Ops:
  3.8 8.5 %copy-start.5 = (bf16[1,128,128]{2,1,0:T(8,128)(2,1)S(1)}, bf16[1,128,128]{2,1,0:T(8,128)(2,1)}, u32[]{:S(2)}) copy-start(bf16[1,128,128]{2,1,0:T(8,128)(2,1)} %param.9) | copy-start | bytes 98308
  3.8 51.7 %copy-start.6 = (bf16[1,128,128]{2,1,0:T(8,128)(2,1)S(1)}, bf16[1,128,128]{2,1,0:T(8,128)(2,1)}, u32[]{:S(2)}) copy-start(bf16[1,128,128]{2,1,0:T(8,128)(2,1)} %param.10) | copy-start | bytes 98308
  3.8 69.4 %copy-start.4 = (bf16[1,128,2048]{2,1,0:T(8,128)(2,1)S(1)}, bf16[1,128,2048]{2,1,0:T(8,128)(2,1)}, u32[]{:S(2)}) copy-start(bf16[1,128,2048]{2,1,0:T(8,128)(2,1)} %param.11) | copy-start | bytes 1572868
  3.8 69.5 %copy-start = (bf16[1,128,2048]{2,1,0:T(8,128)(2,1)S(1)}, bf16[1,128,2048]{2,1,0:T(8,128)(2,1)}, u32[]{:S(2)}) copy-start(bf16[1,128,2048]{2,1,0:T(8,128)(2,1)} %param.12) | copy-start | bytes 1572868
  3.8 51.6 %all-to-all-start = ((bf16[16,64,1024]{2,1,0:T(8,128)(2,1)}), bf16[16,64,1024]{2,1,0:T(8,128)(2,1)}, u32[]{:S(2)}, u32[]{:S(2)}) async-start(bf16[16,64,1024]{2,1,0:T(8,128)(2,1)} %bitcast.47), calls=%async_computation | async-start | bytes 4194304 | tf_op jit(solution)/shard_map/all_to_all | solution.py:192
  55.4 78.1 %collective-permute-start.6 = (bf16[16,64,1024]{2,1,0:T(8,128)(2,1)}, bf16[16,64,1024]{2,1,0:T(8,128)(2,1)}, u32[]{:S(2)}, u32[]{:S(2)}) collective-permute-start(bf16[16,64,1024]{2,1,0:T(8,128)(2,1)} %all-to-all-done), channel_id=1, source_target_pairs={{0,1},{1,0},{2,3},{3,2},{4,5},{5,4},{6,7},{7,6},{8,9},{9,8},{10,11... | collective-permute-start | bytes 6291464 | tf_op jit(solution)/shard_map/ppermute | solution.py:195
  55.4 29.6 %copy-start.1 = (bf16[1,128,2048]{2,1,0:T(8,128)(2,1)S(1)}, bf16[1,128,2048]{2,1,0:T(8,128)(2,1)}, u32[]{:S(2)}) copy-start(bf16[1,128,2048]{2,1,0:T(8,128)(2,1)} %param.8) | copy-start | bytes 1572868
  55.5 29.6 %copy-start.2 = (s32[32]{0:T(128)S(1)}, s32[32]{0:T(128)}, u32[]{:S(2)}) copy-start(s32[32]{0:T(128)} %slots.1) | copy-start | bytes 388
  55.5 29.6 %copy-start.3 = (s32[1,16]{1,0:T(1,128)S(1)}, s32[1,16]{1,0:T(1,128)}, u32[]{:S(2)}) copy-start(s32[1,16]{1,0:T(1,128)} %param.14) | copy-start | bytes 196
  55.5 9.0 %collective-permute-start.2 = (bf16[1,128,256]{2,1,0:T(8,128)(2,1)S(1)}, bf16[1,128,256]{2,1,0:T(8,128)(2,1)S(1)}, u32[]{:S(2)}, u32[]{:S(2)}) collective-permute-start(bf16[1,128,256]{2,1,0:T(8,128)(2,1)S(1)} %constant_dynamic-update-slice_fusion), channel_id=1, source_target_pairs={{0,24},{2,26},{4,28},{6,30},{8,16},{10,18},{12,20},{14,22},{16,8},... | collective-permute-start | bytes 196616 | tf_op jit(solution)/shard_map/ppermute | solution.py:23
  61.7 6.9 %collective-permute-start.1 = (bf16[1,128,256]{2,1,0:T(8,128)(2,1)S(1)}, bf16[1,128,256]{2,1,0:T(8,128)(2,1)S(1)}, u32[]{:S(2)}, u32[]{:S(2)}) collective-permute-start(bf16[1,128,256]{2,1,0:T(8,128)(2,1)S(1)} %constant_dynamic-update-slice_fusion), channel_id=1, source_target_pairs={{0,16},{2,18},{4,20},{6,22},{8,24},{10,26},{12,28},{14,30},{16,0},... | collective-permute-start | bytes 196616 | tf_op jit(solution)/shard_map/ppermute | solution.py:23
  63.4 5.5 %collective-permute-start = (bf16[1,128,256]{2,1,0:T(8,128)(2,1)S(1)}, bf16[1,128,256]{2,1,0:T(8,128)(2,1)S(1)}, u32[]{:S(2)}, u32[]{:S(2)}) collective-permute-start(bf16[1,128,256]{2,1,0:T(8,128)(2,1)S(1)} %constant_dynamic-update-slice_fusion), channel_id=1, source_target_pairs={{0,8},{2,10},{4,12},{6,14},{8,0},{10,2},{12,4},{14,6},{16,24},{18,... | collective-permute-start | bytes 196616 | tf_op jit(solution)/shard_map/ppermute | solution.py:23
  68.9 9.3 %collective-permute-start.4 = (bf16[1,512,256]{2,1,0:T(8,128)(2,1)S(1)}, bf16[1,512,256]{2,1,0:T(8,128)(2,1)S(1)}, u32[]{:S(2)}, u32[]{:S(2)}) collective-permute-start(bf16[1,512,256]{2,1,0:T(8,128)(2,1)S(1)} %get-tuple-element.22), channel_id=1, source_target_pairs={{0,4},{2,6},{4,0},{6,2},{8,12},{10,14},{12,8},{14,10},{16,20},{18,... | collective-permute-start | bytes 786440 | tf_op jit(solution)/shard_map/ppermute | solution.py:23
  71.7 9.2 %collective-permute-start.3 = (bf16[1,512,256]{2,1,0:T(8,128)(2,1)S(1)}, bf16[1,512,256]{2,1,0:T(8,128)(2,1)S(1)}, u32[]{:S(2)}, u32[]{:S(2)}) collective-permute-start(bf16[1,512,256]{2,1,0:T(8,128)(2,1)S(1)} %get-tuple-element.22), channel_id=1, source_target_pairs={{0,2},{2,0},{4,6},{6,4},{8,10},{10,8},{12,14},{14,12},{16,18},{18,... | collective-permute-start | bytes 786440 | tf_op jit(solution)/shard_map/ppermute | solution.py:23
  72.4 12.6 %collective-permute-start.5 = (bf16[1,512,256]{2,1,0:T(8,128)(2,1)S(1)}, bf16[1,512,256]{2,1,0:T(8,128)(2,1)S(1)}, u32[]{:S(2)}, u32[]{:S(2)}) collective-permute-start(bf16[1,512,256]{2,1,0:T(8,128)(2,1)S(1)} %get-tuple-element.22), channel_id=1, source_target_pairs={{0,6},{2,4},{4,2},{6,0},{8,14},{10,12},{12,10},{14,8},{16,22},{18,... | collective-permute-start | bytes 786440 | tf_op jit(solution)/shard_map/ppermute | solution.py:23
  93.3 9.2 %collective-permute-start.7 = (bf16[512,256]{1,0:T(8,128)(2,1)S(1)}, bf16[512,256]{1,0:T(8,128)(2,1)S(1)}, u32[]{:S(2)}, u32[]{:S(2)}) collective-permute-start(bf16[512,256]{1,0:T(8,128)(2,1)S(1)} %get-tuple-element.10), channel_id=1, source_target_pairs={{0,2},{2,0},{4,6},{6,4},{8,10},{10,8},{12,14},{14,12},{16,18},{18,... | collective-permute-start | bytes 786440 | tf_op jit(solution)/shard_map/ppermute | solution.py:23
  93.3 9.2 %collective-permute-start.8 = (bf16[512,256]{1,0:T(8,128)(2,1)S(1)}, bf16[512,256]{1,0:T(8,128)(2,1)S(1)}, u32[]{:S(2)}, u32[]{:S(2)}) collective-permute-start(bf16[512,256]{1,0:T(8,128)(2,1)S(1)} %get-tuple-element.11), channel_id=1, source_target_pairs={{0,4},{2,6},{4,0},{6,2},{8,12},{10,14},{12,8},{14,10},{16,20},{18,... | collective-permute-start | bytes 786440 | tf_op jit(solution)/shard_map/ppermute | solution.py:23
  95.0 12.2 %collective-permute-start.9 = (bf16[512,256]{1,0:T(8,128)(2,1)S(1)}, bf16[512,256]{1,0:T(8,128)(2,1)S(1)}, u32[]{:S(2)}, u32[]{:S(2)}) collective-permute-start(bf16[512,256]{1,0:T(8,128)(2,1)S(1)} %get-tuple-element.12), channel_id=1, source_target_pairs={{0,6},{2,4},{4,2},{6,0},{8,14},{10,12},{12,10},{14,8},{16,22},{18,... | collective-permute-start | bytes 786440 | tf_op jit(solution)/shard_map/ppermute | solution.py:23
  107.3 4.8 %collective-permute-start.10 = (bf16[128,256]{1,0:T(8,128)(2,1)S(1)}, bf16[128,256]{1,0:T(8,128)(2,1)S(1)}, u32[]{:S(2)}, u32[]{:S(2)}) collective-permute-start(bf16[128,256]{1,0:T(8,128)(2,1)S(1)} %get-tuple-element.19), channel_id=1, source_target_pairs={{0,8},{2,10},{4,12},{6,14},{8,0},{10,2},{12,4},{14,6},{16,24},{18,... | collective-permute-start | bytes 196616 | tf_op jit(solution)/shard_map/ppermute | solution.py:23
  107.4 6.2 %collective-permute-start.12 = (bf16[128,256]{1,0:T(8,128)(2,1)S(1)}, bf16[128,256]{1,0:T(8,128)(2,1)S(1)}, u32[]{:S(2)}, u32[]{:S(2)}) collective-permute-start(bf16[128,256]{1,0:T(8,128)(2,1)S(1)} %get-tuple-element.20), channel_id=1, source_target_pairs={{0,24},{2,26},{4,28},{6,30},{8,16},{10,18},{12,20},{14,22},{16,8},... | collective-permute-start | bytes 196616 | tf_op jit(solution)/shard_map/ppermute | solution.py:23
  109.1 6.5 %collective-permute-start.11 = (bf16[128,256]{1,0:T(8,128)(2,1)S(1)}, bf16[128,256]{1,0:T(8,128)(2,1)S(1)}, u32[]{:S(2)}, u32[]{:S(2)}) collective-permute-start(bf16[128,256]{1,0:T(8,128)(2,1)S(1)} %get-tuple-element.21), channel_id=1, source_target_pairs={{0,16},{2,18},{4,20},{6,22},{8,24},{10,26},{12,28},{14,30},{16,0},... | collective-permute-start | bytes 196616 | tf_op jit(solution)/shard_map/ppermute | solution.py:23
  115.7 6.1 %collective-permute-start.15 = (bf16[128,256]{1,0:T(8,128)(2,1)S(1)}, bf16[128,256]{1,0:T(8,128)(2,1)S(1)}, u32[]{:S(2)}, u32[]{:S(2)}) collective-permute-start(bf16[128,256]{1,0:T(8,128)(2,1)S(1)} %fusion.3), channel_id=1, source_target_pairs={{0,24},{2,26},{4,28},{6,30},{8,16},{10,18},{12,20},{14,22},{16,8},... | collective-permute-start | bytes 196616 | tf_op jit(solution)/shard_map/ppermute | solution.py:23
  117.4 5.8 %collective-permute-start.14 = (bf16[128,256]{1,0:T(8,128)(2,1)S(1)}, bf16[128,256]{1,0:T(8,128)(2,1)S(1)}, u32[]{:S(2)}, u32[]{:S(2)}) collective-permute-start(bf16[128,256]{1,0:T(8,128)(2,1)S(1)} %fusion.3), channel_id=1, source_target_pairs={{0,16},{2,18},{4,20},{6,22},{8,24},{10,26},{12,28},{14,30},{16,0},... | collective-permute-start | bytes 196616 | tf_op jit(solution)/shard_map/ppermute | solution.py:23
  117.4 5.8 %collective-permute-start.13 = (bf16[128,256]{1,0:T(8,128)(2,1)S(1)}, bf16[128,256]{1,0:T(8,128)(2,1)S(1)}, u32[]{:S(2)}, u32[]{:S(2)}) collective-permute-start(bf16[128,256]{1,0:T(8,128)(2,1)S(1)} %fusion.3), channel_id=1, source_target_pairs={{0,8},{2,10},{4,12},{6,14},{8,0},{10,2},{12,4},{14,6},{16,24},{18,... | collective-permute-start | bytes 196616 | tf_op jit(solution)/shard_map/ppermute | solution.py:23
  123.2 7.4 %collective-permute-start.18 = (bf16[512,256]{1,0:T(8,128)(2,1)S(1)}, bf16[512,256]{1,0:T(8,128)(2,1)S(1)}, u32[]{:S(2)}, u32[]{:S(2)}) collective-permute-start(bf16[512,256]{1,0:T(8,128)(2,1)S(1)} %pad_maximum_fusion.2), channel_id=1, source_target_pairs={{0,6},{2,4},{4,2},{6,0},{8,14},{10,12},{12,10},{14,8},{16,22},{18,... | collective-permute-start | bytes 786440 | tf_op jit(solution)/shard_map/ppermute | solution.py:23
  126.1 7.2 %collective-permute-start.17 = (bf16[512,256]{1,0:T(8,128)(2,1)S(1)}, bf16[512,256]{1,0:T(8,128)(2,1)S(1)}, u32[]{:S(2)}, u32[]{:S(2)}) collective-permute-start(bf16[512,256]{1,0:T(8,128)(2,1)S(1)} %pad_maximum_fusion.2), channel_id=1, source_target_pairs={{0,4},{2,6},{4,0},{6,2},{8,12},{10,14},{12,8},{14,10},{16,20},{18,... | collective-permute-start | bytes 786440 | tf_op jit(solution)/shard_map/ppermute | solution.py:23
  126.1 7.2 %collective-permute-start.16 = (bf16[512,256]{1,0:T(8,128)(2,1)S(1)}, bf16[512,256]{1,0:T(8,128)(2,1)S(1)}, u32[]{:S(2)}, u32[]{:S(2)}) collective-permute-start(bf16[512,256]{1,0:T(8,128)(2,1)S(1)} %pad_maximum_fusion.2), channel_id=1, source_target_pairs={{0,2},{2,0},{4,6},{6,4},{8,10},{10,8},{12,14},{14,12},{16,18},{18,... | collective-permute-start | bytes 786440 | tf_op jit(solution)/shard_map/ppermute | solution.py:23

commit v2 on v1

--- a/solution.py
+++ b/solution.py
@@ -150,26 +150,47 @@
     )(me, slots, docs, queries, grad_out, delta, *key_values)
 
 
-def turned_columns(me, halves, rows, column_count):
-    count = halves[0].shape[0]
-    spec = pl.BlockSpec((1, rows, column_count), lambda r, me: (me[0] ^ r, 0, 0))
-    tensor_count = len(halves)
-
-    def body(me, *refs):
-        both = jnp.concatenate([ref[0] for ref in refs[:-1]], axis=0)
-        refs[-1][...] = both.T
-
+def weight_kernel(place, *refs, low, parts, rows, head):
+    grad_refs, column_refs, (key_ref, value_ref, sums) = refs[:low], refs[low : low + parts], refs[low + parts :]
+    step = pl.program_id(0)
+    own_high, own_part = place[0] // low, place[1]
+    high = column_refs[0].shape[0]
+    tokens = jnp.concatenate([ref[h, 0] for ref in column_refs for h in range(high)], axis=0)
+
+    for digit in range(low):
+
+        @pl.when(step == digit)
+        def _():
+            starts = [((h ^ own_high) * parts + (part ^ own_part)) * rows for part in range(parts) for h in range(high)]
+            grads = jnp.concatenate([grad_refs[digit][pl.ds(pl.multiple_of(s, rows), rows), :] for s in starts], axis=0)
+            found = dot(grads, tokens, TN)
+            sums[...] = found if digit == 0 else sums[...] + found
+
+    @pl.when(step == low - 1)
+    def _():
+        key_ref[...] = sums[:head, :].T
+        value_ref[...] = sums[head:, :].T
+
+
+def weight_grads(place, columns, grads, head):
+    count, rows, width = columns[0].shape
+    low, parts = len(grads), len(columns)
+    spec = pl.BlockSpec((count // low, 1, rows, width), lambda i, place: (0, (place[0] % low) ^ i, 0, 0))
+    whole = pl.BlockSpec(grads[0].shape, lambda i, place: (0, 0))
+    out = pl.BlockSpec((width, head), lambda i, place: (0, 0))
     return pl.pallas_call(
-        body,
-        out_shape=jax.ShapeDtypeStruct((column_count, count * tensor_count * rows), jnp.bfloat16),
+        functools.partial(weight_kernel, low=low, parts=parts, rows=rows, head=head),
+        out_shape=(jax.ShapeDtypeStruct((width, head), jnp.float32),) * 2,
         grid_spec=pltpu.PrefetchScalarGridSpec(
             num_scalar_prefetch=1,
-            grid=(count,),
-            in_specs=[spec] * tensor_count,
-            out_specs=pl.BlockSpec((column_count, tensor_count * rows), lambda r, me: (0, r)),
+            grid=(low,),
+            in_specs=[whole] * low + [spec] * parts,
+            out_specs=(out, out),
+            scratch_shapes=[pltpu.VMEM((2 * head, width), jnp.float32)],
         ),
-        name="turned_columns",
-    )(me, *halves)
+        compiler_params=pltpu.CompilerParams(vmem_limit_bytes=32 << 20),
+        name="weight_grads",
+    )(place, *grads, *(c.reshape(count // low, low, rows, width) for c in columns))
 
 
 def on_device(queries, keys, values, outputs, grad_out, inputs, block_doc, span_slots):
@@ -187,20 +208,14 @@
     column_count = inputs.shape[2] // count
     me = lax.axis_index("context").astype(jnp.int32).reshape(1)
 
-    sent = inputs.reshape(batch_count, token_rows, count, column_count)
-    sent = jnp.moveaxis(sent, 2, 0).reshape(count, batch_count * token_rows, column_count)
-    mine = lax.all_to_all(sent, "context", split_axis=0, concat_axis=0, tiled=True)
-    tensor_index = lax.axis_index("tensor")
-    if tensor_count == 2:
-        other = lax.ppermute(mine, "tensor", [(0, 1), (1, 0)])
-        halves = [jnp.where(tensor_index == 0, mine, other), jnp.where(tensor_index == 0, other, mine)]
-    else:
-        every = lax.all_gather(mine, "tensor", axis=0)
-        halves = [every[t] for t in range(tensor_count)]
-
     own = jnp.concatenate([keys, values], axis=2)
     column = jnp.concatenate([own] + [swap(own, k * low, count) for k in range(1, high)], axis=1)
     key_values = [column] + [swap(column, k, count) for k in range(1, low)]
+
+    sent = inputs.reshape(batch_count, token_rows, count, column_count)
+    sent = jnp.moveaxis(sent, 2, 0).reshape(count, batch_count * token_rows, column_count)
+    sent, _ = lax.optimization_barrier((sent, column))
+    mine = lax.all_to_all(sent, "context", split_axis=0, concat_axis=0, tiled=True)
 
     delta = jnp.einsum(
         "bqgd,bqgd->bgq",
@@ -210,7 +225,8 @@
     )
     delta = delta.reshape(batch_count, heads, 2, span_rows).swapaxes(1, 2).reshape(batch_count, 2, 1, heads * span_rows)
 
-    query_grads, weight_grads = [], []
+    place = jnp.concatenate([me, lax.axis_index("tensor").astype(jnp.int32).reshape(1)])
+    query_grads, key_sums, value_sums = [], 0.0, 0.0
     for b in range(batch_count):
         query_grad, *partials = attention_grads(
             me, span_slots, block_doc[b], queries[b], grad_out[b], delta[b], [kv[b] for kv in key_values], head, block_tokens
@@ -223,12 +239,13 @@
         own_grads = sum(p.astype(jnp.float32) for p in arrived).astype(jnp.bfloat16)
         column = jnp.concatenate([own_grads] + [swap(own_grads, k * low, count) for k in range(1, high)], axis=0)
         columns = [column] + [swap(column, k, count) for k in range(1, low)]
-        all_grads = jnp.stack([c.reshape(high, row_count, 2 * head) for c in columns], axis=1).reshape(total, 2 * head)
-        own_halves = [h[:, b * token_rows : (b + 1) * token_rows] for h in halves]
-        turned = turned_columns(me, own_halves, token_rows, column_count)
-        weight_grads.append(dot(turned, all_grads, NN))
-    summed = lax.psum(sum(weight_grads), "dp")
-    return jnp.stack(query_grads), summed[:, :head], summed[:, head:]
+        late, _ = lax.optimization_barrier((mine[:, b * token_rows : (b + 1) * token_rows], own_grads))
+        parts = [late] + [
+            lax.ppermute(late, "tensor", [(i, i ^ k) for i in range(tensor_count)]) for k in range(1, tensor_count)
+        ]
+        key_part, value_part = weight_grads(place, parts, columns, head)
+        key_sums, value_sums = key_sums + key_part, value_sums + value_part
+    return jnp.stack(query_grads), lax.psum(key_sums, "dp"), lax.psum(value_sums, "dp")
 
 
 def solution(mesh):

time: 155 us -> 117 us (0.75)
  waiting for transfers between devices: 83.9 us -> 60.1 us
  Pallas kernels: 19.4 us -> 14.3 us
  other arithmetic: 5.24 us -> 1.35 us
  matrix products: 3.44 us -> 0 us
  starting transfers between devices: 36.3 us -> 33.5 us
    all_to_all x1, waiting for transfers between devices: 43.1 us -> 0.01 us  [on_device(): lax.all_to_all(sent, 'context', split_axis=0, concat_axis=0, tiled=True)]
    ppermute x18, waiting for transfers between devices: 40.9 us -> 60.1 us  [swap(): lax.ppermute(value, 'context', [(i, i ^ offset) for i in range(count)])]
    pallas_call x1, Pallas kernels: 11.2 us -> 5.6 us  [weight_grads(): pl.pallas_call(functools.partial(weight_kernel, low=low, parts=parts, row...]
    select_n x1 -> x0, other arithmetic: 4.52 us -> none  [on_device(): jnp.where(tensor_index == 0, other, mine)]
    dot_general x1 -> x0, matrix products: 3.44 us -> none  [dot(): lax.dot_general(left, right, dims, preferred_element_type=jnp.float32)]
    all_to_all x1, starting transfers between devices: 8.51 us -> 6.11 us  [on_device(): lax.all_to_all(sent, 'context', split_axis=0, concat_axis=0, tiled=True)]
    unnamed x17 -> x11, local copies, waits for them, and re-layouts: 0.26 us -> 2.04 us
  transfers between devices with their start and end apart: 20 -> 20, of which waited for: 16 -> 13; matrix products, arithmetic and copies ran while one was open for 1% -> 4% of each run, Pallas kernels for 5% -> 7%
where the time goes in v2:
time: 117 us; the launch traced here: 116 us
  waiting for transfers between devices  60.1 us (51%)
  starting transfers between devices  33.5 us (29%)
  Pallas kernels  14.3 us (12%)
  local copies, waits for them, and re-layouts  6.15 us (5%)
  other arithmetic  1.35 us (1%)
    ppermute x18, waiting for transfers between devices, swap(): lax.ppermute(value, 'context', [(i, i ^ offset) for i in range(count)])  60.1 us
    ppermute x18, starting transfers between devices, swap(): lax.ppermute(value, 'context', [(i, i ^ offset) for i in range(count)])  27.4 us
    pallas_call x1, Pallas kernels, attention_grads(): pl.pallas_call(body, out_shape=(jax.ShapeDtypeStruct((rows, width), jnp.b...  8.69 us
    all_to_all x1, starting transfers between devices, on_device(): lax.all_to_all(sent, 'context', split_axis=0, concat_axis=0, tiled=True)  6.11 us
    pallas_call x1, Pallas kernels, weight_grads(): pl.pallas_call(functools.partial(weight_kernel, low=low, parts=parts, row...  5.6 us
    reshape x1, local copies, waits for them, and re-layouts, on_device(): sent = inputs.reshape(batch_count, token_rows, count, column_count)  3.16 us
  transfers between devices with their start and end apart: 20, of which 13 were waited for; matrix products, arithmetic and copies ran while one was open for 4% of the time, Pallas kernels for 7%

profile of v2, /device:TPU:0, one launch (start us, length us, event | category | flops | bytes accessed | tf_op | source)
XLA Modules:
  0.0 116.2 jit_solution(3393822580470489858)
XLA Ops:
  0.6 0.8 constant_dynamic-update-slice_fusion.1
  1.4 0.8 constant_dynamic-update-slice_fusion
  2.2 5.1 %collective-permute-start.2 = (bf16[1,128,256]{2,1,0:T(8,128)(2,1)S(1)}, bf16[1,128,256]{2,1,0:T(8,128)(2,1)S(1)}, u32[]{:S(2)}, u32[]{:S(2)}) collective-permute-start(bf16[1,128,256]{2,1,0:T(8,128)(2,1)S(1)} %constant_dynamic-update-slice_fusion), channel_id=1, source_target_pairs={{0,24},{2,26},{4,28},{6,30},{8,16},{10,18},{12,20},{14,22},{16,8},... | collective-permute-start | bytes 196616 | tf_op jit(solution)/shard_map/ppermute | solution.py:23
  7.3 0.6 collective-permute-start
  7.9 3.2 %copy.27 = bf16[1,8,16,8,1024]{4,3,1,2,0:T(8,128)(2,1)} copy(bf16[1,8,16,8,1024]{4,3,2,1,0:T(8,128)(2,1)} %bitcast.42) | data formatting | bytes 4194304 | tf_op jit(solution)/shard_map/reshape | solution.py:215
  11.1 1.8 %collective-permute-done.1 = bf16[1,128,256]{2,1,0:T(8,128)(2,1)S(1)} collective-permute-done((bf16[1,128,256]{2,1,0:T(8,128)(2,1)S(1)}, bf16[1,128,256]{2,1,0:T(8,128)(2,1)S(1)}, u32[]{:S(2)}, u32[]{:S(2)}) %collective-permute-start.1) | collective-permute-done | bytes 65568 | tf_op jit(solution)/shard_map/ppermute | solution.py:23
  12.9 0.7 pad_maximum_fusion
  13.6 6.1 %all-to-all-start = ((bf16[16,64,1024]{2,1,0:T(8,128)(2,1)}), bf16[16,64,1024]{2,1,0:T(8,128)(2,1)S(1)}, u32[]{:S(2)}, u32[]{:S(2)}) async-start(bf16[16,64,1024]{2,1,0:T(8,128)(2,1)} %bitcast.41), calls=%async_computation | async-start | bytes 4194304 | tf_op jit(solution)/shard_map/all_to_all | solution.py:218
  19.8 2.9 %collective-permute-start.5 = (bf16[1,512,256]{2,1,0:T(8,128)(2,1)}, bf16[1,512,256]{2,1,0:T(8,128)(2,1)}, u32[]{:S(2)}, u32[]{:S(2)}) collective-permute-start(bf16[1,512,256]{2,1,0:T(8,128)(2,1)} %get-tuple-element.26), channel_id=1, source_target_pairs={{0,6},{2,4},{4,2},{6,0},{8,14},{10,12},{12,10},{14,8},{16,22},{18,... | collective-permute-start | bytes 786440 | tf_op jit(solution)/shard_map/ppermute | solution.py:23
  22.7 0.6 collective-permute-start.4
  23.3 1.1 copy.25
  25.1 12.4 %collective-permute-done.5 = bf16[1,512,256]{2,1,0:T(8,128)(2,1)} collective-permute-done((bf16[1,512,256]{2,1,0:T(8,128)(2,1)}, bf16[1,512,256]{2,1,0:T(8,128)(2,1)}, u32[]{:S(2)}, u32[]{:S(2)}) %collective-permute-start.5) | collective-permute-done | bytes 262176 | tf_op jit(solution)/shard_map/ppermute | solution.py:23
  37.5 11.4 %collective-permute-done.4 = bf16[1,512,256]{2,1,0:T(8,128)(2,1)} collective-permute-done((bf16[1,512,256]{2,1,0:T(8,128)(2,1)}, bf16[1,512,256]{2,1,0:T(8,128)(2,1)}, u32[]{:S(2)}, u32[]{:S(2)}) %collective-permute-start.4) | collective-permute-done | bytes 262176 | tf_op jit(solution)/shard_map/ppermute | solution.py:23
  48.9 8.7 %attention_grads.1 = (bf16[128,2048]{1,0:T(8,128)(2,1)}, bf16[512,256]{1,0:T(8,128)(2,1)S(1)}, bf16[512,256]{1,0:T(8,128)(2,1)S(1)}, bf16[512,256]{1,0:T(8,128)(2,1)S(1)}, bf16[512,256]{1,0:T(8,128)(2,1)S(1)}) custom-call(s32[1]{0:T(128)} %bitcast.2.me, s32[32]{0:T(128)S(1)} %copy-done.2, s32[16]{0:T(128)S(1)} %bitcast.40, bf16[128,2048]{1,0:T(8,128)(2,1)S(1)} %bitcast.39, ...), custom_call_target="tpu_custom_call" | custom-call | tf_op jit(solution)/shard_map/attention_grads/pallas_call | solution.py:131
  57.6 4.8 %collective-permute-start.7 = (bf16[512,256]{1,0:T(8,128)(2,1)S(1)}, bf16[512,256]{1,0:T(8,128)(2,1)S(1)}, u32[]{:S(2)}, u32[]{:S(2)}) collective-permute-start(bf16[512,256]{1,0:T(8,128)(2,1)S(1)} %get-tuple-element.15), channel_id=1, source_target_pairs={{0,4},{2,6},{4,0},{6,2},{8,12},{10,14},{12,8},{14,10},{16,20},{18,... | collective-permute-start | bytes 786440 | tf_op jit(solution)/shard_map/ppermute | solution.py:23
  62.5 5.2 %collective-permute-done.6 = bf16[512,256]{1,0:T(8,128)(2,1)S(1)} collective-permute-done((bf16[512,256]{1,0:T(8,128)(2,1)S(1)}, bf16[512,256]{1,0:T(8,128)(2,1)S(1)}, u32[]{:S(2)}, u32[]{:S(2)}) %collective-permute-start.6) | collective-permute-done | bytes 262176 | tf_op jit(solution)/shard_map/ppermute | solution.py:23
  67.7 5.0 %collective-permute-done.7 = bf16[512,256]{1,0:T(8,128)(2,1)S(1)} collective-permute-done((bf16[512,256]{1,0:T(8,128)(2,1)S(1)}, bf16[512,256]{1,0:T(8,128)(2,1)S(1)}, u32[]{:S(2)}, u32[]{:S(2)}) %collective-permute-start.7) | collective-permute-done | bytes 262176 | tf_op jit(solution)/shard_map/ppermute | solution.py:23
  72.7 2.0 %collective-permute-done.8 = bf16[512,256]{1,0:T(8,128)(2,1)S(1)} collective-permute-done((bf16[512,256]{1,0:T(8,128)(2,1)S(1)}, bf16[512,256]{1,0:T(8,128)(2,1)S(1)}, u32[]{:S(2)}, u32[]{:S(2)}) %collective-permute-start.8) | collective-permute-done | bytes 262176 | tf_op jit(solution)/shard_map/ppermute | solution.py:23
  75.4 3.5 %collective-permute-start.11 = (bf16[128,256]{1,0:T(8,128)(2,1)S(1)}, bf16[128,256]{1,0:T(8,128)(2,1)S(1)}, u32[]{:S(2)}, u32[]{:S(2)}) collective-permute-start(bf16[128,256]{1,0:T(8,128)(2,1)S(1)} %get-tuple-element.24), channel_id=1, source_target_pairs={{0,24},{2,26},{4,28},{6,30},{8,16},{10,18},{12,20},{14,22},{16,8},... | collective-permute-start | bytes 196616 | tf_op jit(solution)/shard_map/ppermute | solution.py:23
  78.8 0.5 collective-permute-start.10
  79.3 3.1 %collective-permute-done.11 = bf16[128,256]{1,0:T(8,128)(2,1)S(1)} collective-permute-done((bf16[128,256]{1,0:T(8,128)(2,1)S(1)}, bf16[128,256]{1,0:T(8,128)(2,1)S(1)}, u32[]{:S(2)}, u32[]{:S(2)}) %collective-permute-start.11) | collective-permute-done | bytes 65568 | tf_op jit(solution)/shard_map/ppermute | solution.py:23
  82.5 2.6 %collective-permute-done.10 = bf16[128,256]{1,0:T(8,128)(2,1)S(1)} collective-permute-done((bf16[128,256]{1,0:T(8,128)(2,1)S(1)}, bf16[128,256]{1,0:T(8,128)(2,1)S(1)}, u32[]{:S(2)}, u32[]{:S(2)}) %collective-permute-start.10) | collective-permute-done | bytes 65568 | tf_op jit(solution)/shard_map/ppermute | solution.py:23
  85.2 2.0 %collective-permute-start.14 = (bf16[128,256]{1,0:T(8,128)(2,1)S(1)}, bf16[128,256]{1,0:T(8,128)(2,1)S(1)}, u32[]{:S(2)}, u32[]{:S(2)}) collective-permute-start(bf16[128,256]{1,0:T(8,128)(2,1)S(1)} %fusion.3), channel_id=1, source_target_pairs={{0,24},{2,26},{4,28},{6,30},{8,16},{10,18},{12,20},{14,22},{16,8},... | collective-permute-start | bytes 196616 | tf_op jit(solution)/shard_map/ppermute | solution.py:23
  87.2 2.5 %collective-permute-start.12 = (bf16[128,256]{1,0:T(8,128)(2,1)S(1)}, bf16[128,256]{1,0:T(8,128)(2,1)S(1)}, u32[]{:S(2)}, u32[]{:S(2)}) collective-permute-start(bf16[128,256]{1,0:T(8,128)(2,1)S(1)} %fusion.3), channel_id=1, source_target_pairs={{0,8},{2,10},{4,12},{6,14},{8,0},{10,2},{12,4},{14,6},{16,24},{18,... | collective-permute-start | bytes 196616 | tf_op jit(solution)/shard_map/ppermute | solution.py:23
  89.7 2.4 %collective-permute-done.14 = bf16[128,256]{1,0:T(8,128)(2,1)S(1)} collective-permute-done((bf16[128,256]{1,0:T(8,128)(2,1)S(1)}, bf16[128,256]{1,0:T(8,128)(2,1)S(1)}, u32[]{:S(2)}, u32[]{:S(2)}) %collective-permute-start.14) | collective-permute-done | bytes 65568 | tf_op jit(solution)/shard_map/ppermute | solution.py:23
  92.1 2.3 %collective-permute-done.13 = bf16[128,256]{1,0:T(8,128)(2,1)S(1)} collective-permute-done((bf16[128,256]{1,0:T(8,128)(2,1)S(1)}, bf16[128,256]{1,0:T(8,128)(2,1)S(1)}, u32[]{:S(2)}, u32[]{:S(2)}) %collective-permute-start.13) | collective-permute-done | bytes 65568 | tf_op jit(solution)/shard_map/ppermute | solution.py:23
  94.4 2.7 %collective-permute-start.17 = (bf16[512,256]{1,0:T(8,128)(2,1)S(1)}, bf16[512,256]{1,0:T(8,128)(2,1)S(1)}, u32[]{:S(2)}, u32[]{:S(2)}) collective-permute-start(bf16[512,256]{1,0:T(8,128)(2,1)S(1)} %pad_maximum_fusion.1.refs_0_), channel_id=1, source_target_pairs={{0,6},{2,4},{4,2},{6,0},{8,14},{10,12},{12,10},{14,8},{16,22},{18,... | collective-permute-start | bytes 786440 | tf_op jit(solution)/shard_map/ppermute | solution.py:23
  97.3 1.4 %collective-permute-start.15 = (bf16[512,256]{1,0:T(8,128)(2,1)S(1)}, bf16[512,256]{1,0:T(8,128)(2,1)S(1)}, u32[]{:S(2)}, u32[]{:S(2)}) collective-permute-start(bf16[512,256]{1,0:T(8,128)(2,1)S(1)} %pad_maximum_fusion.1.refs_0_), channel_id=1, source_target_pairs={{0,2},{2,0},{4,6},{6,4},{8,10},{10,8},{12,14},{14,12},{16,18},{18,... | collective-permute-start | bytes 786440 | tf_op jit(solution)/shard_map/ppermute | solution.py:23
  98.8 5.8 %collective-permute-done.17.refs_3_ = bf16[512,256]{1,0:T(8,128)(2,1)S(1)} collective-permute-done((bf16[512,256]{1,0:T(8,128)(2,1)S(1)}, bf16[512,256]{1,0:T(8,128)(2,1)S(1)}, u32[]{:S(2)}, u32[]{:S(2)}) %collective-permute-start.17) | collective-permute-done | bytes 262176 | tf_op jit(solution)/shard_map/ppermute | solution.py:23
  104.5 4.7 %collective-permute-done.16.refs_2_ = bf16[512,256]{1,0:T(8,128)(2,1)S(1)} collective-permute-done((bf16[512,256]{1,0:T(8,128)(2,1)S(1)}, bf16[512,256]{1,0:T(8,128)(2,1)S(1)}, u32[]{:S(2)}, u32[]{:S(2)}) %collective-permute-start.16) | collective-permute-done | bytes 262176 | tf_op jit(solution)/shard_map/ppermute | solution.py:23
  109.2 1.4 %collective-permute-done.15.refs_1_ = bf16[512,256]{1,0:T(8,128)(2,1)S(1)} collective-permute-done((bf16[512,256]{1,0:T(8,128)(2,1)S(1)}, bf16[512,256]{1,0:T(8,128)(2,1)S(1)}, u32[]{:S(2)}, u32[]{:S(2)}) %collective-permute-start.15) | collective-permute-done | bytes 262176 | tf_op jit(solution)/shard_map/ppermute | solution.py:23
  110.6 5.6 %weight_grads.1 = (f32[1024,128]{1,0:T(8,128)}, f32[1024,128]{1,0:T(8,128)}) custom-call(s32[2]{0:T(128)S(1)} %pad_add_fusion.place, bf16[512,256]{1,0:T(8,128)(2,1)S(1)} %pad_maximum_fusion.1.refs_0_, bf16[512,256]{1,0:T(8,128)(2,1)S(1)} %collective-permute-done.15.refs_1_, bf16[512,256]{1,0:T(8,128)(2,1)S(1)} %collective-permute-done.16.refs_2_, ...), custom_call_target="tpu_custom_call" | custom-call | tf_op jit(solution)/shard_map/weight_grads/pallas_call | solution.py:181
  (33 shorter events, 1.8 us)
Async XLA Ops:
  2.2 8.9 %collective-permute-start.2 = (bf16[1,128,256]{2,1,0:T(8,128)(2,1)S(1)}, bf16[1,128,256]{2,1,0:T(8,128)(2,1)S(1)}, u32[]{:S(2)}, u32[]{:S(2)}) collective-permute-start(bf16[1,128,256]{2,1,0:T(8,128)(2,1)S(1)} %constant_dynamic-update-slice_fusion), channel_id=1, source_target_pairs={{0,24},{2,26},{4,28},{6,30},{8,16},{10,18},{12,20},{14,22},{16,8},... | collective-permute-start | bytes 196616 | tf_op jit(solution)/shard_map/ppermute | solution.py:23
  7.3 5.6 %collective-permute-start.1 = (bf16[1,128,256]{2,1,0:T(8,128)(2,1)S(1)}, bf16[1,128,256]{2,1,0:T(8,128)(2,1)S(1)}, u32[]{:S(2)}, u32[]{:S(2)}) collective-permute-start(bf16[1,128,256]{2,1,0:T(8,128)(2,1)S(1)} %constant_dynamic-update-slice_fusion), channel_id=1, source_target_pairs={{0,16},{2,18},{4,20},{6,22},{8,24},{10,26},{12,28},{14,30},{16,0},... | collective-permute-start | bytes 196616 | tf_op jit(solution)/shard_map/ppermute | solution.py:23
  7.3 5.6 %collective-permute-start = (bf16[1,128,256]{2,1,0:T(8,128)(2,1)S(1)}, bf16[1,128,256]{2,1,0:T(8,128)(2,1)S(1)}, u32[]{:S(2)}, u32[]{:S(2)}) collective-permute-start(bf16[1,128,256]{2,1,0:T(8,128)(2,1)S(1)} %constant_dynamic-update-slice_fusion), channel_id=1, source_target_pairs={{0,8},{2,10},{4,12},{6,14},{8,0},{10,2},{12,4},{14,6},{16,24},{18,... | collective-permute-start | bytes 196616 | tf_op jit(solution)/shard_map/ppermute | solution.py:23
  13.6 10.9 %copy-start = (bf16[1,128,2048]{2,1,0:T(8,128)(2,1)S(1)}, bf16[1,128,2048]{2,1,0:T(8,128)(2,1)}, u32[]{:S(2)}) copy-start(bf16[1,128,2048]{2,1,0:T(8,128)(2,1)} %param.12) | copy-start | bytes 1572868
  13.6 71.5 %all-to-all-start = ((bf16[16,64,1024]{2,1,0:T(8,128)(2,1)}), bf16[16,64,1024]{2,1,0:T(8,128)(2,1)S(1)}, u32[]{:S(2)}, u32[]{:S(2)}) async-start(bf16[16,64,1024]{2,1,0:T(8,128)(2,1)} %bitcast.41), calls=%async_computation | async-start | bytes 4194304 | tf_op jit(solution)/shard_map/all_to_all | solution.py:218
  19.7 29.2 %copy-start.1 = (bf16[1,128,2048]{2,1,0:T(8,128)(2,1)S(1)}, bf16[1,128,2048]{2,1,0:T(8,128)(2,1)}, u32[]{:S(2)}) copy-start(bf16[1,128,2048]{2,1,0:T(8,128)(2,1)} %param.8) | copy-start | bytes 1572868
  19.8 29.2 %copy-start.2 = (s32[32]{0:T(128)S(1)}, s32[32]{0:T(128)}, u32[]{:S(2)}) copy-start(s32[32]{0:T(128)} %slots.1) | copy-start | bytes 388
  19.8 29.2 %copy-start.3 = (s32[1,16]{1,0:T(1,128)S(1)}, s32[1,16]{1,0:T(1,128)}, u32[]{:S(2)}) copy-start(s32[1,16]{1,0:T(1,128)} %param.14) | copy-start | bytes 196
  19.8 17.7 %collective-permute-start.5 = (bf16[1,512,256]{2,1,0:T(8,128)(2,1)}, bf16[1,512,256]{2,1,0:T(8,128)(2,1)}, u32[]{:S(2)}, u32[]{:S(2)}) collective-permute-start(bf16[1,512,256]{2,1,0:T(8,128)(2,1)} %get-tuple-element.26), channel_id=1, source_target_pairs={{0,6},{2,4},{4,2},{6,0},{8,14},{10,12},{12,10},{14,8},{16,22},{18,... | collective-permute-start | bytes 786440 | tf_op jit(solution)/shard_map/ppermute | solution.py:23
  22.7 26.3 %collective-permute-start.4 = (bf16[1,512,256]{2,1,0:T(8,128)(2,1)}, bf16[1,512,256]{2,1,0:T(8,128)(2,1)}, u32[]{:S(2)}, u32[]{:S(2)}) collective-permute-start(bf16[1,512,256]{2,1,0:T(8,128)(2,1)} %get-tuple-element.26), channel_id=1, source_target_pairs={{0,4},{2,6},{4,0},{6,2},{8,12},{10,14},{12,8},{14,10},{16,20},{18,... | collective-permute-start | bytes 786440 | tf_op jit(solution)/shard_map/ppermute | solution.py:23
  23.2 25.7 %collective-permute-start.3 = (bf16[1,512,256]{2,1,0:T(8,128)(2,1)}, bf16[1,512,256]{2,1,0:T(8,128)(2,1)}, u32[]{:S(2)}, u32[]{:S(2)}) collective-permute-start(bf16[1,512,256]{2,1,0:T(8,128)(2,1)} %get-tuple-element.26), channel_id=1, source_target_pairs={{0,2},{2,0},{4,6},{6,4},{8,10},{10,8},{12,14},{14,12},{16,18},{18,... | collective-permute-start | bytes 786440 | tf_op jit(solution)/shard_map/ppermute | solution.py:23
  57.6 10.1 %collective-permute-start.6 = (bf16[512,256]{1,0:T(8,128)(2,1)S(1)}, bf16[512,256]{1,0:T(8,128)(2,1)S(1)}, u32[]{:S(2)}, u32[]{:S(2)}) collective-permute-start(bf16[512,256]{1,0:T(8,128)(2,1)S(1)} %get-tuple-element.14), channel_id=1, source_target_pairs={{0,2},{2,0},{4,6},{6,4},{8,10},{10,8},{12,14},{14,12},{16,18},{18,... | collective-permute-start | bytes 786440 | tf_op jit(solution)/shard_map/ppermute | solution.py:23
  57.6 15.1 %collective-permute-start.7 = (bf16[512,256]{1,0:T(8,128)(2,1)S(1)}, bf16[512,256]{1,0:T(8,128)(2,1)S(1)}, u32[]{:S(2)}, u32[]{:S(2)}) collective-permute-start(bf16[512,256]{1,0:T(8,128)(2,1)S(1)} %get-tuple-element.15), channel_id=1, source_target_pairs={{0,4},{2,6},{4,0},{6,2},{8,12},{10,14},{12,8},{14,10},{16,20},{18,... | collective-permute-start | bytes 786440 | tf_op jit(solution)/shard_map/ppermute | solution.py:23
  62.5 12.3 %collective-permute-start.8 = (bf16[512,256]{1,0:T(8,128)(2,1)S(1)}, bf16[512,256]{1,0:T(8,128)(2,1)S(1)}, u32[]{:S(2)}, u32[]{:S(2)}) collective-permute-start(bf16[512,256]{1,0:T(8,128)(2,1)S(1)} %get-tuple-element.16), channel_id=1, source_target_pairs={{0,6},{2,4},{4,2},{6,0},{8,14},{10,12},{12,10},{14,8},{16,22},{18,... | collective-permute-start | bytes 786440 | tf_op jit(solution)/shard_map/ppermute | solution.py:23
  74.9 4.4 %collective-permute-start.9 = (bf16[128,256]{1,0:T(8,128)(2,1)S(1)}, bf16[128,256]{1,0:T(8,128)(2,1)S(1)}, u32[]{:S(2)}, u32[]{:S(2)}) collective-permute-start(bf16[128,256]{1,0:T(8,128)(2,1)S(1)} %get-tuple-element.23), channel_id=1, source_target_pairs={{0,8},{2,10},{4,12},{6,14},{8,0},{10,2},{12,4},{14,6},{16,24},{18,... | collective-permute-start | bytes 196616 | tf_op jit(solution)/shard_map/ppermute | solution.py:23
  75.4 7.1 %collective-permute-start.11 = (bf16[128,256]{1,0:T(8,128)(2,1)S(1)}, bf16[128,256]{1,0:T(8,128)(2,1)S(1)}, u32[]{:S(2)}, u32[]{:S(2)}) collective-permute-start(bf16[128,256]{1,0:T(8,128)(2,1)S(1)} %get-tuple-element.24), channel_id=1, source_target_pairs={{0,24},{2,26},{4,28},{6,30},{8,16},{10,18},{12,20},{14,22},{16,8},... | collective-permute-start | bytes 196616 | tf_op jit(solution)/shard_map/ppermute | solution.py:23
  78.8 6.2 %collective-permute-start.10 = (bf16[128,256]{1,0:T(8,128)(2,1)S(1)}, bf16[128,256]{1,0:T(8,128)(2,1)S(1)}, u32[]{:S(2)}, u32[]{:S(2)}) collective-permute-start(bf16[128,256]{1,0:T(8,128)(2,1)S(1)} %get-tuple-element.25), channel_id=1, source_target_pairs={{0,16},{2,18},{4,20},{6,22},{8,24},{10,26},{12,28},{14,30},{16,0},... | collective-permute-start | bytes 196616 | tf_op jit(solution)/shard_map/ppermute | solution.py:23
  85.1 25.4 %collective-permute-start.18 = (bf16[16,64,1024]{2,1,0:T(8,128)(2,1)S(1)}, bf16[16,64,1024]{2,1,0:T(8,128)(2,1)}, u32[]{:S(2)}, u32[]{:S(2)}) collective-permute-start(bf16[16,64,1024]{2,1,0:T(8,128)(2,1)S(1)} %all-to-all-done), channel_id=1, source_target_pairs={{0,1},{1,0},{2,3},{3,2},{4,5},{5,4},{6,7},{7,6},{8,9},{9,8},{10,11... | collective-permute-start | bytes 6291464 | tf_op jit(solution)/shard_map/ppermute | solution.py:244
  85.2 6.9 %collective-permute-start.14 = (bf16[128,256]{1,0:T(8,128)(2,1)S(1)}, bf16[128,256]{1,0:T(8,128)(2,1)S(1)}, u32[]{:S(2)}, u32[]{:S(2)}) collective-permute-start(bf16[128,256]{1,0:T(8,128)(2,1)S(1)} %fusion.3), channel_id=1, source_target_pairs={{0,24},{2,26},{4,28},{6,30},{8,16},{10,18},{12,20},{14,22},{16,8},... | collective-permute-start | bytes 196616 | tf_op jit(solution)/shard_map/ppermute | solution.py:23
  87.2 7.1 %collective-permute-start.13 = (bf16[128,256]{1,0:T(8,128)(2,1)S(1)}, bf16[128,256]{1,0:T(8,128)(2,1)S(1)}, u32[]{:S(2)}, u32[]{:S(2)}) collective-permute-start(bf16[128,256]{1,0:T(8,128)(2,1)S(1)} %fusion.3), channel_id=1, source_target_pairs={{0,16},{2,18},{4,20},{6,22},{8,24},{10,26},{12,28},{14,30},{16,0},... | collective-permute-start | bytes 196616 | tf_op jit(solution)/shard_map/ppermute | solution.py:23
  87.2 7.1 %collective-permute-start.12 = (bf16[128,256]{1,0:T(8,128)(2,1)S(1)}, bf16[128,256]{1,0:T(8,128)(2,1)S(1)}, u32[]{:S(2)}, u32[]{:S(2)}) collective-permute-start(bf16[128,256]{1,0:T(8,128)(2,1)S(1)} %fusion.3), channel_id=1, source_target_pairs={{0,8},{2,10},{4,12},{6,14},{8,0},{10,2},{12,4},{14,6},{16,24},{18,... | collective-permute-start | bytes 196616 | tf_op jit(solution)/shard_map/ppermute | solution.py:23
  94.4 10.2 %collective-permute-start.17 = (bf16[512,256]{1,0:T(8,128)(2,1)S(1)}, bf16[512,256]{1,0:T(8,128)(2,1)S(1)}, u32[]{:S(2)}, u32[]{:S(2)}) collective-permute-start(bf16[512,256]{1,0:T(8,128)(2,1)S(1)} %pad_maximum_fusion.1.refs_0_), channel_id=1, source_target_pairs={{0,6},{2,4},{4,2},{6,0},{8,14},{10,12},{12,10},{14,8},{16,22},{18,... | collective-permute-start | bytes 786440 | tf_op jit(solution)/shard_map/ppermute | solution.py:23
  97.1 12.1 %collective-permute-start.16 = (bf16[512,256]{1,0:T(8,128)(2,1)S(1)}, bf16[512,256]{1,0:T(8,128)(2,1)S(1)}, u32[]{:S(2)}, u32[]{:S(2)}) collective-permute-start(bf16[512,256]{1,0:T(8,128)(2,1)S(1)} %pad_maximum_fusion.1.refs_0_), channel_id=1, source_target_pairs={{0,4},{2,6},{4,0},{6,2},{8,12},{10,14},{12,8},{14,10},{16,20},{18,... | collective-permute-start | bytes 786440 | tf_op jit(solution)/shard_map/ppermute | solution.py:23
  97.3 13.3 %collective-permute-start.15 = (bf16[512,256]{1,0:T(8,128)(2,1)S(1)}, bf16[512,256]{1,0:T(8,128)(2,1)S(1)}, u32[]{:S(2)}, u32[]{:S(2)}) collective-permute-start(bf16[512,256]{1,0:T(8,128)(2,1)S(1)} %pad_maximum_fusion.1.refs_0_), channel_id=1, source_target_pairs={{0,2},{2,0},{4,6},{6,4},{8,10},{10,8},{12,14},{14,12},{16,18},{18,... | collective-permute-start | bytes 786440 | tf_op jit(solution)/shard_map/ppermute | solution.py:23

commit v3 on v2

--- a/solution.py
+++ b/solution.py
@@ -150,47 +150,47 @@
     )(me, slots, docs, queries, grad_out, delta, *key_values)
 
 
-def weight_kernel(place, *refs, low, parts, rows, head):
-    grad_refs, column_refs, (key_ref, value_ref, sums) = refs[:low], refs[low : low + parts], refs[low + parts :]
-    step = pl.program_id(0)
+def weight_kernel(place, grad_ref, *refs, low, parts, rows, digit, head):
+    column_refs, refs = refs[:parts], refs[parts:]
     own_high, own_part = place[0] // low, place[1]
     high = column_refs[0].shape[0]
-    tokens = jnp.concatenate([ref[h, 0] for ref in column_refs for h in range(high)], axis=0)
-
-    for digit in range(low):
-
-        @pl.when(step == digit)
-        def _():
-            starts = [((h ^ own_high) * parts + (part ^ own_part)) * rows for part in range(parts) for h in range(high)]
-            grads = jnp.concatenate([grad_refs[digit][pl.ds(pl.multiple_of(s, rows), rows), :] for s in starts], axis=0)
-            found = dot(grads, tokens, TN)
-            sums[...] = found if digit == 0 else sums[...] + found
-
-    @pl.when(step == low - 1)
-    def _():
-        key_ref[...] = sums[:head, :].T
-        value_ref[...] = sums[head:, :].T
-
-
-def weight_grads(place, columns, grads, head):
+    tokens = jnp.concatenate([ref[...].reshape(high * rows, ref.shape[-1]) for ref in column_refs], axis=0)
+    starts = [((h ^ own_high) * parts + (part ^ own_part)) * rows for part in range(parts) for h in range(high)]
+    grads = jnp.concatenate([grad_ref[pl.ds(pl.multiple_of(s, rows), rows), :] for s in starts], axis=0)
+    found = dot(grads, tokens, TN)
+    if digit:
+        found = refs[0][...] + found
+    if digit == low - 1:
+        refs[-2][...] = found[:head, :].T
+        refs[-1][...] = found[head:, :].T
+    else:
+        refs[-1][...] = found
+
+
+def weight_step(place, digit, low, columns, grads, sums, head):
     count, rows, width = columns[0].shape
-    low, parts = len(grads), len(columns)
-    spec = pl.BlockSpec((count // low, 1, rows, width), lambda i, place: (0, (place[0] % low) ^ i, 0, 0))
-    whole = pl.BlockSpec(grads[0].shape, lambda i, place: (0, 0))
-    out = pl.BlockSpec((width, head), lambda i, place: (0, 0))
+    parts = len(columns)
+    spec = pl.BlockSpec((count // low, 1, rows, width), lambda i, place: (0, (place[0] % low) ^ digit, 0, 0))
+    shapes = ((width, head),) * 2 if digit == low - 1 else ((2 * head, width),)
+    before = [sums] if digit else []
     return pl.pallas_call(
-        functools.partial(weight_kernel, low=low, parts=parts, rows=rows, head=head),
-        out_shape=(jax.ShapeDtypeStruct((width, head), jnp.float32),) * 2,
+        functools.partial(weight_kernel, low=low, parts=parts, rows=rows, digit=digit, head=head),
+        out_shape=tuple(jax.ShapeDtypeStruct(s, jnp.float32) for s in shapes),
         grid_spec=pltpu.PrefetchScalarGridSpec(
             num_scalar_prefetch=1,
-            grid=(low,),
-            in_specs=[whole] * low + [spec] * parts,
-            out_specs=(out, out),
-            scratch_shapes=[pltpu.VMEM((2 * head, width), jnp.float32)],
+            grid=(1,),
+            in_specs=[pl.BlockSpec(grads.shape, lambda i, place: (0, 0))]
+            + [spec] * parts
+            + [pl.BlockSpec((2 * head, width), lambda i, place: (0, 0))] * len(before),
+            out_specs=tuple(pl.BlockSpec(s, lambda i, place: (0, 0)) for s in shapes),
         ),
         compiler_params=pltpu.CompilerParams(vmem_limit_bytes=32 << 20),
-        name="weight_grads",
-    )(place, *grads, *(c.reshape(count // low, low, rows, width) for c in columns))
+        name="weight_step",
+    )(place, grads, *(c.reshape(count // low, low, rows, width) for c in columns), *before)
+
+
+def after(value, *others):
+    return lax.optimization_barrier((value, *others))[0]
 
 
 def on_device(queries, keys, values, outputs, grad_out, inputs, block_doc, span_slots):
@@ -209,12 +209,13 @@
     me = lax.axis_index("context").astype(jnp.int32).reshape(1)
 
     own = jnp.concatenate([keys, values], axis=2)
-    column = jnp.concatenate([own] + [swap(own, k * low, count) for k in range(1, high)], axis=1)
+    by_high = [own] + [swap(own, k * low, count) for k in range(1, high)]
+    column = jnp.concatenate(by_high, axis=1)
     key_values = [column] + [swap(column, k, count) for k in range(1, low)]
 
     sent = inputs.reshape(batch_count, token_rows, count, column_count)
     sent = jnp.moveaxis(sent, 2, 0).reshape(count, batch_count * token_rows, column_count)
-    sent, _ = lax.optimization_barrier((sent, column))
+    sent = after(sent, column)
     mine = lax.all_to_all(sent, "context", split_axis=0, concat_axis=0, tiled=True)
 
     delta = jnp.einsum(
@@ -239,12 +240,14 @@
         own_grads = sum(p.astype(jnp.float32) for p in arrived).astype(jnp.bfloat16)
         column = jnp.concatenate([own_grads] + [swap(own_grads, k * low, count) for k in range(1, high)], axis=0)
         columns = [column] + [swap(column, k, count) for k in range(1, low)]
-        late, _ = lax.optimization_barrier((mine[:, b * token_rows : (b + 1) * token_rows], own_grads))
+        late = after(mine[:, b * token_rows : (b + 1) * token_rows], own_grads)
         parts = [late] + [
             lax.ppermute(late, "tensor", [(i, i ^ k) for i in range(tensor_count)]) for k in range(1, tensor_count)
         ]
-        key_part, value_part = weight_grads(place, parts, columns, head)
-        key_sums, value_sums = key_sums + key_part, value_sums + value_part
+        found = [None]
+        for k in range(low):
+            found = weight_step(place, k, low, parts, columns[k], found[0], head)
+        key_sums, value_sums = key_sums + found[0], value_sums + found[1]
     return jnp.stack(query_grads), lax.psum(key_sums, "dp"), lax.psum(value_sums, "dp")
 
 

time: 117 us -> 112 us (0.957); the launches traced: 116 us -> 112 us
  waiting for transfers between devices: 60.1 us -> 55.5 us
    ppermute x18, waiting for transfers between devices: 60.1 us -> 55.5 us  [swap(): lax.ppermute(value, 'context', [(i, i ^ offset) for i in range(count)])]
    pallas_call x1 -> x4, Pallas kernels: 5.6 us -> 9.41 us  [weight_step(): pl.pallas_call(functools.partial(weight_kernel, low=low, parts=parts, row...]
    pallas_call x1, Pallas kernels: 8.69 us -> 5.41 us  [attention_grads(): pl.pallas_call(body, out_shape=(jax.ShapeDtypeStruct((rows, width), jnp.b...]
    ppermute x18, starting transfers between devices: 27.4 us -> 28.6 us  [swap(): lax.ppermute(value, 'context', [(i, i ^ offset) for i in range(count)])]
  transfers between devices with their start and end apart: 20 -> 20, of which waited for: 13 -> 11; matrix products, arithmetic and copies ran while one was open for 4% -> 5% of each run, Pallas kernels for 7% -> 10%
where the time goes in v3:
time: 112 us
  waiting for transfers between devices  55.5 us (50%)
  starting transfers between devices  33.8 us (30%)
  Pallas kernels  14.8 us (13%)
  local copies, waits for them, and re-layouts  6.15 us (5%)
  other arithmetic  1.35 us (1%)
    ppermute x18, waiting for transfers between devices, swap(): lax.ppermute(value, 'context', [(i, i ^ offset) for i in range(count)])  55.5 us
    ppermute x18, starting transfers between devices, swap(): lax.ppermute(value, 'context', [(i, i ^ offset) for i in range(count)])  28.6 us
    pallas_call x4, Pallas kernels, weight_step(): pl.pallas_call(functools.partial(weight_kernel, low=low, parts=parts, row...  9.41 us
    pallas_call x1, Pallas kernels, attention_grads(): pl.pallas_call(body, out_shape=(jax.ShapeDtypeStruct((rows, width), jnp.b...  5.41 us
    all_to_all x1, starting transfers between devices, on_device(): lax.all_to_all(sent, 'context', split_axis=0, concat_axis=0, tiled=True)  5.17 us
    reshape x1, local copies, waits for them, and re-layouts, on_device(): sent = inputs.reshape(batch_count, token_rows, count, column_count)  3.16 us
  transfers between devices with their start and end apart: 20, of which 11 were waited for; matrix products, arithmetic and copies ran while one was open for 5% of the time, Pallas kernels for 10%

profile of v3, /device:TPU:0, one launch (start us, length us, event | category | flops | bytes accessed | tf_op | source)
XLA Modules:
  0.0 112.5 jit_solution(16687103795269498127)
XLA Ops:
  0.6 0.8 constant_dynamic-update-slice_fusion.1
  1.4 0.8 constant_dynamic-update-slice_fusion
  2.2 3.1 %collective-permute-start = (bf16[1,128,256]{2,1,0:T(8,128)(2,1)S(1)}, bf16[1,128,256]{2,1,0:T(8,128)(2,1)S(1)}, u32[]{:S(2)}, u32[]{:S(2)}) collective-permute-start(bf16[1,128,256]{2,1,0:T(8,128)(2,1)S(1)} %constant_dynamic-update-slice_fusion), channel_id=1, source_target_pairs={{0,8},{2,10},{4,12},{6,14},{8,0},{10,2},{12,4},{14,6},{16,24},{18,... | collective-permute-start | bytes 196616 | tf_op jit(solution)/shard_map/ppermute | solution.py:23
  5.2 2.6 %collective-permute-start.1 = (bf16[1,128,256]{2,1,0:T(8,128)(2,1)S(1)}, bf16[1,128,256]{2,1,0:T(8,128)(2,1)S(1)}, u32[]{:S(2)}, u32[]{:S(2)}) collective-permute-start(bf16[1,128,256]{2,1,0:T(8,128)(2,1)S(1)} %constant_dynamic-update-slice_fusion), channel_id=1, source_target_pairs={{0,16},{2,18},{4,20},{6,22},{8,24},{10,26},{12,28},{14,30},{16,0},... | collective-permute-start | bytes 196616 | tf_op jit(solution)/shard_map/ppermute | solution.py:23
  7.8 3.2 %copy.27 = bf16[1,8,16,8,1024]{4,3,1,2,0:T(8,128)(2,1)} copy(bf16[1,8,16,8,1024]{4,3,2,1,0:T(8,128)(2,1)} %bitcast.45) | data formatting | bytes 4194304 | tf_op jit(solution)/shard_map/reshape | solution.py:216
  11.0 1.5 %collective-permute-done.1 = bf16[1,128,256]{2,1,0:T(8,128)(2,1)S(1)} collective-permute-done((bf16[1,128,256]{2,1,0:T(8,128)(2,1)S(1)}, bf16[1,128,256]{2,1,0:T(8,128)(2,1)S(1)}, u32[]{:S(2)}, u32[]{:S(2)}) %collective-permute-start.1) | collective-permute-done | bytes 65568 | tf_op jit(solution)/shard_map/ppermute | solution.py:23
  12.5 1.4 %collective-permute-done.2 = bf16[1,128,256]{2,1,0:T(8,128)(2,1)S(1)} collective-permute-done((bf16[1,128,256]{2,1,0:T(8,128)(2,1)S(1)}, bf16[1,128,256]{2,1,0:T(8,128)(2,1)S(1)}, u32[]{:S(2)}, u32[]{:S(2)}) %collective-permute-start.2) | collective-permute-done | bytes 65568 | tf_op jit(solution)/shard_map/ppermute | solution.py:23
  14.7 5.2 %all-to-all-start = ((bf16[16,64,1024]{2,1,0:T(8,128)(2,1)}), bf16[16,64,1024]{2,1,0:T(8,128)(2,1)S(1)}, u32[]{:S(2)}, u32[]{:S(2)}) async-start(bf16[16,64,1024]{2,1,0:T(8,128)(2,1)} %bitcast.44), calls=%async_computation | async-start | bytes 4194304 | tf_op jit(solution)/shard_map/all_to_all | solution.py:219
  19.9 2.0 %collective-permute-start.4 = (bf16[1,512,256]{2,1,0:T(8,128)(2,1)}, bf16[1,512,256]{2,1,0:T(8,128)(2,1)}, u32[]{:S(2)}, u32[]{:S(2)}) collective-permute-start(bf16[1,512,256]{2,1,0:T(8,128)(2,1)} %get-tuple-element.26), channel_id=1, source_target_pairs={{0,4},{2,6},{4,0},{6,2},{8,12},{10,14},{12,8},{14,10},{16,20},{18,... | collective-permute-start | bytes 786440 | tf_op jit(solution)/shard_map/ppermute | solution.py:23
  21.9 1.5 %collective-permute-start.5 = (bf16[1,512,256]{2,1,0:T(8,128)(2,1)}, bf16[1,512,256]{2,1,0:T(8,128)(2,1)}, u32[]{:S(2)}, u32[]{:S(2)}) collective-permute-start(bf16[1,512,256]{2,1,0:T(8,128)(2,1)} %get-tuple-element.26), channel_id=1, source_target_pairs={{0,6},{2,4},{4,2},{6,0},{8,14},{10,12},{12,10},{14,8},{16,22},{18,... | collective-permute-start | bytes 786440 | tf_op jit(solution)/shard_map/ppermute | solution.py:23
  23.5 1.1 %copy.25 = bf16[16,8,16,128]{3,2,1,0:T(8,128)(2,1)S(1)} copy(bf16[16,8,16,128]{3,1,2,0:T(8,128)(2,1)} %bitcast.48) | data formatting | bytes 1048576
  25.2 23.7 %collective-permute-done.4 = bf16[1,512,256]{2,1,0:T(8,128)(2,1)} collective-permute-done((bf16[1,512,256]{2,1,0:T(8,128)(2,1)}, bf16[1,512,256]{2,1,0:T(8,128)(2,1)}, u32[]{:S(2)}, u32[]{:S(2)}) %collective-permute-start.4) | collective-permute-done | bytes 262176 | tf_op jit(solution)/shard_map/ppermute | solution.py:23
  48.9 5.4 %attention_grads.1 = (bf16[128,2048]{1,0:T(8,128)(2,1)}, bf16[512,256]{1,0:T(8,128)(2,1)S(1)}, bf16[512,256]{1,0:T(8,128)(2,1)S(1)}, bf16[512,256]{1,0:T(8,128)(2,1)S(1)}, bf16[512,256]{1,0:T(8,128)(2,1)S(1)}) custom-call(s32[1]{0:T(128)} %bitcast.2.me, s32[32]{0:T(128)S(1)} %copy-done.2, s32[16]{0:T(128)S(1)} %bitcast.43, bf16[128,2048]{1,0:T(8,128)(2,1)S(1)} %bitcast.42, ...), custom_call_target="tpu_custom_call" | custom-call | tf_op jit(solution)/shard_map/attention_grads/pallas_call | solution.py:131
  54.3 5.6 %collective-permute-start.6 = (bf16[512,256]{1,0:T(8,128)(2,1)S(1)}, bf16[512,256]{1,0:T(8,128)(2,1)S(1)}, u32[]{:S(2)}, u32[]{:S(2)}) collective-permute-start(bf16[512,256]{1,0:T(8,128)(2,1)S(1)} %get-tuple-element.14), channel_id=1, source_target_pairs={{0,2},{2,0},{4,6},{6,4},{8,10},{10,8},{12,14},{14,12},{16,18},{18,... | collective-permute-start | bytes 786440 | tf_op jit(solution)/shard_map/ppermute | solution.py:23
  60.3 1.2 %collective-permute-start.8 = (bf16[512,256]{1,0:T(8,128)(2,1)S(1)}, bf16[512,256]{1,0:T(8,128)(2,1)S(1)}, u32[]{:S(2)}, u32[]{:S(2)}) collective-permute-start(bf16[512,256]{1,0:T(8,128)(2,1)S(1)} %get-tuple-element.16), channel_id=1, source_target_pairs={{0,6},{2,4},{4,2},{6,0},{8,14},{10,12},{12,10},{14,8},{16,22},{18,... | collective-permute-start | bytes 786440 | tf_op jit(solution)/shard_map/ppermute | solution.py:23
  61.5 6.5 %collective-permute-done.6 = bf16[512,256]{1,0:T(8,128)(2,1)S(1)} collective-permute-done((bf16[512,256]{1,0:T(8,128)(2,1)S(1)}, bf16[512,256]{1,0:T(8,128)(2,1)S(1)}, u32[]{:S(2)}, u32[]{:S(2)}) %collective-permute-start.6) | collective-permute-done | bytes 262176 | tf_op jit(solution)/shard_map/ppermute | solution.py:23
  67.9 6.8 %collective-permute-done.8 = bf16[512,256]{1,0:T(8,128)(2,1)S(1)} collective-permute-done((bf16[512,256]{1,0:T(8,128)(2,1)S(1)}, bf16[512,256]{1,0:T(8,128)(2,1)S(1)}, u32[]{:S(2)}, u32[]{:S(2)}) %collective-permute-start.8) | collective-permute-done | bytes 262176 | tf_op jit(solution)/shard_map/ppermute | solution.py:23
  75.0 3.7 %collective-permute-start.11 = (bf16[128,256]{1,0:T(8,128)(2,1)S(1)}, bf16[128,256]{1,0:T(8,128)(2,1)S(1)}, u32[]{:S(2)}, u32[]{:S(2)}) collective-permute-start(bf16[128,256]{1,0:T(8,128)(2,1)S(1)} %get-tuple-element.24), channel_id=1, source_target_pairs={{0,24},{2,26},{4,28},{6,30},{8,16},{10,18},{12,20},{14,22},{16,8},... | collective-permute-start | bytes 196616 | tf_op jit(solution)/shard_map/ppermute | solution.py:23
  79.2 3.8 %collective-permute-done.10 = bf16[128,256]{1,0:T(8,128)(2,1)S(1)} collective-permute-done((bf16[128,256]{1,0:T(8,128)(2,1)S(1)}, bf16[128,256]{1,0:T(8,128)(2,1)S(1)}, u32[]{:S(2)}, u32[]{:S(2)}) %collective-permute-start.10) | collective-permute-done | bytes 65568 | tf_op jit(solution)/shard_map/ppermute | solution.py:23
  83.4 1.2 %collective-permute-start.12 = (bf16[128,256]{1,0:T(8,128)(2,1)S(1)}, bf16[128,256]{1,0:T(8,128)(2,1)S(1)}, u32[]{:S(2)}, u32[]{:S(2)}) collective-permute-start(bf16[128,256]{1,0:T(8,128)(2,1)S(1)} %fusion.3), channel_id=1, source_target_pairs={{0,8},{2,10},{4,12},{6,14},{8,0},{10,2},{12,4},{14,6},{16,24},{18,... | collective-permute-start | bytes 196616 | tf_op jit(solution)/shard_map/ppermute | solution.py:23
  84.7 1.4 %collective-permute-start.13 = (bf16[128,256]{1,0:T(8,128)(2,1)S(1)}, bf16[128,256]{1,0:T(8,128)(2,1)S(1)}, u32[]{:S(2)}, u32[]{:S(2)}) collective-permute-start(bf16[128,256]{1,0:T(8,128)(2,1)S(1)} %fusion.3), channel_id=1, source_target_pairs={{0,16},{2,18},{4,20},{6,22},{8,24},{10,26},{12,28},{14,30},{16,0},... | collective-permute-start | bytes 196616 | tf_op jit(solution)/shard_map/ppermute | solution.py:23
  86.1 1.8 %collective-permute-start.14 = (bf16[128,256]{1,0:T(8,128)(2,1)S(1)}, bf16[128,256]{1,0:T(8,128)(2,1)S(1)}, u32[]{:S(2)}, u32[]{:S(2)}) collective-permute-start(bf16[128,256]{1,0:T(8,128)(2,1)S(1)} %fusion.3), channel_id=1, source_target_pairs={{0,24},{2,26},{4,28},{6,30},{8,16},{10,18},{12,20},{14,22},{16,8},... | collective-permute-start | bytes 196616 | tf_op jit(solution)/shard_map/ppermute | solution.py:23
  87.9 5.1 %collective-permute-done.13 = bf16[128,256]{1,0:T(8,128)(2,1)S(1)} collective-permute-done((bf16[128,256]{1,0:T(8,128)(2,1)S(1)}, bf16[128,256]{1,0:T(8,128)(2,1)S(1)}, u32[]{:S(2)}, u32[]{:S(2)}) %collective-permute-start.13) | collective-permute-done | bytes 65568 | tf_op jit(solution)/shard_map/ppermute | solution.py:23
  93.0 1.2 %collective-permute-start.18 = (bf16[512,256]{1,0:T(8,128)(2,1)S(1)}, bf16[512,256]{1,0:T(8,128)(2,1)S(1)}, u32[]{:S(2)}, u32[]{:S(2)}) collective-permute-start(bf16[512,256]{1,0:T(8,128)(2,1)S(1)} %pad_maximum_fusion.1.grad_ref), channel_id=1, source_target_pairs={{0,2},{2,0},{4,6},{6,4},{8,10},{10,8},{12,14},{14,12},{16,18},{18,... | collective-permute-start | bytes 786440 | tf_op jit(solution)/shard_map/ppermute | solution.py:23
  94.2 0.8 collective-permute-start.17
  95.0 1.6 %collective-permute-start.15 = (bf16[512,256]{1,0:T(8,128)(2,1)S(1)}, bf16[512,256]{1,0:T(8,128)(2,1)S(1)}, u32[]{:S(2)}, u32[]{:S(2)}) collective-permute-start(bf16[512,256]{1,0:T(8,128)(2,1)S(1)} %pad_maximum_fusion.1.grad_ref), channel_id=1, source_target_pairs={{0,6},{2,4},{4,2},{6,0},{8,14},{10,12},{12,10},{14,8},{16,22},{18,... | collective-permute-start | bytes 786440 | tf_op jit(solution)/shard_map/ppermute | solution.py:23
  96.7 2.1 %weight_step.4.refs_2_ = f32[256,1024]{1,0:T(8,128)S(1)} custom-call(s32[2]{0:T(128)S(1)} %pad_add_fusion.place, bf16[512,256]{1,0:T(8,128)(2,1)S(1)} %pad_maximum_fusion.1.grad_ref, bf16[4,4,64,1024]{3,2,1,0:T(8,128)(2,1)S(1)} %bitcast.36, bf16[4,4,64,1024]{3,2,1,0:T(8,128)(2,1)} %bitcast.17.refs_1_), custom_call_target="tpu_custom_call" | custom-call | tf_op jit(solution)/shard_map/weight_step/pallas_call | solution.py:176
  98.8 3.6 %collective-permute-done.18.grad_ref = bf16[512,256]{1,0:T(8,128)(2,1)S(1)} collective-permute-done((bf16[512,256]{1,0:T(8,128)(2,1)S(1)}, bf16[512,256]{1,0:T(8,128)(2,1)S(1)}, u32[]{:S(2)}, u32[]{:S(2)}) %collective-permute-start.18) | collective-permute-done | bytes 262176 | tf_op jit(solution)/shard_map/ppermute | solution.py:23
  102.4 2.1 %weight_step.5.refs_2_ = f32[256,1024]{1,0:T(8,128)S(1)} custom-call(s32[2]{0:T(128)S(1)} %pad_add_fusion.place, bf16[512,256]{1,0:T(8,128)(2,1)S(1)} %collective-permute-done.18.grad_ref, bf16[4,4,64,1024]{3,2,1,0:T(8,128)(2,1)S(1)} %bitcast.37, bf16[4,4,64,1024]{3,2,1,0:T(8,128)(2,1)} %bitcast.17.refs_1_, f32[256,1024]{1,0:T(8,128)S(1)} %weight_step.4.refs_2_), custom_call_target="tpu_custom_call" | custom-call | tf_op jit(solution)/shard_map/weight_step/pallas_call | solution.py:176
  104.5 2.8 %collective-permute-done.17.grad_ref = bf16[512,256]{1,0:T(8,128)(2,1)S(1)} collective-permute-done((bf16[512,256]{1,0:T(8,128)(2,1)S(1)}, bf16[512,256]{1,0:T(8,128)(2,1)S(1)}, u32[]{:S(2)}, u32[]{:S(2)}) %collective-permute-start.17) | collective-permute-done | bytes 262176 | tf_op jit(solution)/shard_map/ppermute | solution.py:23
  107.2 2.1 %weight_step.6.refs_2_ = f32[256,1024]{1,0:T(8,128)S(1)} custom-call(s32[2]{0:T(128)S(1)} %pad_add_fusion.place, bf16[512,256]{1,0:T(8,128)(2,1)S(1)} %collective-permute-done.17.grad_ref, bf16[4,4,64,1024]{3,2,1,0:T(8,128)(2,1)S(1)} %bitcast.38, bf16[4,4,64,1024]{3,2,1,0:T(8,128)(2,1)} %bitcast.17.refs_1_, f32[256,1024]{1,0:T(8,128)S(1)} %weight_step.5.refs_2_), custom_call_target="tpu_custom_call" | custom-call | tf_op jit(solution)/shard_map/weight_step/pallas_call | solution.py:176
  109.3 3.1 %weight_step.7 = (f32[1024,128]{1,0:T(8,128)}, f32[1024,128]{1,0:T(8,128)}) custom-call(s32[2]{0:T(128)S(1)} %pad_add_fusion.place, bf16[512,256]{1,0:T(8,128)(2,1)S(1)} %collective-permute-done.15.grad_ref, bf16[4,4,64,1024]{3,2,1,0:T(8,128)(2,1)S(1)} %bitcast.39, bf16[4,4,64,1024]{3,2,1,0:T(8,128)(2,1)} %bitcast.17.refs_1_, f32[256,1024]{1,0:T(8,128)S(1)} %weight_step.6.refs_2_), custom_call_target="tpu_custom_call" | custom-call | tf_op jit(solution)/shard_map/weight_step/pallas_call | solution.py:176
  (36 shorter events, 3.1 us)
Async XLA Ops:
  2.2 8.8 %collective-permute-start = (bf16[1,128,256]{2,1,0:T(8,128)(2,1)S(1)}, bf16[1,128,256]{2,1,0:T(8,128)(2,1)S(1)}, u32[]{:S(2)}, u32[]{:S(2)}) collective-permute-start(bf16[1,128,256]{2,1,0:T(8,128)(2,1)S(1)} %constant_dynamic-update-slice_fusion), channel_id=1, source_target_pairs={{0,8},{2,10},{4,12},{6,14},{8,0},{10,2},{12,4},{14,6},{16,24},{18,... | collective-permute-start | bytes 196616 | tf_op jit(solution)/shard_map/ppermute | solution.py:23
  5.2 7.3 %collective-permute-start.1 = (bf16[1,128,256]{2,1,0:T(8,128)(2,1)S(1)}, bf16[1,128,256]{2,1,0:T(8,128)(2,1)S(1)}, u32[]{:S(2)}, u32[]{:S(2)}) collective-permute-start(bf16[1,128,256]{2,1,0:T(8,128)(2,1)S(1)} %constant_dynamic-update-slice_fusion), channel_id=1, source_target_pairs={{0,16},{2,18},{4,20},{6,22},{8,24},{10,26},{12,28},{14,30},{16,0},... | collective-permute-start | bytes 196616 | tf_op jit(solution)/shard_map/ppermute | solution.py:23
  7.8 6.1 %collective-permute-start.2 = (bf16[1,128,256]{2,1,0:T(8,128)(2,1)S(1)}, bf16[1,128,256]{2,1,0:T(8,128)(2,1)S(1)}, u32[]{:S(2)}, u32[]{:S(2)}) collective-permute-start(bf16[1,128,256]{2,1,0:T(8,128)(2,1)S(1)} %constant_dynamic-update-slice_fusion), channel_id=1, source_target_pairs={{0,24},{2,26},{4,28},{6,30},{8,16},{10,18},{12,20},{14,22},{16,8},... | collective-permute-start | bytes 196616 | tf_op jit(solution)/shard_map/ppermute | solution.py:23
  14.6 8.8 %copy-start = (bf16[1,128,2048]{2,1,0:T(8,128)(2,1)S(1)}, bf16[1,128,2048]{2,1,0:T(8,128)(2,1)}, u32[]{:S(2)}) copy-start(bf16[1,128,2048]{2,1,0:T(8,128)(2,1)} %param.12) | copy-start | bytes 1572868
  14.7 68.7 %all-to-all-start = ((bf16[16,64,1024]{2,1,0:T(8,128)(2,1)}), bf16[16,64,1024]{2,1,0:T(8,128)(2,1)S(1)}, u32[]{:S(2)}, u32[]{:S(2)}) async-start(bf16[16,64,1024]{2,1,0:T(8,128)(2,1)} %bitcast.44), calls=%async_computation | async-start | bytes 4194304 | tf_op jit(solution)/shard_map/all_to_all | solution.py:219
  19.8 29.1 %copy-start.1 = (bf16[1,128,2048]{2,1,0:T(8,128)(2,1)S(1)}, bf16[1,128,2048]{2,1,0:T(8,128)(2,1)}, u32[]{:S(2)}) copy-start(bf16[1,128,2048]{2,1,0:T(8,128)(2,1)} %param.8) | copy-start | bytes 1572868
  19.8 29.1 %copy-start.2 = (s32[32]{0:T(128)S(1)}, s32[32]{0:T(128)}, u32[]{:S(2)}) copy-start(s32[32]{0:T(128)} %slots.1) | copy-start | bytes 388
  19.9 29.1 %copy-start.3 = (s32[1,16]{1,0:T(1,128)S(1)}, s32[1,16]{1,0:T(1,128)}, u32[]{:S(2)}) copy-start(s32[1,16]{1,0:T(1,128)} %param.14) | copy-start | bytes 196
  19.9 29.0 %collective-permute-start.4 = (bf16[1,512,256]{2,1,0:T(8,128)(2,1)}, bf16[1,512,256]{2,1,0:T(8,128)(2,1)}, u32[]{:S(2)}, u32[]{:S(2)}) collective-permute-start(bf16[1,512,256]{2,1,0:T(8,128)(2,1)} %get-tuple-element.26), channel_id=1, source_target_pairs={{0,4},{2,6},{4,0},{6,2},{8,12},{10,14},{12,8},{14,10},{16,20},{18,... | collective-permute-start | bytes 786440 | tf_op jit(solution)/shard_map/ppermute | solution.py:23
  21.9 27.0 %collective-permute-start.5 = (bf16[1,512,256]{2,1,0:T(8,128)(2,1)}, bf16[1,512,256]{2,1,0:T(8,128)(2,1)}, u32[]{:S(2)}, u32[]{:S(2)}) collective-permute-start(bf16[1,512,256]{2,1,0:T(8,128)(2,1)} %get-tuple-element.26), channel_id=1, source_target_pairs={{0,6},{2,4},{4,2},{6,0},{8,14},{10,12},{12,10},{14,8},{16,22},{18,... | collective-permute-start | bytes 786440 | tf_op jit(solution)/shard_map/ppermute | solution.py:23
  23.3 25.6 %collective-permute-start.3 = (bf16[1,512,256]{2,1,0:T(8,128)(2,1)}, bf16[1,512,256]{2,1,0:T(8,128)(2,1)}, u32[]{:S(2)}, u32[]{:S(2)}) collective-permute-start(bf16[1,512,256]{2,1,0:T(8,128)(2,1)} %get-tuple-element.26), channel_id=1, source_target_pairs={{0,2},{2,0},{4,6},{6,4},{8,10},{10,8},{12,14},{14,12},{16,18},{18,... | collective-permute-start | bytes 786440 | tf_op jit(solution)/shard_map/ppermute | solution.py:23
  54.3 13.6 %collective-permute-start.6 = (bf16[512,256]{1,0:T(8,128)(2,1)S(1)}, bf16[512,256]{1,0:T(8,128)(2,1)S(1)}, u32[]{:S(2)}, u32[]{:S(2)}) collective-permute-start(bf16[512,256]{1,0:T(8,128)(2,1)S(1)} %get-tuple-element.14), channel_id=1, source_target_pairs={{0,2},{2,0},{4,6},{6,4},{8,10},{10,8},{12,14},{14,12},{16,18},{18,... | collective-permute-start | bytes 786440 | tf_op jit(solution)/shard_map/ppermute | solution.py:23
  60.0 7.9 %collective-permute-start.7 = (bf16[512,256]{1,0:T(8,128)(2,1)S(1)}, bf16[512,256]{1,0:T(8,128)(2,1)S(1)}, u32[]{:S(2)}, u32[]{:S(2)}) collective-permute-start(bf16[512,256]{1,0:T(8,128)(2,1)S(1)} %get-tuple-element.15), channel_id=1, source_target_pairs={{0,4},{2,6},{4,0},{6,2},{8,12},{10,14},{12,8},{14,10},{16,20},{18,... | collective-permute-start | bytes 786440 | tf_op jit(solution)/shard_map/ppermute | solution.py:23
  60.3 14.5 %collective-permute-start.8 = (bf16[512,256]{1,0:T(8,128)(2,1)S(1)}, bf16[512,256]{1,0:T(8,128)(2,1)S(1)}, u32[]{:S(2)}, u32[]{:S(2)}) collective-permute-start(bf16[512,256]{1,0:T(8,128)(2,1)S(1)} %get-tuple-element.16), channel_id=1, source_target_pairs={{0,6},{2,4},{4,2},{6,0},{8,14},{10,12},{12,10},{14,8},{16,22},{18,... | collective-permute-start | bytes 786440 | tf_op jit(solution)/shard_map/ppermute | solution.py:23
  74.9 8.0 %collective-permute-start.10 = (bf16[128,256]{1,0:T(8,128)(2,1)S(1)}, bf16[128,256]{1,0:T(8,128)(2,1)S(1)}, u32[]{:S(2)}, u32[]{:S(2)}) collective-permute-start(bf16[128,256]{1,0:T(8,128)(2,1)S(1)} %get-tuple-element.25), channel_id=1, source_target_pairs={{0,16},{2,18},{4,20},{6,22},{8,24},{10,26},{12,28},{14,30},{16,0},... | collective-permute-start | bytes 196616 | tf_op jit(solution)/shard_map/ppermute | solution.py:23
  75.0 7.9 %collective-permute-start.11 = (bf16[128,256]{1,0:T(8,128)(2,1)S(1)}, bf16[128,256]{1,0:T(8,128)(2,1)S(1)}, u32[]{:S(2)}, u32[]{:S(2)}) collective-permute-start(bf16[128,256]{1,0:T(8,128)(2,1)S(1)} %get-tuple-element.24), channel_id=1, source_target_pairs={{0,24},{2,26},{4,28},{6,30},{8,16},{10,18},{12,20},{14,22},{16,8},... | collective-permute-start | bytes 196616 | tf_op jit(solution)/shard_map/ppermute | solution.py:23
  78.7 4.6 %collective-permute-start.9 = (bf16[128,256]{1,0:T(8,128)(2,1)S(1)}, bf16[128,256]{1,0:T(8,128)(2,1)S(1)}, u32[]{:S(2)}, u32[]{:S(2)}) collective-permute-start(bf16[128,256]{1,0:T(8,128)(2,1)S(1)} %get-tuple-element.23), channel_id=1, source_target_pairs={{0,8},{2,10},{4,12},{6,14},{8,0},{10,2},{12,4},{14,6},{16,24},{18,... | collective-permute-start | bytes 196616 | tf_op jit(solution)/shard_map/ppermute | solution.py:23
  83.4 13.3 %collective-permute-start.16 = (bf16[16,64,1024]{2,1,0:T(8,128)(2,1)S(1)}, bf16[16,64,1024]{2,1,0:T(8,128)(2,1)}, u32[]{:S(2)}, u32[]{:S(2)}) collective-permute-start(bf16[16,64,1024]{2,1,0:T(8,128)(2,1)S(1)} %all-to-all-done), channel_id=1, source_target_pairs={{0,1},{1,0},{2,3},{3,2},{4,5},{5,4},{6,7},{7,6},{8,9},{9,8},{10,11... | collective-permute-start | bytes 6291464 | tf_op jit(solution)/shard_map/ppermute | solution.py:245
  83.4 4.5 %collective-permute-start.12 = (bf16[128,256]{1,0:T(8,128)(2,1)S(1)}, bf16[128,256]{1,0:T(8,128)(2,1)S(1)}, u32[]{:S(2)}, u32[]{:S(2)}) collective-permute-start(bf16[128,256]{1,0:T(8,128)(2,1)S(1)} %fusion.3), channel_id=1, source_target_pairs={{0,8},{2,10},{4,12},{6,14},{8,0},{10,2},{12,4},{14,6},{16,24},{18,... | collective-permute-start | bytes 196616 | tf_op jit(solution)/shard_map/ppermute | solution.py:23
  84.7 8.4 %collective-permute-start.13 = (bf16[128,256]{1,0:T(8,128)(2,1)S(1)}, bf16[128,256]{1,0:T(8,128)(2,1)S(1)}, u32[]{:S(2)}, u32[]{:S(2)}) collective-permute-start(bf16[128,256]{1,0:T(8,128)(2,1)S(1)} %fusion.3), channel_id=1, source_target_pairs={{0,16},{2,18},{4,20},{6,22},{8,24},{10,26},{12,28},{14,30},{16,0},... | collective-permute-start | bytes 196616 | tf_op jit(solution)/shard_map/ppermute | solution.py:23
  86.1 7.0 %collective-permute-start.14 = (bf16[128,256]{1,0:T(8,128)(2,1)S(1)}, bf16[128,256]{1,0:T(8,128)(2,1)S(1)}, u32[]{:S(2)}, u32[]{:S(2)}) collective-permute-start(bf16[128,256]{1,0:T(8,128)(2,1)S(1)} %fusion.3), channel_id=1, source_target_pairs={{0,24},{2,26},{4,28},{6,30},{8,16},{10,18},{12,20},{14,22},{16,8},... | collective-permute-start | bytes 196616 | tf_op jit(solution)/shard_map/ppermute | solution.py:23
  93.0 9.3 %collective-permute-start.18 = (bf16[512,256]{1,0:T(8,128)(2,1)S(1)}, bf16[512,256]{1,0:T(8,128)(2,1)S(1)}, u32[]{:S(2)}, u32[]{:S(2)}) collective-permute-start(bf16[512,256]{1,0:T(8,128)(2,1)S(1)} %pad_maximum_fusion.1.grad_ref), channel_id=1, source_target_pairs={{0,2},{2,0},{4,6},{6,4},{8,10},{10,8},{12,14},{14,12},{16,18},{18,... | collective-permute-start | bytes 786440 | tf_op jit(solution)/shard_map/ppermute | solution.py:23
  94.2 13.0 %collective-permute-start.17 = (bf16[512,256]{1,0:T(8,128)(2,1)S(1)}, bf16[512,256]{1,0:T(8,128)(2,1)S(1)}, u32[]{:S(2)}, u32[]{:S(2)}) collective-permute-start(bf16[512,256]{1,0:T(8,128)(2,1)S(1)} %pad_maximum_fusion.1.grad_ref), channel_id=1, source_target_pairs={{0,4},{2,6},{4,0},{6,2},{8,12},{10,14},{12,8},{14,10},{16,20},{18,... | collective-permute-start | bytes 786440 | tf_op jit(solution)/shard_map/ppermute | solution.py:23
  95.0 14.3 %collective-permute-start.15 = (bf16[512,256]{1,0:T(8,128)(2,1)S(1)}, bf16[512,256]{1,0:T(8,128)(2,1)S(1)}, u32[]{:S(2)}, u32[]{:S(2)}) collective-permute-start(bf16[512,256]{1,0:T(8,128)(2,1)S(1)} %pad_maximum_fusion.1.grad_ref), channel_id=1, source_target_pairs={{0,6},{2,4},{4,2},{6,0},{8,14},{10,12},{12,10},{14,8},{16,22},{18,... | collective-permute-start | bytes 786440 | tf_op jit(solution)/shard_map/ppermute | solution.py:23

commit v4 on v3

--- a/solution.py
+++ b/solution.py
@@ -146,47 +146,65 @@
             pltpu.VMEM((head, lanes), jnp.float32),
         ],
         compiler_params=pltpu.CompilerParams(vmem_limit_bytes=48 << 20),
+        cost_estimate=pl.CostEstimate(flops=60000000000, transcendentals=0, bytes_accessed=0),
         name="attention_grads",
     )(me, slots, docs, queries, grad_out, delta, *key_values)
 
 
-def weight_kernel(place, grad_ref, *refs, low, parts, rows, digit, head):
-    column_refs, refs = refs[:parts], refs[parts:]
+def weight_kernel(place, *refs, low, parts, splits, digits, last, head):
+    grad_refs, refs = refs[: len(digits)], refs[len(digits) :]
+    column_refs, refs = refs[: len(digits) * parts * len(splits)], refs[len(digits) * parts * len(splits) :]
     own_high, own_part = place[0] // low, place[1]
     high = column_refs[0].shape[0]
-    tokens = jnp.concatenate([ref[...].reshape(high * rows, ref.shape[-1]) for ref in column_refs], axis=0)
-    starts = [((h ^ own_high) * parts + (part ^ own_part)) * rows for part in range(parts) for h in range(high)]
-    grads = jnp.concatenate([grad_ref[pl.ds(pl.multiple_of(s, rows), rows), :] for s in starts], axis=0)
-    found = dot(grads, tokens, TN)
-    if digit:
+    rows = sum(splits)
+    tokens = jnp.concatenate([ref[...].reshape(-1, ref.shape[-1]) for ref in column_refs], axis=0)
+    grads = []
+    for ref in grad_refs:
+        for part in range(parts):
+            for number, size in enumerate(splits):
+                for h in range(high):
+                    start = ((h ^ own_high) * parts + (part ^ own_part)) * rows + sum(splits[:number])
+                    grads.append(ref[pl.ds(pl.multiple_of(start, 16), size), :])
+    found = dot(jnp.concatenate(grads, axis=0), tokens, TN)
+    if digits[0]:
         found = refs[0][...] + found
-    if digit == low - 1:
+    if last:
         refs[-2][...] = found[:head, :].T
         refs[-1][...] = found[head:, :].T
     else:
         refs[-1][...] = found
 
 
-def weight_step(place, digit, low, columns, grads, sums, head):
-    count, rows, width = columns[0].shape
+def weight_step(place, digits, low, columns, grads, sums, head):
+    count, _, width = columns[0][0].shape
     parts = len(columns)
-    spec = pl.BlockSpec((count // low, 1, rows, width), lambda i, place: (0, (place[0] % low) ^ digit, 0, 0))
-    shapes = ((width, head),) * 2 if digit == low - 1 else ((2 * head, width),)
-    before = [sums] if digit else []
+    splits = [c.shape[1] for c in columns[0]]
+    last = digits[-1] == low - 1
+    columns = [c.reshape(count // low, low, c.shape[1], width) for part in columns for c in part]
+
+    def spec(array, digit):
+        return pl.BlockSpec(
+            (count // low, 1, *array.shape[2:]), lambda i, place: (0, (place[0] % low) ^ digit, 0, 0)
+        )
+
+    shapes = ((width, head),) * 2 if last else ((2 * head, width),)
+    before = [sums] if digits[0] else []
     return pl.pallas_call(
-        functools.partial(weight_kernel, low=low, parts=parts, rows=rows, digit=digit, head=head),
+        functools.partial(
+            weight_kernel, low=low, parts=parts, splits=splits, digits=digits, last=last, head=head
+        ),
         out_shape=tuple(jax.ShapeDtypeStruct(s, jnp.float32) for s in shapes),
         grid_spec=pltpu.PrefetchScalarGridSpec(
             num_scalar_prefetch=1,
             grid=(1,),
-            in_specs=[pl.BlockSpec(grads.shape, lambda i, place: (0, 0))]
-            + [spec] * parts
+            in_specs=[pl.BlockSpec(grads[d].shape, lambda i, place: (0, 0)) for d in digits]
+            + [spec(c, d) for d in digits for c in columns]
             + [pl.BlockSpec((2 * head, width), lambda i, place: (0, 0))] * len(before),
             out_specs=tuple(pl.BlockSpec(s, lambda i, place: (0, 0)) for s in shapes),
         ),
         compiler_params=pltpu.CompilerParams(vmem_limit_bytes=32 << 20),
         name="weight_step",
-    )(place, grads, *(c.reshape(count // low, low, rows, width) for c in columns), *before)
+    )(place, *(grads[d] for d in digits), *(columns * len(digits)), *before)
 
 
 def after(value, *others):
@@ -208,16 +226,15 @@
     column_count = inputs.shape[2] // count
     me = lax.axis_index("context").astype(jnp.int32).reshape(1)
 
-    own = jnp.concatenate([keys, values], axis=2)
+    own = jnp.pad(keys, ((0, 0), (0, 0), (0, head))) + jnp.pad(values, ((0, 0), (0, 0), (head, 0)))
     by_high = [own] + [swap(own, k * low, count) for k in range(1, high)]
     column = jnp.concatenate(by_high, axis=1)
+
+    sent = jnp.moveaxis(inputs.reshape(-1, count, column_count), 1, 0)
+    column, sent = lax.optimization_barrier((column, sent))
+    mine = [lax.all_to_all(sent, "context", split_axis=0, concat_axis=0, tiled=True)]
+
     key_values = [column] + [swap(column, k, count) for k in range(1, low)]
-
-    sent = inputs.reshape(batch_count, token_rows, count, column_count)
-    sent = jnp.moveaxis(sent, 2, 0).reshape(count, batch_count * token_rows, column_count)
-    sent = after(sent, column)
-    mine = lax.all_to_all(sent, "context", split_axis=0, concat_axis=0, tiled=True)
-
     delta = jnp.einsum(
         "bqgd,bqgd->bgq",
         grad_out.reshape(batch_count, row_count, heads, head),
@@ -240,13 +257,16 @@
         own_grads = sum(p.astype(jnp.float32) for p in arrived).astype(jnp.bfloat16)
         column = jnp.concatenate([own_grads] + [swap(own_grads, k * low, count) for k in range(1, high)], axis=0)
         columns = [column] + [swap(column, k, count) for k in range(1, low)]
-        late = after(mine[:, b * token_rows : (b + 1) * token_rows], own_grads)
-        parts = [late] + [
-            lax.ppermute(late, "tensor", [(i, i ^ k) for i in range(tensor_count)]) for k in range(1, tensor_count)
+        held = [
+            after(m.reshape(count, batch_count, -1, column_count)[:, b], w) for m, w in zip(mine, [own_grads])
+        ]
+        held = [held] + [
+            [lax.ppermute(m, "tensor", [(i, i ^ k) for i in range(tensor_count)]) for m in held]
+            for k in range(1, tensor_count)
         ]
         found = [None]
-        for k in range(low):
-            found = weight_step(place, k, low, parts, columns[k], found[0], head)
+        for digits in [[0], [1], list(range(2, low))]:
+            found = weight_step(place, digits, low, held, columns, found[0], head)
         key_sums, value_sums = key_sums + found[0], value_sums + found[1]
     return jnp.stack(query_grads), lax.psum(key_sums, "dp"), lax.psum(value_sums, "dp")
 

time: 112 us -> 104 us (0.929)
  waiting for transfers between devices: 55.5 us -> 43.2 us
  starting transfers between devices: 33.8 us -> 38.6 us
    ppermute x18, waiting for transfers between devices: 55.5 us -> 43.2 us  [swap(): lax.ppermute(value, 'context', [(i, i ^ offset) for i in range(count)])]
    ppermute x18, starting transfers between devices: 28.6 us -> 32.1 us  [swap(): lax.ppermute(value, 'context', [(i, i ^ offset) for i in range(count)])]
    pallas_call x4 -> x3, Pallas kernels: 9.41 us -> 7.77 us  [weight_step(): pl.pallas_call(functools.partial(weight_kernel, low=low, parts=parts, spl...]
    all_to_all x1, starting transfers between devices: 5.17 us -> 6.48 us  [on_device(): lax.all_to_all(sent, 'context', split_axis=0, concat_axis=0, tiled=True)]
    unnamed x11 -> x13, local copies, waits for them, and re-layouts: 2.05 us -> 3.05 us
  transfers between devices with their start and end apart: 20 -> 20, of which waited for: 11 -> 10; matrix products, arithmetic and copies ran while one was open for 5% -> 6% of each run, Pallas kernels for 10% -> 10%
where the time goes in v4:
time: 104 us
  waiting for transfers between devices  43.2 us (42%)
  starting transfers between devices  38.6 us (37%)
  Pallas kernels  14.3 us (14%)
  local copies, waits for them, and re-layouts  5.71 us (5%)
  other arithmetic  1.41 us (1%)
    ppermute x18, waiting for transfers between devices, swap(): lax.ppermute(value, 'context', [(i, i ^ offset) for i in range(count)])  43.2 us
    ppermute x18, starting transfers between devices, swap(): lax.ppermute(value, 'context', [(i, i ^ offset) for i in range(count)])  32.1 us
    pallas_call x3, Pallas kernels, weight_step(): pl.pallas_call(functools.partial(weight_kernel, low=low, parts=parts, spl...  7.77 us
    pallas_call x1, Pallas kernels, attention_grads(): pl.pallas_call(body, out_shape=(jax.ShapeDtypeStruct((rows, width), jnp.b...  6.51 us
    all_to_all x1, starting transfers between devices, on_device(): lax.all_to_all(sent, 'context', split_axis=0, concat_axis=0, tiled=True)  6.48 us
    unnamed x13, local copies, waits for them, and re-layouts  3.05 us
    reshape x1, local copies, waits for them, and re-layouts, on_device(): sent = jnp.moveaxis(inputs.reshape(-1, count, column_count), 1, 0)  2.48 us
  transfers between devices with their start and end apart: 20, of which 10 were waited for; matrix products, arithmetic and copies ran while one was open for 6% of the time, Pallas kernels for 10%

profile of v4, /device:TPU:0, one launch (start us, length us, event | category | flops | bytes accessed | tf_op | source)
XLA Modules:
  0.0 104.1 jit_solution(4115756743014479259)
XLA Ops:
  0.6 0.8 pad_add_fusion
  1.4 3.1 %collective-permute-start = (bf16[1,128,256]{2,1,0:T(8,128)(2,1)S(1)}, bf16[1,128,256]{2,1,0:T(8,128)(2,1)S(1)}, u32[]{:S(2)}, u32[]{:S(2)}) collective-permute-start(bf16[1,128,256]{2,1,0:T(8,128)(2,1)S(1)} %pad_add_fusion), channel_id=1, source_target_pairs={{0,8},{2,10},{4,12},{6,14},{8,0},{10,2},{12,4},{14,6},{16,24},{18,... | collective-permute-start | bytes 196616 | tf_op jit(solution)/shard_map/ppermute | solution.py:23
  4.5 2.6 %collective-permute-start.1 = (bf16[1,128,256]{2,1,0:T(8,128)(2,1)S(1)}, bf16[1,128,256]{2,1,0:T(8,128)(2,1)S(1)}, u32[]{:S(2)}, u32[]{:S(2)}) collective-permute-start(bf16[1,128,256]{2,1,0:T(8,128)(2,1)S(1)} %pad_add_fusion), channel_id=1, source_target_pairs={{0,16},{2,18},{4,20},{6,22},{8,24},{10,26},{12,28},{14,30},{16,0},... | collective-permute-start | bytes 196616 | tf_op jit(solution)/shard_map/ppermute | solution.py:23
  7.1 2.8 %copy.25 = bf16[8,8,16,1024]{3,2,1,0:T(8,128)(2,1)S(1)} copy(bf16[8,8,16,1024]{3,1,2,0:T(8,128)(2,1)} %bitcast.43) | data formatting | bytes 4194304
  9.9 2.5 %copy.27 = bf16[64,16,1024]{2,0,1:T(8,128)(2,1)} copy(bf16[64,16,1024]{2,1,0:T(8,128)(2,1)S(1)} %bitcast.42) | data formatting | bytes 4194304 | tf_op jit(solution)/shard_map/reshape | solution.py:233
  12.4 0.8 collective-permute-done.2
  13.2 1.6 %collective-permute-start.3 = (bf16[1,512,256]{2,1,0:T(8,128)(2,1)S(1)}, bf16[1,512,256]{2,1,0:T(8,128)(2,1)}, u32[]{:S(2)}, u32[]{:S(2)}) collective-permute-start(bf16[1,512,256]{2,1,0:T(8,128)(2,1)S(1)} %pad_maximum_fusion), channel_id=1, source_target_pairs={{0,2},{2,0},{4,6},{6,4},{8,10},{10,8},{12,14},{14,12},{16,18},{18,... | collective-permute-start | bytes 786440 | tf_op jit(solution)/shard_map/ppermute | solution.py:23
  14.7 1.5 %collective-permute-start.4 = (bf16[1,512,256]{2,1,0:T(8,128)(2,1)S(1)}, bf16[1,512,256]{2,1,0:T(8,128)(2,1)}, u32[]{:S(2)}, u32[]{:S(2)}) collective-permute-start(bf16[1,512,256]{2,1,0:T(8,128)(2,1)S(1)} %pad_maximum_fusion), channel_id=1, source_target_pairs={{0,4},{2,6},{4,0},{6,2},{8,12},{10,14},{12,8},{14,10},{16,20},{18,... | collective-permute-start | bytes 786440 | tf_op jit(solution)/shard_map/ppermute | solution.py:23
  16.3 0.5 collective-permute-start.5
  17.5 6.5 %all-to-all-start = ((bf16[16,64,1024]{2,1,0:T(8,128)(2,1)}), bf16[16,64,1024]{2,1,0:T(8,128)(2,1)S(1)}, u32[]{:S(2)}, u32[]{:S(2)}) async-start(bf16[16,64,1024]{2,1,0:T(8,128)(2,1)} %bitcast.41), calls=%async_computation | async-start | bytes 4194304 | tf_op jit(solution)/shard_map/all_to_all | solution.py:235
  24.0 9.1 %collective-permute-done.4 = bf16[1,512,256]{2,1,0:T(8,128)(2,1)} collective-permute-done((bf16[1,512,256]{2,1,0:T(8,128)(2,1)S(1)}, bf16[1,512,256]{2,1,0:T(8,128)(2,1)}, u32[]{:S(2)}, u32[]{:S(2)}) %collective-permute-start.4) | collective-permute-done | bytes 262176 | tf_op jit(solution)/shard_map/ppermute | solution.py:23
  33.1 6.5 %attention_grads.1 = (bf16[128,2048]{1,0:T(8,128)(2,1)}, bf16[512,256]{1,0:T(8,128)(2,1)S(1)}, bf16[512,256]{1,0:T(8,128)(2,1)S(1)}, bf16[512,256]{1,0:T(8,128)(2,1)S(1)}, bf16[512,256]{1,0:T(8,128)(2,1)S(1)}) custom-call(s32[1]{0:T(128)} %bitcast.2.me, s32[32]{0:T(128)S(1)} %copy-done.2, s32[16]{0:T(128)S(1)} %bitcast.40, bf16[128,2048]{1,0:T(8,128)(2,1)S(1)} %bitcast.39, ...), custom_call_target="tpu_custom_call" | custom-call | flops 60000002048 | tf_op jit(solution)/shard_map/attention_grads/pallas_call | solution.py:131
  39.7 4.9 %collective-permute-start.7 = (bf16[512,256]{1,0:T(8,128)(2,1)S(1)}, bf16[512,256]{1,0:T(8,128)(2,1)S(1)}, u32[]{:S(2)}, u32[]{:S(2)}) collective-permute-start(bf16[512,256]{1,0:T(8,128)(2,1)S(1)} %get-tuple-element.17), channel_id=1, source_target_pairs={{0,4},{2,6},{4,0},{6,2},{8,12},{10,14},{12,8},{14,10},{16,20},{18,... | collective-permute-start | bytes 786440 | tf_op jit(solution)/shard_map/ppermute | solution.py:23
  44.6 1.5 %collective-permute-start.8 = (bf16[512,256]{1,0:T(8,128)(2,1)S(1)}, bf16[512,256]{1,0:T(8,128)(2,1)S(1)}, u32[]{:S(2)}, u32[]{:S(2)}) collective-permute-start(bf16[512,256]{1,0:T(8,128)(2,1)S(1)} %get-tuple-element.18), channel_id=1, source_target_pairs={{0,6},{2,4},{4,2},{6,0},{8,14},{10,12},{12,10},{14,8},{16,22},{18,... | collective-permute-start | bytes 786440 | tf_op jit(solution)/shard_map/ppermute | solution.py:23
  46.0 9.2 %collective-permute-done.6 = bf16[512,256]{1,0:T(8,128)(2,1)S(1)} collective-permute-done((bf16[512,256]{1,0:T(8,128)(2,1)S(1)}, bf16[512,256]{1,0:T(8,128)(2,1)S(1)}, u32[]{:S(2)}, u32[]{:S(2)}) %collective-permute-start.6) | collective-permute-done | bytes 262176 | tf_op jit(solution)/shard_map/ppermute | solution.py:23
  55.2 5.1 %collective-permute-done.8 = bf16[512,256]{1,0:T(8,128)(2,1)S(1)} collective-permute-done((bf16[512,256]{1,0:T(8,128)(2,1)S(1)}, bf16[512,256]{1,0:T(8,128)(2,1)S(1)}, u32[]{:S(2)}, u32[]{:S(2)}) %collective-permute-start.8) | collective-permute-done | bytes 262176 | tf_op jit(solution)/shard_map/ppermute | solution.py:23
  60.5 7.4 %collective-permute-start.10 = (bf16[128,256]{1,0:T(8,128)(2,1)S(1)}, bf16[128,256]{1,0:T(8,128)(2,1)S(1)}, u32[]{:S(2)}, u32[]{:S(2)}) collective-permute-start(bf16[128,256]{1,0:T(8,128)(2,1)S(1)} %get-tuple-element.27), channel_id=1, source_target_pairs={{0,16},{2,18},{4,20},{6,22},{8,24},{10,26},{12,28},{14,30},{16,0},... | collective-permute-start | bytes 196616 | tf_op jit(solution)/shard_map/ppermute | solution.py:23
  67.9 0.6 collective-permute-start.9
  68.6 6.8 %collective-permute-done.10 = bf16[128,256]{1,0:T(8,128)(2,1)S(1)} collective-permute-done((bf16[128,256]{1,0:T(8,128)(2,1)S(1)}, bf16[128,256]{1,0:T(8,128)(2,1)S(1)}, u32[]{:S(2)}, u32[]{:S(2)}) %collective-permute-start.10) | collective-permute-done | bytes 65568 | tf_op jit(solution)/shard_map/ppermute | solution.py:23
  75.5 1.3 %collective-permute-start.12 = (bf16[128,256]{1,0:T(8,128)(2,1)S(1)}, bf16[128,256]{1,0:T(8,128)(2,1)S(1)}, u32[]{:S(2)}, u32[]{:S(2)}) collective-permute-start(bf16[128,256]{1,0:T(8,128)(2,1)S(1)} %fusion.3), channel_id=1, source_target_pairs={{0,8},{2,10},{4,12},{6,14},{8,0},{10,2},{12,4},{14,6},{16,24},{18,... | collective-permute-start | bytes 196616 | tf_op jit(solution)/shard_map/ppermute | solution.py:23
  76.9 1.7 %collective-permute-start.13 = (bf16[128,256]{1,0:T(8,128)(2,1)S(1)}, bf16[128,256]{1,0:T(8,128)(2,1)S(1)}, u32[]{:S(2)}, u32[]{:S(2)}) collective-permute-start(bf16[128,256]{1,0:T(8,128)(2,1)S(1)} %fusion.3), channel_id=1, source_target_pairs={{0,16},{2,18},{4,20},{6,22},{8,24},{10,26},{12,28},{14,30},{16,0},... | collective-permute-start | bytes 196616 | tf_op jit(solution)/shard_map/ppermute | solution.py:23
  78.6 1.4 %collective-permute-start.14 = (bf16[128,256]{1,0:T(8,128)(2,1)S(1)}, bf16[128,256]{1,0:T(8,128)(2,1)S(1)}, u32[]{:S(2)}, u32[]{:S(2)}) collective-permute-start(bf16[128,256]{1,0:T(8,128)(2,1)S(1)} %fusion.3), channel_id=1, source_target_pairs={{0,24},{2,26},{4,28},{6,30},{8,16},{10,18},{12,20},{14,22},{16,8},... | collective-permute-start | bytes 196616 | tf_op jit(solution)/shard_map/ppermute | solution.py:23
  80.1 5.1 %collective-permute-done.13 = bf16[128,256]{1,0:T(8,128)(2,1)S(1)} collective-permute-done((bf16[128,256]{1,0:T(8,128)(2,1)S(1)}, bf16[128,256]{1,0:T(8,128)(2,1)S(1)}, u32[]{:S(2)}, u32[]{:S(2)}) %collective-permute-start.13) | collective-permute-done | bytes 65568 | tf_op jit(solution)/shard_map/ppermute | solution.py:23
  85.2 1.5 %collective-permute-start.18 = (bf16[512,256]{1,0:T(8,128)(2,1)S(1)}, bf16[512,256]{1,0:T(8,128)(2,1)S(1)}, u32[]{:S(2)}, u32[]{:S(2)}) collective-permute-start(bf16[512,256]{1,0:T(8,128)(2,1)S(1)} %pad_maximum_fusion.1.refs_0_), channel_id=1, source_target_pairs={{0,2},{2,0},{4,6},{6,4},{8,10},{10,8},{12,14},{14,12},{16,18},{18,... | collective-permute-start | bytes 786440 | tf_op jit(solution)/shard_map/ppermute | solution.py:23
  86.7 1.9 %collective-permute-start.15 = (bf16[512,256]{1,0:T(8,128)(2,1)S(1)}, bf16[512,256]{1,0:T(8,128)(2,1)S(1)}, u32[]{:S(2)}, u32[]{:S(2)}) collective-permute-start(bf16[512,256]{1,0:T(8,128)(2,1)S(1)} %pad_maximum_fusion.1.refs_0_), channel_id=1, source_target_pairs={{0,4},{2,6},{4,0},{6,2},{8,12},{10,14},{12,8},{14,10},{16,20},{18,... | collective-permute-start | bytes 786440 | tf_op jit(solution)/shard_map/ppermute | solution.py:23
  88.6 0.6 collective-permute-start.16
  89.2 2.1 %weight_step.3.refs_3_ = f32[256,1024]{1,0:T(8,128)S(1)} custom-call(s32[2]{0:T(128)S(1)} %pad_add_fusion.1.place, bf16[512,256]{1,0:T(8,128)(2,1)S(1)} %pad_maximum_fusion.1.refs_0_, bf16[4,4,64,1024]{3,2,1,0:T(8,128)(2,1)S(1)} %bitcast.32, bf16[4,4,64,1024]{3,2,1,0:T(8,128)(2,1)} %bitcast.16.refs_2_.refs_3_.refs_5_), custom_call_target="tpu_custom_call" | custom-call | tf_op jit(solution)/shard_map/weight_step/pallas_call | solution.py:192
  91.3 3.2 %collective-permute-done.18.refs_0_ = bf16[512,256]{1,0:T(8,128)(2,1)S(1)} collective-permute-done((bf16[512,256]{1,0:T(8,128)(2,1)S(1)}, bf16[512,256]{1,0:T(8,128)(2,1)S(1)}, u32[]{:S(2)}, u32[]{:S(2)}) %collective-permute-start.18) | collective-permute-done | bytes 262176 | tf_op jit(solution)/shard_map/ppermute | solution.py:23
  94.5 2.1 %weight_step.4.refs_6_ = f32[256,1024]{1,0:T(8,128)S(1)} custom-call(s32[2]{0:T(128)S(1)} %pad_add_fusion.1.place, bf16[512,256]{1,0:T(8,128)(2,1)S(1)} %collective-permute-done.18.refs_0_, bf16[4,4,64,1024]{3,2,1,0:T(8,128)(2,1)S(1)} %bitcast.33, bf16[4,4,64,1024]{3,2,1,0:T(8,128)(2,1)} %bitcast.16.refs_2_.refs_3_.refs_5_, f32[256,1024]{1,0:T(8,128)S(1)} %weight_step.3.refs_3_), custom_call_target="tpu_custom_call" | custom-call | tf_op jit(solution)/shard_map/weight_step/pallas_call | solution.py:192
  96.6 2.6 %collective-permute-done.15.refs_0_ = bf16[512,256]{1,0:T(8,128)(2,1)S(1)} collective-permute-done((bf16[512,256]{1,0:T(8,128)(2,1)S(1)}, bf16[512,256]{1,0:T(8,128)(2,1)S(1)}, u32[]{:S(2)}, u32[]{:S(2)}) %collective-permute-start.15) | collective-permute-done | bytes 262176 | tf_op jit(solution)/shard_map/ppermute | solution.py:23
  99.2 1.3 %collective-permute-done.16.refs_1_ = bf16[512,256]{1,0:T(8,128)(2,1)S(1)} collective-permute-done((bf16[512,256]{1,0:T(8,128)(2,1)S(1)}, bf16[512,256]{1,0:T(8,128)(2,1)S(1)}, u32[]{:S(2)}, u32[]{:S(2)}) %collective-permute-start.16) | collective-permute-done | bytes 262176 | tf_op jit(solution)/shard_map/ppermute | solution.py:23
  100.5 3.6 %weight_step.5 = (f32[1024,128]{1,0:T(8,128)}, f32[1024,128]{1,0:T(8,128)}) custom-call(s32[2]{0:T(128)S(1)} %pad_add_fusion.1.place, bf16[512,256]{1,0:T(8,128)(2,1)S(1)} %collective-permute-done.15.refs_0_, bf16[512,256]{1,0:T(8,128)(2,1)S(1)} %collective-permute-done.16.refs_1_, bf16[4,4,64,1024]{3,2,1,0:T(8,128)(2,1)S(1)} %bitcast.34, ...), custom_call_target="tpu_custom_call" | custom-call | tf_op jit(solution)/shard_map/weight_step/pallas_call | solution.py:192
  (37 shorter events, 1.2 us)
Async XLA Ops:
  1.4 11.0 %collective-permute-start = (bf16[1,128,256]{2,1,0:T(8,128)(2,1)S(1)}, bf16[1,128,256]{2,1,0:T(8,128)(2,1)S(1)}, u32[]{:S(2)}, u32[]{:S(2)}) collective-permute-start(bf16[1,128,256]{2,1,0:T(8,128)(2,1)S(1)} %pad_add_fusion), channel_id=1, source_target_pairs={{0,8},{2,10},{4,12},{6,14},{8,0},{10,2},{12,4},{14,6},{16,24},{18,... | collective-permute-start | bytes 196616 | tf_op jit(solution)/shard_map/ppermute | solution.py:23
  4.5 7.9 %collective-permute-start.1 = (bf16[1,128,256]{2,1,0:T(8,128)(2,1)S(1)}, bf16[1,128,256]{2,1,0:T(8,128)(2,1)S(1)}, u32[]{:S(2)}, u32[]{:S(2)}) collective-permute-start(bf16[1,128,256]{2,1,0:T(8,128)(2,1)S(1)} %pad_add_fusion), channel_id=1, source_target_pairs={{0,16},{2,18},{4,20},{6,22},{8,24},{10,26},{12,28},{14,30},{16,0},... | collective-permute-start | bytes 196616 | tf_op jit(solution)/shard_map/ppermute | solution.py:23
  7.1 6.1 %collective-permute-start.2 = (bf16[1,128,256]{2,1,0:T(8,128)(2,1)S(1)}, bf16[1,128,256]{2,1,0:T(8,128)(2,1)S(1)}, u32[]{:S(2)}, u32[]{:S(2)}) collective-permute-start(bf16[1,128,256]{2,1,0:T(8,128)(2,1)S(1)} %pad_add_fusion), channel_id=1, source_target_pairs={{0,24},{2,26},{4,28},{6,30},{8,16},{10,18},{12,20},{14,22},{16,8},... | collective-permute-start | bytes 196616 | tf_op jit(solution)/shard_map/ppermute | solution.py:23
  9.9 6.9 %copy-start = (bf16[1,128,2048]{2,1,0:T(8,128)(2,1)S(1)}, bf16[1,128,2048]{2,1,0:T(8,128)(2,1)}, u32[]{:S(2)}) copy-start(bf16[1,128,2048]{2,1,0:T(8,128)(2,1)} %param.12) | copy-start | bytes 1572868
  9.9 7.0 %copy-start.4 = (bf16[1,128,2048]{2,1,0:T(8,128)(2,1)S(1)}, bf16[1,128,2048]{2,1,0:T(8,128)(2,1)}, u32[]{:S(2)}) copy-start(bf16[1,128,2048]{2,1,0:T(8,128)(2,1)} %param.11) | copy-start | bytes 1572868
  13.2 10.8 %collective-permute-start.3 = (bf16[1,512,256]{2,1,0:T(8,128)(2,1)S(1)}, bf16[1,512,256]{2,1,0:T(8,128)(2,1)}, u32[]{:S(2)}, u32[]{:S(2)}) collective-permute-start(bf16[1,512,256]{2,1,0:T(8,128)(2,1)S(1)} %pad_maximum_fusion), channel_id=1, source_target_pairs={{0,2},{2,0},{4,6},{6,4},{8,10},{10,8},{12,14},{14,12},{16,18},{18,... | collective-permute-start | bytes 786440 | tf_op jit(solution)/shard_map/ppermute | solution.py:23
  14.7 18.4 %collective-permute-start.4 = (bf16[1,512,256]{2,1,0:T(8,128)(2,1)S(1)}, bf16[1,512,256]{2,1,0:T(8,128)(2,1)}, u32[]{:S(2)}, u32[]{:S(2)}) collective-permute-start(bf16[1,512,256]{2,1,0:T(8,128)(2,1)S(1)} %pad_maximum_fusion), channel_id=1, source_target_pairs={{0,4},{2,6},{4,0},{6,2},{8,12},{10,14},{12,8},{14,10},{16,20},{18,... | collective-permute-start | bytes 786440 | tf_op jit(solution)/shard_map/ppermute | solution.py:23
  16.3 16.9 %collective-permute-start.5 = (bf16[1,512,256]{2,1,0:T(8,128)(2,1)S(1)}, bf16[1,512,256]{2,1,0:T(8,128)(2,1)}, u32[]{:S(2)}, u32[]{:S(2)}) collective-permute-start(bf16[1,512,256]{2,1,0:T(8,128)(2,1)S(1)} %pad_maximum_fusion), channel_id=1, source_target_pairs={{0,6},{2,4},{4,2},{6,0},{8,14},{10,12},{12,10},{14,8},{16,22},{18,... | collective-permute-start | bytes 786440 | tf_op jit(solution)/shard_map/ppermute | solution.py:23
  17.5 15.6 %copy-start.1 = (bf16[1,128,2048]{2,1,0:T(8,128)(2,1)S(1)}, bf16[1,128,2048]{2,1,0:T(8,128)(2,1)}, u32[]{:S(2)}) copy-start(bf16[1,128,2048]{2,1,0:T(8,128)(2,1)} %param.8) | copy-start | bytes 1572868
  17.5 15.6 %copy-start.2 = (s32[32]{0:T(128)S(1)}, s32[32]{0:T(128)}, u32[]{:S(2)}) copy-start(s32[32]{0:T(128)} %slots.1) | copy-start | bytes 388
  17.5 15.6 %copy-start.3 = (s32[1,16]{1,0:T(1,128)S(1)}, s32[1,16]{1,0:T(1,128)}, u32[]{:S(2)}) copy-start(s32[1,16]{1,0:T(1,128)} %param.14) | copy-start | bytes 196
  17.5 57.9 %all-to-all-start = ((bf16[16,64,1024]{2,1,0:T(8,128)(2,1)}), bf16[16,64,1024]{2,1,0:T(8,128)(2,1)S(1)}, u32[]{:S(2)}, u32[]{:S(2)}) async-start(bf16[16,64,1024]{2,1,0:T(8,128)(2,1)} %bitcast.41), calls=%async_computation | async-start | bytes 4194304 | tf_op jit(solution)/shard_map/all_to_all | solution.py:235
  39.7 15.6 %collective-permute-start.6 = (bf16[512,256]{1,0:T(8,128)(2,1)S(1)}, bf16[512,256]{1,0:T(8,128)(2,1)S(1)}, u32[]{:S(2)}, u32[]{:S(2)}) collective-permute-start(bf16[512,256]{1,0:T(8,128)(2,1)S(1)} %get-tuple-element.16), channel_id=1, source_target_pairs={{0,2},{2,0},{4,6},{6,4},{8,10},{10,8},{12,14},{14,12},{16,18},{18,... | collective-permute-start | bytes 786440 | tf_op jit(solution)/shard_map/ppermute | solution.py:23
  39.7 15.6 %collective-permute-start.7 = (bf16[512,256]{1,0:T(8,128)(2,1)S(1)}, bf16[512,256]{1,0:T(8,128)(2,1)S(1)}, u32[]{:S(2)}, u32[]{:S(2)}) collective-permute-start(bf16[512,256]{1,0:T(8,128)(2,1)S(1)} %get-tuple-element.17), channel_id=1, source_target_pairs={{0,4},{2,6},{4,0},{6,2},{8,12},{10,14},{12,8},{14,10},{16,20},{18,... | collective-permute-start | bytes 786440 | tf_op jit(solution)/shard_map/ppermute | solution.py:23
  44.6 15.8 %collective-permute-start.8 = (bf16[512,256]{1,0:T(8,128)(2,1)S(1)}, bf16[512,256]{1,0:T(8,128)(2,1)S(1)}, u32[]{:S(2)}, u32[]{:S(2)}) collective-permute-start(bf16[512,256]{1,0:T(8,128)(2,1)S(1)} %get-tuple-element.18), channel_id=1, source_target_pairs={{0,6},{2,4},{4,2},{6,0},{8,14},{10,12},{12,10},{14,8},{16,22},{18,... | collective-permute-start | bytes 786440 | tf_op jit(solution)/shard_map/ppermute | solution.py:23
  60.5 14.9 %collective-permute-start.10 = (bf16[128,256]{1,0:T(8,128)(2,1)S(1)}, bf16[128,256]{1,0:T(8,128)(2,1)S(1)}, u32[]{:S(2)}, u32[]{:S(2)}) collective-permute-start(bf16[128,256]{1,0:T(8,128)(2,1)S(1)} %get-tuple-element.27), channel_id=1, source_target_pairs={{0,16},{2,18},{4,20},{6,22},{8,24},{10,26},{12,28},{14,30},{16,0},... | collective-permute-start | bytes 196616 | tf_op jit(solution)/shard_map/ppermute | solution.py:23
  67.9 7.5 %collective-permute-start.11 = (bf16[128,256]{1,0:T(8,128)(2,1)S(1)}, bf16[128,256]{1,0:T(8,128)(2,1)S(1)}, u32[]{:S(2)}, u32[]{:S(2)}) collective-permute-start(bf16[128,256]{1,0:T(8,128)(2,1)S(1)} %get-tuple-element.26), channel_id=1, source_target_pairs={{0,24},{2,26},{4,28},{6,30},{8,16},{10,18},{12,20},{14,22},{16,8},... | collective-permute-start | bytes 196616 | tf_op jit(solution)/shard_map/ppermute | solution.py:23
  67.9 7.5 %collective-permute-start.9 = (bf16[128,256]{1,0:T(8,128)(2,1)S(1)}, bf16[128,256]{1,0:T(8,128)(2,1)S(1)}, u32[]{:S(2)}, u32[]{:S(2)}) collective-permute-start(bf16[128,256]{1,0:T(8,128)(2,1)S(1)} %get-tuple-element.25), channel_id=1, source_target_pairs={{0,8},{2,10},{4,12},{6,14},{8,0},{10,2},{12,4},{14,6},{16,24},{18,... | collective-permute-start | bytes 196616 | tf_op jit(solution)/shard_map/ppermute | solution.py:23
  75.5 13.8 %collective-permute-start.17 = (bf16[16,64,1024]{2,1,0:T(8,128)(2,1)S(1)}, bf16[16,64,1024]{2,1,0:T(8,128)(2,1)}, u32[]{:S(2)}, u32[]{:S(2)}) collective-permute-start(bf16[16,64,1024]{2,1,0:T(8,128)(2,1)S(1)} %all-to-all-done), channel_id=1, source_target_pairs={{0,1},{1,0},{2,3},{3,2},{4,5},{5,4},{6,7},{7,6},{8,9},{9,8},{10,11... | collective-permute-start | bytes 6291464 | tf_op jit(solution)/shard_map/ppermute | solution.py:264
  75.5 4.5 %collective-permute-start.12 = (bf16[128,256]{1,0:T(8,128)(2,1)S(1)}, bf16[128,256]{1,0:T(8,128)(2,1)S(1)}, u32[]{:S(2)}, u32[]{:S(2)}) collective-permute-start(bf16[128,256]{1,0:T(8,128)(2,1)S(1)} %fusion.3), channel_id=1, source_target_pairs={{0,8},{2,10},{4,12},{6,14},{8,0},{10,2},{12,4},{14,6},{16,24},{18,... | collective-permute-start | bytes 196616 | tf_op jit(solution)/shard_map/ppermute | solution.py:23
  76.9 8.3 %collective-permute-start.13 = (bf16[128,256]{1,0:T(8,128)(2,1)S(1)}, bf16[128,256]{1,0:T(8,128)(2,1)S(1)}, u32[]{:S(2)}, u32[]{:S(2)}) collective-permute-start(bf16[128,256]{1,0:T(8,128)(2,1)S(1)} %fusion.3), channel_id=1, source_target_pairs={{0,16},{2,18},{4,20},{6,22},{8,24},{10,26},{12,28},{14,30},{16,0},... | collective-permute-start | bytes 196616 | tf_op jit(solution)/shard_map/ppermute | solution.py:23
  78.6 6.6 %collective-permute-start.14 = (bf16[128,256]{1,0:T(8,128)(2,1)S(1)}, bf16[128,256]{1,0:T(8,128)(2,1)S(1)}, u32[]{:S(2)}, u32[]{:S(2)}) collective-permute-start(bf16[128,256]{1,0:T(8,128)(2,1)S(1)} %fusion.3), channel_id=1, source_target_pairs={{0,24},{2,26},{4,28},{6,30},{8,16},{10,18},{12,20},{14,22},{16,8},... | collective-permute-start | bytes 196616 | tf_op jit(solution)/shard_map/ppermute | solution.py:23
  85.2 9.3 %collective-permute-start.18 = (bf16[512,256]{1,0:T(8,128)(2,1)S(1)}, bf16[512,256]{1,0:T(8,128)(2,1)S(1)}, u32[]{:S(2)}, u32[]{:S(2)}) collective-permute-start(bf16[512,256]{1,0:T(8,128)(2,1)S(1)} %pad_maximum_fusion.1.refs_0_), channel_id=1, source_target_pairs={{0,2},{2,0},{4,6},{6,4},{8,10},{10,8},{12,14},{14,12},{16,18},{18,... | collective-permute-start | bytes 786440 | tf_op jit(solution)/shard_map/ppermute | solution.py:23
  86.7 12.5 %collective-permute-start.15 = (bf16[512,256]{1,0:T(8,128)(2,1)S(1)}, bf16[512,256]{1,0:T(8,128)(2,1)S(1)}, u32[]{:S(2)}, u32[]{:S(2)}) collective-permute-start(bf16[512,256]{1,0:T(8,128)(2,1)S(1)} %pad_maximum_fusion.1.refs_0_), channel_id=1, source_target_pairs={{0,4},{2,6},{4,0},{6,2},{8,12},{10,14},{12,8},{14,10},{16,20},{18,... | collective-permute-start | bytes 786440 | tf_op jit(solution)/shard_map/ppermute | solution.py:23
  88.6 11.9 %collective-permute-start.16 = (bf16[512,256]{1,0:T(8,128)(2,1)S(1)}, bf16[512,256]{1,0:T(8,128)(2,1)S(1)}, u32[]{:S(2)}, u32[]{:S(2)}) collective-permute-start(bf16[512,256]{1,0:T(8,128)(2,1)S(1)} %pad_maximum_fusion.1.refs_0_), channel_id=1, source_target_pairs={{0,6},{2,4},{4,2},{6,0},{8,14},{10,12},{12,10},{14,8},{16,22},{18,... | collective-permute-start | bytes 786440 | tf_op jit(solution)/shard_map/ppermute | solution.py:23

commit v5 on v4

--- a/solution.py
+++ b/solution.py
@@ -121,7 +121,7 @@
     total = low * key_values[0].shape[0]
     heads = width // head
     span_rows = rows // 2
-    chunk = min(256, total)
+    chunk = min(128, total)
     vmem = pl.BlockSpec(memory_space=pltpu.VMEM)
     smem = pl.BlockSpec(memory_space=pltpu.SMEM)
     lanes = heads * span_rows
@@ -151,22 +151,20 @@
     )(me, slots, docs, queries, grad_out, delta, *key_values)
 
 
-def weight_kernel(place, *refs, low, parts, splits, digits, last, head):
+def weight_kernel(place, *refs, low, parts, digits, more, last, head):
     grad_refs, refs = refs[: len(digits)], refs[len(digits) :]
-    column_refs, refs = refs[: len(digits) * parts * len(splits)], refs[len(digits) * parts * len(splits) :]
-    own_high, own_part = place[0] // low, place[1]
-    high = column_refs[0].shape[0]
-    rows = sum(splits)
-    tokens = jnp.concatenate([ref[...].reshape(-1, ref.shape[-1]) for ref in column_refs], axis=0)
-    grads = []
-    for ref in grad_refs:
-        for part in range(parts):
-            for number, size in enumerate(splits):
-                for h in range(high):
-                    start = ((h ^ own_high) * parts + (part ^ own_part)) * rows + sum(splits[:number])
-                    grads.append(ref[pl.ds(pl.multiple_of(start, 16), size), :])
-    found = dot(jnp.concatenate(grads, axis=0), tokens, TN)
-    if digits[0]:
+    column_refs, refs = refs[:parts], refs[parts:]
+    own_high, own_low, own_part = place[0] // low, place[0] % low, place[1]
+    high, _, rows, width = column_refs[0].shape
+    tokens, grads = [], []
+    for digit, grad_ref in zip(digits, grad_refs):
+        for part, ref in enumerate(column_refs):
+            for h in range(high):
+                tokens.append(ref[h, own_low ^ digit])
+                start = ((h ^ own_high) * parts + (part ^ own_part)) * rows
+                grads.append(grad_ref[pl.ds(pl.multiple_of(start, rows), rows), :])
+    found = dot(jnp.concatenate(grads, axis=0), jnp.concatenate(tokens, axis=0), TN)
+    if more:
         found = refs[0][...] + found
     if last:
         refs[-2][...] = found[:head, :].T
@@ -176,35 +174,23 @@
 
 
 def weight_step(place, digits, low, columns, grads, sums, head):
-    count, _, width = columns[0][0].shape
+    count, rows, width = columns[0].shape
     parts = len(columns)
-    splits = [c.shape[1] for c in columns[0]]
     last = digits[-1] == low - 1
-    columns = [c.reshape(count // low, low, c.shape[1], width) for part in columns for c in part]
-
-    def spec(array, digit):
-        return pl.BlockSpec(
-            (count // low, 1, *array.shape[2:]), lambda i, place: (0, (place[0] % low) ^ digit, 0, 0)
-        )
-
+    columns = [c.reshape(count // low, low, rows, width) for c in columns]
     shapes = ((width, head),) * 2 if last else ((2 * head, width),)
-    before = [sums] if digits[0] else []
+    operands = [grads[d] for d in digits] + columns + ([] if sums is None else [sums])
+    vmem = pl.BlockSpec(memory_space=pltpu.VMEM)
     return pl.pallas_call(
         functools.partial(
-            weight_kernel, low=low, parts=parts, splits=splits, digits=digits, last=last, head=head
+            weight_kernel, low=low, parts=parts, digits=digits, more=sums is not None, last=last, head=head
         ),
         out_shape=tuple(jax.ShapeDtypeStruct(s, jnp.float32) for s in shapes),
-        grid_spec=pltpu.PrefetchScalarGridSpec(
-            num_scalar_prefetch=1,
-            grid=(1,),
-            in_specs=[pl.BlockSpec(grads[d].shape, lambda i, place: (0, 0)) for d in digits]
-            + [spec(c, d) for d in digits for c in columns]
-            + [pl.BlockSpec((2 * head, width), lambda i, place: (0, 0))] * len(before),
-            out_specs=tuple(pl.BlockSpec(s, lambda i, place: (0, 0)) for s in shapes),
-        ),
-        compiler_params=pltpu.CompilerParams(vmem_limit_bytes=32 << 20),
+        in_specs=[pl.BlockSpec(memory_space=pltpu.SMEM)] + [vmem] * len(operands),
+        out_specs=(vmem,) * len(shapes),
+        compiler_params=pltpu.CompilerParams(vmem_limit_bytes=24 << 20),
         name="weight_step",
-    )(place, *(grads[d] for d in digits), *(columns * len(digits)), *before)
+    )(place, *operands)
 
 
 def after(value, *others):
@@ -232,7 +218,7 @@
 
     sent = jnp.moveaxis(inputs.reshape(-1, count, column_count), 1, 0)
     column, sent = lax.optimization_barrier((column, sent))
-    mine = [lax.all_to_all(sent, "context", split_axis=0, concat_axis=0, tiled=True)]
+    mine = lax.all_to_all(sent, "context", split_axis=0, concat_axis=0, tiled=True)
 
     key_values = [column] + [swap(column, k, count) for k in range(1, low)]
     delta = jnp.einsum(
@@ -257,12 +243,9 @@
         own_grads = sum(p.astype(jnp.float32) for p in arrived).astype(jnp.bfloat16)
         column = jnp.concatenate([own_grads] + [swap(own_grads, k * low, count) for k in range(1, high)], axis=0)
         columns = [column] + [swap(column, k, count) for k in range(1, low)]
-        held = [
-            after(m.reshape(count, batch_count, -1, column_count)[:, b], w) for m, w in zip(mine, [own_grads])
-        ]
+        held = after(mine.reshape(count, batch_count, -1, column_count)[:, b], own_grads)
         held = [held] + [
-            [lax.ppermute(m, "tensor", [(i, i ^ k) for i in range(tensor_count)]) for m in held]
-            for k in range(1, tensor_count)
+            lax.ppermute(held, "tensor", [(i, i ^ k) for i in range(tensor_count)]) for k in range(1, tensor_count)
         ]
         found = [None]
         for digits in [[0], [1], list(range(2, low))]:

time: 104 us -> 104 us (level)
  starting transfers between devices: 38.6 us -> 35.4 us
  waiting for transfers between devices: 43.2 us -> 46.1 us
    ppermute x18, starting transfers between devices: 32.1 us -> 28.8 us  [swap(): lax.ppermute(value, 'context', [(i, i ^ offset) for i in range(count)])]
    ppermute x18, waiting for transfers between devices: 43.2 us -> 46.1 us  [swap(): lax.ppermute(value, 'context', [(i, i ^ offset) for i in range(count)])]
  transfers between devices with their start and end apart: 20 -> 20, of which waited for: 10 -> 12; matrix products, arithmetic and copies ran while one was open for 6% -> 6% of each run, Pallas kernels for 10% -> 11%
where the time goes in v5:
time: 104 us
  waiting for transfers between devices  46.1 us (44%)
  starting transfers between devices  35.4 us (34%)
  Pallas kernels  14.8 us (14%)
  local copies, waits for them, and re-layouts  5.71 us (5%)
  other arithmetic  1.41 us (1%)
    ppermute x18, waiting for transfers between devices, swap(): lax.ppermute(value, 'context', [(i, i ^ offset) for i in range(count)])  46.1 us
    ppermute x18, starting transfers between devices, swap(): lax.ppermute(value, 'context', [(i, i ^ offset) for i in range(count)])  28.8 us
    pallas_call x3, Pallas kernels, weight_step(): pl.pallas_call(functools.partial(weight_kernel, low=low, parts=parts, dig...  7.53 us
    pallas_call x1, Pallas kernels, attention_grads(): pl.pallas_call(body, out_shape=(jax.ShapeDtypeStruct((rows, width), jnp.b...  7.28 us
    all_to_all x1, starting transfers between devices, on_device(): lax.all_to_all(sent, 'context', split_axis=0, concat_axis=0, tiled=True)  6.48 us
    unnamed x13, local copies, waits for them, and re-layouts  3.05 us
    reshape x1, local copies, waits for them, and re-layouts, on_device(): sent = jnp.moveaxis(inputs.reshape(-1, count, column_count), 1, 0)  2.48 us
  transfers between devices with their start and end apart: 20, of which 12 were waited for; matrix products, arithmetic and copies ran while one was open for 6% of the time, Pallas kernels for 11%

profile of v5, /device:TPU:0, one launch (start us, length us, event | category | flops | bytes accessed | tf_op | source)
XLA Modules:
  0.0 104.3 jit_solution(2343973494304060143)
XLA Ops:
  0.6 0.8 pad_add_fusion
  1.4 3.1 %collective-permute-start = (bf16[1,128,256]{2,1,0:T(8,128)(2,1)S(1)}, bf16[1,128,256]{2,1,0:T(8,128)(2,1)S(1)}, u32[]{:S(2)}, u32[]{:S(2)}) collective-permute-start(bf16[1,128,256]{2,1,0:T(8,128)(2,1)S(1)} %pad_add_fusion), channel_id=1, source_target_pairs={{0,8},{2,10},{4,12},{6,14},{8,0},{10,2},{12,4},{14,6},{16,24},{18,... | collective-permute-start | bytes 196616 | tf_op jit(solution)/shard_map/ppermute | solution.py:23
  4.5 2.6 %collective-permute-start.1 = (bf16[1,128,256]{2,1,0:T(8,128)(2,1)S(1)}, bf16[1,128,256]{2,1,0:T(8,128)(2,1)S(1)}, u32[]{:S(2)}, u32[]{:S(2)}) collective-permute-start(bf16[1,128,256]{2,1,0:T(8,128)(2,1)S(1)} %pad_add_fusion), channel_id=1, source_target_pairs={{0,16},{2,18},{4,20},{6,22},{8,24},{10,26},{12,28},{14,30},{16,0},... | collective-permute-start | bytes 196616 | tf_op jit(solution)/shard_map/ppermute | solution.py:23
  7.1 2.8 %copy.25 = bf16[8,8,16,1024]{3,2,1,0:T(8,128)(2,1)S(1)} copy(bf16[8,8,16,1024]{3,1,2,0:T(8,128)(2,1)} %bitcast.42) | data formatting | bytes 4194304
  9.9 2.5 %copy.27 = bf16[64,16,1024]{2,0,1:T(8,128)(2,1)} copy(bf16[64,16,1024]{2,1,0:T(8,128)(2,1)S(1)} %bitcast.41) | data formatting | bytes 4194304 | tf_op jit(solution)/shard_map/reshape | solution.py:219
  12.4 0.8 collective-permute-done.2
  13.2 1.6 %collective-permute-start.3 = (bf16[1,512,256]{2,1,0:T(8,128)(2,1)S(1)}, bf16[1,512,256]{2,1,0:T(8,128)(2,1)}, u32[]{:S(2)}, u32[]{:S(2)}) collective-permute-start(bf16[1,512,256]{2,1,0:T(8,128)(2,1)S(1)} %pad_maximum_fusion), channel_id=1, source_target_pairs={{0,2},{2,0},{4,6},{6,4},{8,10},{10,8},{12,14},{14,12},{16,18},{18,... | collective-permute-start | bytes 786440 | tf_op jit(solution)/shard_map/ppermute | solution.py:23
  14.7 1.5 %collective-permute-start.4 = (bf16[1,512,256]{2,1,0:T(8,128)(2,1)S(1)}, bf16[1,512,256]{2,1,0:T(8,128)(2,1)}, u32[]{:S(2)}, u32[]{:S(2)}) collective-permute-start(bf16[1,512,256]{2,1,0:T(8,128)(2,1)S(1)} %pad_maximum_fusion), channel_id=1, source_target_pairs={{0,4},{2,6},{4,0},{6,2},{8,12},{10,14},{12,8},{14,10},{16,20},{18,... | collective-permute-start | bytes 786440 | tf_op jit(solution)/shard_map/ppermute | solution.py:23
  17.5 6.5 %all-to-all-start = ((bf16[16,64,1024]{2,1,0:T(8,128)(2,1)}), bf16[16,64,1024]{2,1,0:T(8,128)(2,1)S(1)}, u32[]{:S(2)}, u32[]{:S(2)}) async-start(bf16[16,64,1024]{2,1,0:T(8,128)(2,1)} %bitcast.40), calls=%async_computation | async-start | bytes 4194304 | tf_op jit(solution)/shard_map/all_to_all | solution.py:221
  24.0 9.1 %collective-permute-done.4 = bf16[1,512,256]{2,1,0:T(8,128)(2,1)} collective-permute-done((bf16[1,512,256]{2,1,0:T(8,128)(2,1)S(1)}, bf16[1,512,256]{2,1,0:T(8,128)(2,1)}, u32[]{:S(2)}, u32[]{:S(2)}) %collective-permute-start.4) | collective-permute-done | bytes 262176 | tf_op jit(solution)/shard_map/ppermute | solution.py:23
  33.1 7.3 %attention_grads.1 = (bf16[128,2048]{1,0:T(8,128)(2,1)}, bf16[512,256]{1,0:T(8,128)(2,1)S(1)}, bf16[512,256]{1,0:T(8,128)(2,1)S(1)}, bf16[512,256]{1,0:T(8,128)(2,1)S(1)}, bf16[512,256]{1,0:T(8,128)(2,1)S(1)}) custom-call(s32[1]{0:T(128)} %bitcast.2.me, s32[32]{0:T(128)S(1)} %copy-done.2, s32[16]{0:T(128)S(1)} %bitcast.39, bf16[128,2048]{1,0:T(8,128)(2,1)S(1)} %bitcast.38, ...), custom_call_target="tpu_custom_call" | custom-call | flops 60000002048 | tf_op jit(solution)/shard_map/attention_grads/pallas_call | solution.py:131
  40.4 4.6 %collective-permute-start.6 = (bf16[512,256]{1,0:T(8,128)(2,1)S(1)}, bf16[512,256]{1,0:T(8,128)(2,1)S(1)}, u32[]{:S(2)}, u32[]{:S(2)}) collective-permute-start(bf16[512,256]{1,0:T(8,128)(2,1)S(1)} %get-tuple-element.16), channel_id=1, source_target_pairs={{0,2},{2,0},{4,6},{6,4},{8,10},{10,8},{12,14},{14,12},{16,18},{18,... | collective-permute-start | bytes 786440 | tf_op jit(solution)/shard_map/ppermute | solution.py:23
  45.0 1.5 %collective-permute-start.8 = (bf16[512,256]{1,0:T(8,128)(2,1)S(1)}, bf16[512,256]{1,0:T(8,128)(2,1)S(1)}, u32[]{:S(2)}, u32[]{:S(2)}) collective-permute-start(bf16[512,256]{1,0:T(8,128)(2,1)S(1)} %get-tuple-element.18), channel_id=1, source_target_pairs={{0,6},{2,4},{4,2},{6,0},{8,14},{10,12},{12,10},{14,8},{16,22},{18,... | collective-permute-start | bytes 786440 | tf_op jit(solution)/shard_map/ppermute | solution.py:23
  46.5 12.6 %collective-permute-done.6 = bf16[512,256]{1,0:T(8,128)(2,1)S(1)} collective-permute-done((bf16[512,256]{1,0:T(8,128)(2,1)S(1)}, bf16[512,256]{1,0:T(8,128)(2,1)S(1)}, u32[]{:S(2)}, u32[]{:S(2)}) %collective-permute-start.6) | collective-permute-done | bytes 262176 | tf_op jit(solution)/shard_map/ppermute | solution.py:23
  59.0 7.6 %collective-permute-done.8 = bf16[512,256]{1,0:T(8,128)(2,1)S(1)} collective-permute-done((bf16[512,256]{1,0:T(8,128)(2,1)S(1)}, bf16[512,256]{1,0:T(8,128)(2,1)S(1)}, u32[]{:S(2)}, u32[]{:S(2)}) %collective-permute-start.8) | collective-permute-done | bytes 262176 | tf_op jit(solution)/shard_map/ppermute | solution.py:23
  66.8 4.9 %collective-permute-start.10 = (bf16[128,256]{1,0:T(8,128)(2,1)S(1)}, bf16[128,256]{1,0:T(8,128)(2,1)S(1)}, u32[]{:S(2)}, u32[]{:S(2)}) collective-permute-start(bf16[128,256]{1,0:T(8,128)(2,1)S(1)} %get-tuple-element.27), channel_id=1, source_target_pairs={{0,16},{2,18},{4,20},{6,22},{8,24},{10,26},{12,28},{14,30},{16,0},... | collective-permute-start | bytes 196616 | tf_op jit(solution)/shard_map/ppermute | solution.py:23
  71.7 0.6 collective-permute-start.9
  72.3 2.4 %collective-permute-done.10 = bf16[128,256]{1,0:T(8,128)(2,1)S(1)} collective-permute-done((bf16[128,256]{1,0:T(8,128)(2,1)S(1)}, bf16[128,256]{1,0:T(8,128)(2,1)S(1)}, u32[]{:S(2)}, u32[]{:S(2)}) %collective-permute-start.10) | collective-permute-done | bytes 65568 | tf_op jit(solution)/shard_map/ppermute | solution.py:23
  74.7 3.0 %collective-permute-done.11 = bf16[128,256]{1,0:T(8,128)(2,1)S(1)} collective-permute-done((bf16[128,256]{1,0:T(8,128)(2,1)S(1)}, bf16[128,256]{1,0:T(8,128)(2,1)S(1)}, u32[]{:S(2)}, u32[]{:S(2)}) %collective-permute-start.11) | collective-permute-done | bytes 65568 | tf_op jit(solution)/shard_map/ppermute | solution.py:23
  78.0 2.6 %collective-permute-start.13 = (bf16[128,256]{1,0:T(8,128)(2,1)S(1)}, bf16[128,256]{1,0:T(8,128)(2,1)S(1)}, u32[]{:S(2)}, u32[]{:S(2)}) collective-permute-start(bf16[128,256]{1,0:T(8,128)(2,1)S(1)} %fusion.3), channel_id=1, source_target_pairs={{0,16},{2,18},{4,20},{6,22},{8,24},{10,26},{12,28},{14,30},{16,0},... | collective-permute-start | bytes 196616 | tf_op jit(solution)/shard_map/ppermute | solution.py:23
  80.5 1.8 %collective-permute-start.14 = (bf16[128,256]{1,0:T(8,128)(2,1)S(1)}, bf16[128,256]{1,0:T(8,128)(2,1)S(1)}, u32[]{:S(2)}, u32[]{:S(2)}) collective-permute-start(bf16[128,256]{1,0:T(8,128)(2,1)S(1)} %fusion.3), channel_id=1, source_target_pairs={{0,24},{2,26},{4,28},{6,30},{8,16},{10,18},{12,20},{14,22},{16,8},... | collective-permute-start | bytes 196616 | tf_op jit(solution)/shard_map/ppermute | solution.py:23
  82.3 1.3 %collective-permute-done.12 = bf16[128,256]{1,0:T(8,128)(2,1)S(1)} collective-permute-done((bf16[128,256]{1,0:T(8,128)(2,1)S(1)}, bf16[128,256]{1,0:T(8,128)(2,1)S(1)}, u32[]{:S(2)}, u32[]{:S(2)}) %collective-permute-start.12) | collective-permute-done | bytes 65568 | tf_op jit(solution)/shard_map/ppermute | solution.py:23
  83.6 2.0 %collective-permute-done.13 = bf16[128,256]{1,0:T(8,128)(2,1)S(1)} collective-permute-done((bf16[128,256]{1,0:T(8,128)(2,1)S(1)}, bf16[128,256]{1,0:T(8,128)(2,1)S(1)}, u32[]{:S(2)}, u32[]{:S(2)}) %collective-permute-start.13) | collective-permute-done | bytes 65568 | tf_op jit(solution)/shard_map/ppermute | solution.py:23
  85.7 1.0 collective-permute-done.14
  87.2 1.9 %collective-permute-start.15 = (bf16[512,256]{1,0:T(8,128)(2,1)S(1)}, bf16[512,256]{1,0:T(8,128)(2,1)S(1)}, u32[]{:S(2)}, u32[]{:S(2)}) collective-permute-start(bf16[512,256]{1,0:T(8,128)(2,1)S(1)} %pad_maximum_fusion.1.refs_0_), channel_id=1, source_target_pairs={{0,4},{2,6},{4,0},{6,2},{8,12},{10,14},{12,8},{14,10},{16,20},{18,... | collective-permute-start | bytes 786440 | tf_op jit(solution)/shard_map/ppermute | solution.py:23
  89.0 1.2 %collective-permute-start.16 = (bf16[512,256]{1,0:T(8,128)(2,1)S(1)}, bf16[512,256]{1,0:T(8,128)(2,1)S(1)}, u32[]{:S(2)}, u32[]{:S(2)}) collective-permute-start(bf16[512,256]{1,0:T(8,128)(2,1)S(1)} %pad_maximum_fusion.1.refs_0_), channel_id=1, source_target_pairs={{0,6},{2,4},{4,2},{6,0},{8,14},{10,12},{12,10},{14,8},{16,22},{18,... | collective-permute-start | bytes 786440 | tf_op jit(solution)/shard_map/ppermute | solution.py:23
  90.3 2.1 %weight_step.3.refs_3_ = f32[256,1024]{1,0:T(8,128)S(1)} custom-call(s32[2]{0:T(128)S(1)} %pad_add_fusion.1.place, bf16[512,256]{1,0:T(8,128)(2,1)S(1)} %pad_maximum_fusion.1.refs_0_, bf16[4,4,64,1024]{3,2,1,0:T(8,128)(2,1)S(1)} %bitcast.32, bf16[4,4,64,1024]{3,2,1,0:T(8,128)(2,1)} %bitcast.16.refs_2_.refs_3_), custom_call_target="tpu_custom_call" | custom-call | tf_op jit(solution)/shard_map/weight_step/pallas_call | solution.py:184
  92.4 3.6 %collective-permute-done.18.refs_0_ = bf16[512,256]{1,0:T(8,128)(2,1)S(1)} collective-permute-done((bf16[512,256]{1,0:T(8,128)(2,1)S(1)}, bf16[512,256]{1,0:T(8,128)(2,1)S(1)}, u32[]{:S(2)}, u32[]{:S(2)}) %collective-permute-start.18) | collective-permute-done | bytes 262176 | tf_op jit(solution)/shard_map/ppermute | solution.py:23
  96.0 2.1 %weight_step.4.refs_4_ = f32[256,1024]{1,0:T(8,128)S(1)} custom-call(s32[2]{0:T(128)S(1)} %pad_add_fusion.1.place, bf16[512,256]{1,0:T(8,128)(2,1)S(1)} %collective-permute-done.18.refs_0_, bf16[4,4,64,1024]{3,2,1,0:T(8,128)(2,1)S(1)} %bitcast.33, bf16[4,4,64,1024]{3,2,1,0:T(8,128)(2,1)} %bitcast.16.refs_2_.refs_3_, f32[256,1024]{1,0:T(8,128)S(1)} %weight_step.3.refs_3_), custom_call_target="tpu_custom_call" | custom-call | tf_op jit(solution)/shard_map/weight_step/pallas_call | solution.py:184
  98.1 1.3 %collective-permute-done.15.refs_0_ = bf16[512,256]{1,0:T(8,128)(2,1)S(1)} collective-permute-done((bf16[512,256]{1,0:T(8,128)(2,1)S(1)}, bf16[512,256]{1,0:T(8,128)(2,1)S(1)}, u32[]{:S(2)}, u32[]{:S(2)}) %collective-permute-start.15) | collective-permute-done | bytes 262176 | tf_op jit(solution)/shard_map/ppermute | solution.py:23
  99.3 1.5 %collective-permute-done.16.refs_1_ = bf16[512,256]{1,0:T(8,128)(2,1)S(1)} collective-permute-done((bf16[512,256]{1,0:T(8,128)(2,1)S(1)}, bf16[512,256]{1,0:T(8,128)(2,1)S(1)}, u32[]{:S(2)}, u32[]{:S(2)}) %collective-permute-start.16) | collective-permute-done | bytes 262176 | tf_op jit(solution)/shard_map/ppermute | solution.py:23
  100.9 3.4 %weight_step.5 = (f32[1024,128]{1,0:T(8,128)}, f32[1024,128]{1,0:T(8,128)}) custom-call(s32[2]{0:T(128)S(1)} %pad_add_fusion.1.place, bf16[512,256]{1,0:T(8,128)(2,1)S(1)} %collective-permute-done.15.refs_0_, bf16[512,256]{1,0:T(8,128)(2,1)S(1)} %collective-permute-done.16.refs_1_, bf16[4,4,64,1024]{3,2,1,0:T(8,128)(2,1)S(1)} %bitcast.34, ...), custom_call_target="tpu_custom_call" | custom-call | tf_op jit(solution)/shard_map/weight_step/pallas_call | solution.py:184
  (37 shorter events, 2.2 us)
Async XLA Ops:
  1.4 11.0 %collective-permute-start = (bf16[1,128,256]{2,1,0:T(8,128)(2,1)S(1)}, bf16[1,128,256]{2,1,0:T(8,128)(2,1)S(1)}, u32[]{:S(2)}, u32[]{:S(2)}) collective-permute-start(bf16[1,128,256]{2,1,0:T(8,128)(2,1)S(1)} %pad_add_fusion), channel_id=1, source_target_pairs={{0,8},{2,10},{4,12},{6,14},{8,0},{10,2},{12,4},{14,6},{16,24},{18,... | collective-permute-start | bytes 196616 | tf_op jit(solution)/shard_map/ppermute | solution.py:23
  4.5 7.9 %collective-permute-start.1 = (bf16[1,128,256]{2,1,0:T(8,128)(2,1)S(1)}, bf16[1,128,256]{2,1,0:T(8,128)(2,1)S(1)}, u32[]{:S(2)}, u32[]{:S(2)}) collective-permute-start(bf16[1,128,256]{2,1,0:T(8,128)(2,1)S(1)} %pad_add_fusion), channel_id=1, source_target_pairs={{0,16},{2,18},{4,20},{6,22},{8,24},{10,26},{12,28},{14,30},{16,0},... | collective-permute-start | bytes 196616 | tf_op jit(solution)/shard_map/ppermute | solution.py:23
  7.1 6.1 %collective-permute-start.2 = (bf16[1,128,256]{2,1,0:T(8,128)(2,1)S(1)}, bf16[1,128,256]{2,1,0:T(8,128)(2,1)S(1)}, u32[]{:S(2)}, u32[]{:S(2)}) collective-permute-start(bf16[1,128,256]{2,1,0:T(8,128)(2,1)S(1)} %pad_add_fusion), channel_id=1, source_target_pairs={{0,24},{2,26},{4,28},{6,30},{8,16},{10,18},{12,20},{14,22},{16,8},... | collective-permute-start | bytes 196616 | tf_op jit(solution)/shard_map/ppermute | solution.py:23
  9.9 6.9 %copy-start = (bf16[1,128,2048]{2,1,0:T(8,128)(2,1)S(1)}, bf16[1,128,2048]{2,1,0:T(8,128)(2,1)}, u32[]{:S(2)}) copy-start(bf16[1,128,2048]{2,1,0:T(8,128)(2,1)} %param.12) | copy-start | bytes 1572868
  9.9 7.0 %copy-start.4 = (bf16[1,128,2048]{2,1,0:T(8,128)(2,1)S(1)}, bf16[1,128,2048]{2,1,0:T(8,128)(2,1)}, u32[]{:S(2)}) copy-start(bf16[1,128,2048]{2,1,0:T(8,128)(2,1)} %param.11) | copy-start | bytes 1572868
  13.2 10.8 %collective-permute-start.3 = (bf16[1,512,256]{2,1,0:T(8,128)(2,1)S(1)}, bf16[1,512,256]{2,1,0:T(8,128)(2,1)}, u32[]{:S(2)}, u32[]{:S(2)}) collective-permute-start(bf16[1,512,256]{2,1,0:T(8,128)(2,1)S(1)} %pad_maximum_fusion), channel_id=1, source_target_pairs={{0,2},{2,0},{4,6},{6,4},{8,10},{10,8},{12,14},{14,12},{16,18},{18,... | collective-permute-start | bytes 786440 | tf_op jit(solution)/shard_map/ppermute | solution.py:23
  14.7 18.4 %collective-permute-start.4 = (bf16[1,512,256]{2,1,0:T(8,128)(2,1)S(1)}, bf16[1,512,256]{2,1,0:T(8,128)(2,1)}, u32[]{:S(2)}, u32[]{:S(2)}) collective-permute-start(bf16[1,512,256]{2,1,0:T(8,128)(2,1)S(1)} %pad_maximum_fusion), channel_id=1, source_target_pairs={{0,4},{2,6},{4,0},{6,2},{8,12},{10,14},{12,8},{14,10},{16,20},{18,... | collective-permute-start | bytes 786440 | tf_op jit(solution)/shard_map/ppermute | solution.py:23
  16.3 16.9 %collective-permute-start.5 = (bf16[1,512,256]{2,1,0:T(8,128)(2,1)S(1)}, bf16[1,512,256]{2,1,0:T(8,128)(2,1)}, u32[]{:S(2)}, u32[]{:S(2)}) collective-permute-start(bf16[1,512,256]{2,1,0:T(8,128)(2,1)S(1)} %pad_maximum_fusion), channel_id=1, source_target_pairs={{0,6},{2,4},{4,2},{6,0},{8,14},{10,12},{12,10},{14,8},{16,22},{18,... | collective-permute-start | bytes 786440 | tf_op jit(solution)/shard_map/ppermute | solution.py:23
  17.5 15.6 %copy-start.1 = (bf16[1,128,2048]{2,1,0:T(8,128)(2,1)S(1)}, bf16[1,128,2048]{2,1,0:T(8,128)(2,1)}, u32[]{:S(2)}) copy-start(bf16[1,128,2048]{2,1,0:T(8,128)(2,1)} %param.8) | copy-start | bytes 1572868
  17.5 15.6 %copy-start.2 = (s32[32]{0:T(128)S(1)}, s32[32]{0:T(128)}, u32[]{:S(2)}) copy-start(s32[32]{0:T(128)} %slots.1) | copy-start | bytes 388
  17.5 15.6 %copy-start.3 = (s32[1,16]{1,0:T(1,128)S(1)}, s32[1,16]{1,0:T(1,128)}, u32[]{:S(2)}) copy-start(s32[1,16]{1,0:T(1,128)} %param.14) | copy-start | bytes 196
  17.5 60.2 %all-to-all-start = ((bf16[16,64,1024]{2,1,0:T(8,128)(2,1)}), bf16[16,64,1024]{2,1,0:T(8,128)(2,1)S(1)}, u32[]{:S(2)}, u32[]{:S(2)}) async-start(bf16[16,64,1024]{2,1,0:T(8,128)(2,1)} %bitcast.40), calls=%async_computation | async-start | bytes 4194304 | tf_op jit(solution)/shard_map/all_to_all | solution.py:221
  40.4 18.6 %collective-permute-start.6 = (bf16[512,256]{1,0:T(8,128)(2,1)S(1)}, bf16[512,256]{1,0:T(8,128)(2,1)S(1)}, u32[]{:S(2)}, u32[]{:S(2)}) collective-permute-start(bf16[512,256]{1,0:T(8,128)(2,1)S(1)} %get-tuple-element.16), channel_id=1, source_target_pairs={{0,2},{2,0},{4,6},{6,4},{8,10},{10,8},{12,14},{14,12},{16,18},{18,... | collective-permute-start | bytes 786440 | tf_op jit(solution)/shard_map/ppermute | solution.py:23
  45.0 14.0 %collective-permute-start.7 = (bf16[512,256]{1,0:T(8,128)(2,1)S(1)}, bf16[512,256]{1,0:T(8,128)(2,1)S(1)}, u32[]{:S(2)}, u32[]{:S(2)}) collective-permute-start(bf16[512,256]{1,0:T(8,128)(2,1)S(1)} %get-tuple-element.17), channel_id=1, source_target_pairs={{0,4},{2,6},{4,0},{6,2},{8,12},{10,14},{12,8},{14,10},{16,20},{18,... | collective-permute-start | bytes 786440 | tf_op jit(solution)/shard_map/ppermute | solution.py:23
  45.0 21.6 %collective-permute-start.8 = (bf16[512,256]{1,0:T(8,128)(2,1)S(1)}, bf16[512,256]{1,0:T(8,128)(2,1)S(1)}, u32[]{:S(2)}, u32[]{:S(2)}) collective-permute-start(bf16[512,256]{1,0:T(8,128)(2,1)S(1)} %get-tuple-element.18), channel_id=1, source_target_pairs={{0,6},{2,4},{4,2},{6,0},{8,14},{10,12},{12,10},{14,8},{16,22},{18,... | collective-permute-start | bytes 786440 | tf_op jit(solution)/shard_map/ppermute | solution.py:23
  66.8 8.0 %collective-permute-start.10 = (bf16[128,256]{1,0:T(8,128)(2,1)S(1)}, bf16[128,256]{1,0:T(8,128)(2,1)S(1)}, u32[]{:S(2)}, u32[]{:S(2)}) collective-permute-start(bf16[128,256]{1,0:T(8,128)(2,1)S(1)} %get-tuple-element.27), channel_id=1, source_target_pairs={{0,16},{2,18},{4,20},{6,22},{8,24},{10,26},{12,28},{14,30},{16,0},... | collective-permute-start | bytes 196616 | tf_op jit(solution)/shard_map/ppermute | solution.py:23
  71.7 6.1 %collective-permute-start.11 = (bf16[128,256]{1,0:T(8,128)(2,1)S(1)}, bf16[128,256]{1,0:T(8,128)(2,1)S(1)}, u32[]{:S(2)}, u32[]{:S(2)}) collective-permute-start(bf16[128,256]{1,0:T(8,128)(2,1)S(1)} %get-tuple-element.26), channel_id=1, source_target_pairs={{0,24},{2,26},{4,28},{6,30},{8,16},{10,18},{12,20},{14,22},{16,8},... | collective-permute-start | bytes 196616 | tf_op jit(solution)/shard_map/ppermute | solution.py:23
  71.7 6.1 %collective-permute-start.9 = (bf16[128,256]{1,0:T(8,128)(2,1)S(1)}, bf16[128,256]{1,0:T(8,128)(2,1)S(1)}, u32[]{:S(2)}, u32[]{:S(2)}) collective-permute-start(bf16[128,256]{1,0:T(8,128)(2,1)S(1)} %get-tuple-element.25), channel_id=1, source_target_pairs={{0,8},{2,10},{4,12},{6,14},{8,0},{10,2},{12,4},{14,6},{16,24},{18,... | collective-permute-start | bytes 196616 | tf_op jit(solution)/shard_map/ppermute | solution.py:23
  77.8 12.5 %collective-permute-start.17 = (bf16[16,64,1024]{2,1,0:T(8,128)(2,1)S(1)}, bf16[16,64,1024]{2,1,0:T(8,128)(2,1)}, u32[]{:S(2)}, u32[]{:S(2)}) collective-permute-start(bf16[16,64,1024]{2,1,0:T(8,128)(2,1)S(1)} %all-to-all-done), channel_id=1, source_target_pairs={{0,1},{1,0},{2,3},{3,2},{4,5},{5,4},{6,7},{7,6},{8,9},{9,8},{10,11... | collective-permute-start | bytes 6291464 | tf_op jit(solution)/shard_map/ppermute | solution.py:248
  77.9 5.7 %collective-permute-start.12 = (bf16[128,256]{1,0:T(8,128)(2,1)S(1)}, bf16[128,256]{1,0:T(8,128)(2,1)S(1)}, u32[]{:S(2)}, u32[]{:S(2)}) collective-permute-start(bf16[128,256]{1,0:T(8,128)(2,1)S(1)} %fusion.3), channel_id=1, source_target_pairs={{0,8},{2,10},{4,12},{6,14},{8,0},{10,2},{12,4},{14,6},{16,24},{18,... | collective-permute-start | bytes 196616 | tf_op jit(solution)/shard_map/ppermute | solution.py:23
  78.0 7.7 %collective-permute-start.13 = (bf16[128,256]{1,0:T(8,128)(2,1)S(1)}, bf16[128,256]{1,0:T(8,128)(2,1)S(1)}, u32[]{:S(2)}, u32[]{:S(2)}) collective-permute-start(bf16[128,256]{1,0:T(8,128)(2,1)S(1)} %fusion.3), channel_id=1, source_target_pairs={{0,16},{2,18},{4,20},{6,22},{8,24},{10,26},{12,28},{14,30},{16,0},... | collective-permute-start | bytes 196616 | tf_op jit(solution)/shard_map/ppermute | solution.py:23
  80.5 6.1 %collective-permute-start.14 = (bf16[128,256]{1,0:T(8,128)(2,1)S(1)}, bf16[128,256]{1,0:T(8,128)(2,1)S(1)}, u32[]{:S(2)}, u32[]{:S(2)}) collective-permute-start(bf16[128,256]{1,0:T(8,128)(2,1)S(1)} %fusion.3), channel_id=1, source_target_pairs={{0,24},{2,26},{4,28},{6,30},{8,16},{10,18},{12,20},{14,22},{16,8},... | collective-permute-start | bytes 196616 | tf_op jit(solution)/shard_map/ppermute | solution.py:23
  86.7 9.3 %collective-permute-start.18 = (bf16[512,256]{1,0:T(8,128)(2,1)S(1)}, bf16[512,256]{1,0:T(8,128)(2,1)S(1)}, u32[]{:S(2)}, u32[]{:S(2)}) collective-permute-start(bf16[512,256]{1,0:T(8,128)(2,1)S(1)} %pad_maximum_fusion.1.refs_0_), channel_id=1, source_target_pairs={{0,2},{2,0},{4,6},{6,4},{8,10},{10,8},{12,14},{14,12},{16,18},{18,... | collective-permute-start | bytes 786440 | tf_op jit(solution)/shard_map/ppermute | solution.py:23
  87.2 12.2 %collective-permute-start.15 = (bf16[512,256]{1,0:T(8,128)(2,1)S(1)}, bf16[512,256]{1,0:T(8,128)(2,1)S(1)}, u32[]{:S(2)}, u32[]{:S(2)}) collective-permute-start(bf16[512,256]{1,0:T(8,128)(2,1)S(1)} %pad_maximum_fusion.1.refs_0_), channel_id=1, source_target_pairs={{0,4},{2,6},{4,0},{6,2},{8,12},{10,14},{12,8},{14,10},{16,20},{18,... | collective-permute-start | bytes 786440 | tf_op jit(solution)/shard_map/ppermute | solution.py:23
  89.0 11.8 %collective-permute-start.16 = (bf16[512,256]{1,0:T(8,128)(2,1)S(1)}, bf16[512,256]{1,0:T(8,128)(2,1)S(1)}, u32[]{:S(2)}, u32[]{:S(2)}) collective-permute-start(bf16[512,256]{1,0:T(8,128)(2,1)S(1)} %pad_maximum_fusion.1.refs_0_), channel_id=1, source_target_pairs={{0,6},{2,4},{4,2},{6,0},{8,14},{10,12},{12,10},{14,8},{16,22},{18,... | collective-permute-start | bytes 786440 | tf_op jit(solution)/shard_map/ppermute | solution.py:23

commit v6 on v5

--- a/solution.py
+++ b/solution.py
@@ -69,17 +69,19 @@
         def score_place(i):
             return pl.ds(pl.multiple_of(i * chunk, chunk), chunk)
 
-        row_in_span = lax.broadcasted_iota(jnp.int32, (chunk, lanes), 1) % span_rows
-        key_in_chunk = lax.broadcasted_iota(jnp.int32, (chunk, lanes), 0)
-        ahead = key_in_chunk - row_in_span
-
-        def raw_scores(i, largest):
+        def raw_scores(i, largest, masked):
             found = dot(k_pos[key_place(i), :], q_rows[...], NT)
-            found = jnp.where(ahead <= span * span_rows - first - i * chunk, found, -1e30)
+            if masked:
+                row_in_span = lax.broadcasted_iota(jnp.int32, (chunk, lanes), 1) % span_rows
+                ahead = lax.broadcasted_iota(jnp.int32, (chunk, lanes), 0) - row_in_span
+                found = jnp.where(ahead <= span * span_rows - first - i * chunk, found, -1e30)
             scores[score_place(i), :] = found
             return jnp.maximum(largest, jnp.max(found.reshape(chunk // 8, 8, lanes), axis=0))
 
-        largest = lax.fori_loop(0, chunks, raw_scores, jnp.full((8, lanes), -1e30, jnp.float32))
+        largest = lax.fori_loop(
+            0, chunks - 1, functools.partial(raw_scores, masked=False), jnp.full((8, lanes), -1e30, jnp.float32)
+        )
+        largest = raw_scores(chunks - 1, largest, True)
         largest = jnp.max(largest, axis=0, keepdims=True)
 
         def weigh(i, total_weight):
@@ -163,12 +165,12 @@
                 tokens.append(ref[h, own_low ^ digit])
                 start = ((h ^ own_high) * parts + (part ^ own_part)) * rows
                 grads.append(grad_ref[pl.ds(pl.multiple_of(start, rows), rows), :])
-    found = dot(jnp.concatenate(grads, axis=0), jnp.concatenate(tokens, axis=0), TN)
+    found = dot(jnp.concatenate(tokens, axis=0), jnp.concatenate(grads, axis=0), TN)
     if more:
         found = refs[0][...] + found
     if last:
-        refs[-2][...] = found[:head, :].T
-        refs[-1][...] = found[head:, :].T
+        refs[-2][...] = found[:, :head]
+        refs[-1][...] = found[:, head:]
     else:
         refs[-1][...] = found
 
@@ -178,7 +180,7 @@
     parts = len(columns)
     last = digits[-1] == low - 1
     columns = [c.reshape(count // low, low, rows, width) for c in columns]
-    shapes = ((width, head),) * 2 if last else ((2 * head, width),)
+    shapes = ((width, head),) * 2 if last else ((width, 2 * head),)
     operands = [grads[d] for d in digits] + columns + ([] if sums is None else [sums])
     vmem = pl.BlockSpec(memory_space=pltpu.VMEM)
     return pl.pallas_call(
@@ -243,7 +245,7 @@
         own_grads = sum(p.astype(jnp.float32) for p in arrived).astype(jnp.bfloat16)
         column = jnp.concatenate([own_grads] + [swap(own_grads, k * low, count) for k in range(1, high)], axis=0)
         columns = [column] + [swap(column, k, count) for k in range(1, low)]
-        held = after(mine.reshape(count, batch_count, -1, column_count)[:, b], own_grads)
+        held = after(mine.reshape(count, batch_count, -1, column_count)[:, b], column)
         held = [held] + [
             lax.ppermute(held, "tensor", [(i, i ^ k) for i in range(tensor_count)]) for k in range(1, tensor_count)
         ]

time: 104 us -> 106 us (1.019)
  starting transfers between devices: 35.4 us -> 42.3 us
  waiting for transfers between devices: 46.1 us -> 41.3 us
    ppermute x18, starting transfers between devices: 28.8 us -> 35.7 us  [swap(): lax.ppermute(value, 'context', [(i, i ^ offset) for i in range(count)])]
    ppermute x18, waiting for transfers between devices: 46.1 us -> 40.7 us  [swap(): lax.ppermute(value, 'context', [(i, i ^ offset) for i in range(count)])]
  transfers between devices with their start and end apart: 20 -> 20, of which waited for: 12 -> 11; matrix products, arithmetic and copies ran while one was open for 6% -> 6% of each run, Pallas kernels for 11% -> 11%
where the time goes in v6:
time: 106 us
  starting transfers between devices  42.3 us (40%)
  waiting for transfers between devices  41.3 us (39%)
  Pallas kernels  14.9 us (14%)
  local copies, waits for them, and re-layouts  5.71 us (5%)
  other arithmetic  1.41 us (1%)
    ppermute x18, waiting for transfers between devices, swap(): lax.ppermute(value, 'context', [(i, i ^ offset) for i in range(count)])  40.7 us
    ppermute x18, starting transfers between devices, swap(): lax.ppermute(value, 'context', [(i, i ^ offset) for i in range(count)])  35.7 us
    pallas_call x3, Pallas kernels, weight_step(): pl.pallas_call(functools.partial(weight_kernel, low=low, parts=parts, dig...  7.63 us
    pallas_call x1, Pallas kernels, attention_grads(): pl.pallas_call(body, out_shape=(jax.ShapeDtypeStruct((rows, width), jnp.b...  7.24 us
    all_to_all x1, starting transfers between devices, on_device(): lax.all_to_all(sent, 'context', split_axis=0, concat_axis=0, tiled=True)  6.48 us
    unnamed x13, local copies, waits for them, and re-layouts  3.05 us
    reshape x1, local copies, waits for them, and re-layouts, on_device(): sent = jnp.moveaxis(inputs.reshape(-1, count, column_count), 1, 0)  2.48 us
  transfers between devices with their start and end apart: 20, of which 11 were waited for; matrix products, arithmetic and copies ran while one was open for 6% of the time, Pallas kernels for 11%

profile of v6, /device:TPU:0, one launch (start us, length us, event | category | flops | bytes accessed | tf_op | source)
XLA Modules:
  0.0 106.4 jit_solution(17896628283493905997)
XLA Ops:
  0.6 0.8 pad_add_fusion
  1.4 3.1 %collective-permute-start = (bf16[1,128,256]{2,1,0:T(8,128)(2,1)S(1)}, bf16[1,128,256]{2,1,0:T(8,128)(2,1)S(1)}, u32[]{:S(2)}, u32[]{:S(2)}) collective-permute-start(bf16[1,128,256]{2,1,0:T(8,128)(2,1)S(1)} %pad_add_fusion), channel_id=1, source_target_pairs={{0,8},{2,10},{4,12},{6,14},{8,0},{10,2},{12,4},{14,6},{16,24},{18,... | collective-permute-start | bytes 196616 | tf_op jit(solution)/shard_map/ppermute | solution.py:23
  4.5 2.6 %collective-permute-start.1 = (bf16[1,128,256]{2,1,0:T(8,128)(2,1)S(1)}, bf16[1,128,256]{2,1,0:T(8,128)(2,1)S(1)}, u32[]{:S(2)}, u32[]{:S(2)}) collective-permute-start(bf16[1,128,256]{2,1,0:T(8,128)(2,1)S(1)} %pad_add_fusion), channel_id=1, source_target_pairs={{0,16},{2,18},{4,20},{6,22},{8,24},{10,26},{12,28},{14,30},{16,0},... | collective-permute-start | bytes 196616 | tf_op jit(solution)/shard_map/ppermute | solution.py:23
  7.1 2.8 %copy.25 = bf16[8,8,16,1024]{3,2,1,0:T(8,128)(2,1)S(1)} copy(bf16[8,8,16,1024]{3,1,2,0:T(8,128)(2,1)} %bitcast.42) | data formatting | bytes 4194304
  9.9 2.5 %copy.27 = bf16[64,16,1024]{2,0,1:T(8,128)(2,1)} copy(bf16[64,16,1024]{2,1,0:T(8,128)(2,1)S(1)} %bitcast.41) | data formatting | bytes 4194304 | tf_op jit(solution)/shard_map/reshape | solution.py:221
  12.4 0.8 collective-permute-done.2
  13.2 1.6 %collective-permute-start.3 = (bf16[1,512,256]{2,1,0:T(8,128)(2,1)S(1)}, bf16[1,512,256]{2,1,0:T(8,128)(2,1)}, u32[]{:S(2)}, u32[]{:S(2)}) collective-permute-start(bf16[1,512,256]{2,1,0:T(8,128)(2,1)S(1)} %pad_maximum_fusion), channel_id=1, source_target_pairs={{0,2},{2,0},{4,6},{6,4},{8,10},{10,8},{12,14},{14,12},{16,18},{18,... | collective-permute-start | bytes 786440 | tf_op jit(solution)/shard_map/ppermute | solution.py:23
  14.7 1.5 %collective-permute-start.4 = (bf16[1,512,256]{2,1,0:T(8,128)(2,1)S(1)}, bf16[1,512,256]{2,1,0:T(8,128)(2,1)}, u32[]{:S(2)}, u32[]{:S(2)}) collective-permute-start(bf16[1,512,256]{2,1,0:T(8,128)(2,1)S(1)} %pad_maximum_fusion), channel_id=1, source_target_pairs={{0,4},{2,6},{4,0},{6,2},{8,12},{10,14},{12,8},{14,10},{16,20},{18,... | collective-permute-start | bytes 786440 | tf_op jit(solution)/shard_map/ppermute | solution.py:23
  16.3 0.5 collective-permute-start.5
  17.0 0.4 fusion
  17.5 6.5 %all-to-all-start = ((bf16[16,64,1024]{2,1,0:T(8,128)(2,1)}), bf16[16,64,1024]{2,1,0:T(8,128)(2,1)S(1)}, u32[]{:S(2)}, u32[]{:S(2)}) async-start(bf16[16,64,1024]{2,1,0:T(8,128)(2,1)} %bitcast.40), calls=%async_computation | async-start | bytes 4194304 | tf_op jit(solution)/shard_map/all_to_all | solution.py:223
  24.0 9.1 %collective-permute-done.4 = bf16[1,512,256]{2,1,0:T(8,128)(2,1)} collective-permute-done((bf16[1,512,256]{2,1,0:T(8,128)(2,1)S(1)}, bf16[1,512,256]{2,1,0:T(8,128)(2,1)}, u32[]{:S(2)}, u32[]{:S(2)}) %collective-permute-start.4) | collective-permute-done | bytes 262176 | tf_op jit(solution)/shard_map/ppermute | solution.py:23
  33.1 7.2 %attention_grads.1 = (bf16[128,2048]{1,0:T(8,128)(2,1)}, bf16[512,256]{1,0:T(8,128)(2,1)S(1)}, bf16[512,256]{1,0:T(8,128)(2,1)S(1)}, bf16[512,256]{1,0:T(8,128)(2,1)S(1)}, bf16[512,256]{1,0:T(8,128)(2,1)S(1)}) custom-call(s32[1]{0:T(128)} %bitcast.2.me, s32[32]{0:T(128)S(1)} %copy-done.2, s32[16]{0:T(128)S(1)} %bitcast.39, bf16[128,2048]{1,0:T(8,128)(2,1)S(1)} %bitcast.38, ...), custom_call_target="tpu_custom_call" | custom-call | flops 60000002048 | tf_op jit(solution)/shard_map/attention_grads/pallas_call | solution.py:133
  40.4 3.5 %collective-permute-start.8 = (bf16[512,256]{1,0:T(8,128)(2,1)S(1)}, bf16[512,256]{1,0:T(8,128)(2,1)S(1)}, u32[]{:S(2)}, u32[]{:S(2)}) collective-permute-start(bf16[512,256]{1,0:T(8,128)(2,1)S(1)} %get-tuple-element.18), channel_id=1, source_target_pairs={{0,6},{2,4},{4,2},{6,0},{8,14},{10,12},{12,10},{14,8},{16,22},{18,... | collective-permute-start | bytes 786440 | tf_op jit(solution)/shard_map/ppermute | solution.py:23
  43.9 11.6 %collective-permute-done.6 = bf16[512,256]{1,0:T(8,128)(2,1)S(1)} collective-permute-done((bf16[512,256]{1,0:T(8,128)(2,1)S(1)}, bf16[512,256]{1,0:T(8,128)(2,1)S(1)}, u32[]{:S(2)}, u32[]{:S(2)}) %collective-permute-start.6) | collective-permute-done | bytes 262176 | tf_op jit(solution)/shard_map/ppermute | solution.py:23
  55.5 2.0 %collective-permute-done.8 = bf16[512,256]{1,0:T(8,128)(2,1)S(1)} collective-permute-done((bf16[512,256]{1,0:T(8,128)(2,1)S(1)}, bf16[512,256]{1,0:T(8,128)(2,1)S(1)}, u32[]{:S(2)}, u32[]{:S(2)}) %collective-permute-start.8) | collective-permute-done | bytes 262176 | tf_op jit(solution)/shard_map/ppermute | solution.py:23
  57.7 14.4 %collective-permute-start.10 = (bf16[128,256]{1,0:T(8,128)(2,1)S(1)}, bf16[128,256]{1,0:T(8,128)(2,1)S(1)}, u32[]{:S(2)}, u32[]{:S(2)}) collective-permute-start(bf16[128,256]{1,0:T(8,128)(2,1)S(1)} %get-tuple-element.27), channel_id=1, source_target_pairs={{0,16},{2,18},{4,20},{6,22},{8,24},{10,26},{12,28},{14,30},{16,0},... | collective-permute-start | bytes 196616 | tf_op jit(solution)/shard_map/ppermute | solution.py:23
  72.0 0.6 collective-permute-start.9
  72.7 2.0 %collective-permute-done.10 = bf16[128,256]{1,0:T(8,128)(2,1)S(1)} collective-permute-done((bf16[128,256]{1,0:T(8,128)(2,1)S(1)}, bf16[128,256]{1,0:T(8,128)(2,1)S(1)}, u32[]{:S(2)}, u32[]{:S(2)}) %collective-permute-start.10) | collective-permute-done | bytes 65568 | tf_op jit(solution)/shard_map/ppermute | solution.py:23
  74.7 3.9 %collective-permute-done.11 = bf16[128,256]{1,0:T(8,128)(2,1)S(1)} collective-permute-done((bf16[128,256]{1,0:T(8,128)(2,1)S(1)}, bf16[128,256]{1,0:T(8,128)(2,1)S(1)}, u32[]{:S(2)}, u32[]{:S(2)}) %collective-permute-start.11) | collective-permute-done | bytes 65568 | tf_op jit(solution)/shard_map/ppermute | solution.py:23
  78.7 2.8 %collective-permute-start.13 = (bf16[128,256]{1,0:T(8,128)(2,1)S(1)}, bf16[128,256]{1,0:T(8,128)(2,1)S(1)}, u32[]{:S(2)}, u32[]{:S(2)}) collective-permute-start(bf16[128,256]{1,0:T(8,128)(2,1)S(1)} %fusion.3), channel_id=1, source_target_pairs={{0,16},{2,18},{4,20},{6,22},{8,24},{10,26},{12,28},{14,30},{16,0},... | collective-permute-start | bytes 196616 | tf_op jit(solution)/shard_map/ppermute | solution.py:23
  81.6 1.5 %collective-permute-start.14 = (bf16[128,256]{1,0:T(8,128)(2,1)S(1)}, bf16[128,256]{1,0:T(8,128)(2,1)S(1)}, u32[]{:S(2)}, u32[]{:S(2)}) collective-permute-start(bf16[128,256]{1,0:T(8,128)(2,1)S(1)} %fusion.3), channel_id=1, source_target_pairs={{0,24},{2,26},{4,28},{6,30},{8,16},{10,18},{12,20},{14,22},{16,8},... | collective-permute-start | bytes 196616 | tf_op jit(solution)/shard_map/ppermute | solution.py:23
  83.1 0.9 collective-permute-done.13
  84.0 3.7 %collective-permute-done.14 = bf16[128,256]{1,0:T(8,128)(2,1)S(1)} collective-permute-done((bf16[128,256]{1,0:T(8,128)(2,1)S(1)}, bf16[128,256]{1,0:T(8,128)(2,1)S(1)}, u32[]{:S(2)}, u32[]{:S(2)}) %collective-permute-start.14) | collective-permute-done | bytes 65568 | tf_op jit(solution)/shard_map/ppermute | solution.py:23
  87.7 1.3 %collective-permute-start.18 = (bf16[512,256]{1,0:T(8,128)(2,1)S(1)}, bf16[512,256]{1,0:T(8,128)(2,1)S(1)}, u32[]{:S(2)}, u32[]{:S(2)}) collective-permute-start(bf16[512,256]{1,0:T(8,128)(2,1)S(1)} %pad_maximum_fusion.1.refs_0_), channel_id=1, source_target_pairs={{0,2},{2,0},{4,6},{6,4},{8,10},{10,8},{12,14},{14,12},{16,18},{18,... | collective-permute-start | bytes 786440 | tf_op jit(solution)/shard_map/ppermute | solution.py:23
  89.2 2.1 %collective-permute-start.16 = (bf16[512,256]{1,0:T(8,128)(2,1)S(1)}, bf16[512,256]{1,0:T(8,128)(2,1)S(1)}, u32[]{:S(2)}, u32[]{:S(2)}) collective-permute-start(bf16[512,256]{1,0:T(8,128)(2,1)S(1)} %pad_maximum_fusion.1.refs_0_), channel_id=1, source_target_pairs={{0,6},{2,4},{4,2},{6,0},{8,14},{10,12},{12,10},{14,8},{16,22},{18,... | collective-permute-start | bytes 786440 | tf_op jit(solution)/shard_map/ppermute | solution.py:23
  91.4 0.6 collective-permute-done.17
  92.0 2.1 %weight_step.3.refs_3_ = f32[1024,256]{1,0:T(8,128)S(1)} custom-call(s32[2]{0:T(128)S(1)} %pad_add_fusion.1.place, bf16[512,256]{1,0:T(8,128)(2,1)S(1)} %pad_maximum_fusion.1.refs_0_, bf16[4,4,64,1024]{3,2,1,0:T(8,128)(2,1)S(1)} %bitcast.32, bf16[4,4,64,1024]{3,2,1,0:T(8,128)(2,1)} %bitcast.16.refs_2_.refs_3_), custom_call_target="tpu_custom_call" | custom-call | tf_op jit(solution)/shard_map/weight_step/pallas_call | solution.py:186
  94.2 2.8 %collective-permute-done.18.refs_0_ = bf16[512,256]{1,0:T(8,128)(2,1)S(1)} collective-permute-done((bf16[512,256]{1,0:T(8,128)(2,1)S(1)}, bf16[512,256]{1,0:T(8,128)(2,1)S(1)}, u32[]{:S(2)}, u32[]{:S(2)}) %collective-permute-start.18) | collective-permute-done | bytes 262176 | tf_op jit(solution)/shard_map/ppermute | solution.py:23
  96.9 2.1 %weight_step.4.refs_4_ = f32[1024,256]{1,0:T(8,128)S(1)} custom-call(s32[2]{0:T(128)S(1)} %pad_add_fusion.1.place, bf16[512,256]{1,0:T(8,128)(2,1)S(1)} %collective-permute-done.18.refs_0_, bf16[4,4,64,1024]{3,2,1,0:T(8,128)(2,1)S(1)} %bitcast.33, bf16[4,4,64,1024]{3,2,1,0:T(8,128)(2,1)} %bitcast.16.refs_2_.refs_3_, f32[1024,256]{1,0:T(8,128)S(1)} %weight_step.3.refs_3_), custom_call_target="tpu_custom_call" | custom-call | tf_op jit(solution)/shard_map/weight_step/pallas_call | solution.py:186
  99.1 4.0 %collective-permute-done.15.refs_0_ = bf16[512,256]{1,0:T(8,128)(2,1)S(1)} collective-permute-done((bf16[512,256]{1,0:T(8,128)(2,1)S(1)}, bf16[512,256]{1,0:T(8,128)(2,1)S(1)}, u32[]{:S(2)}, u32[]{:S(2)}) %collective-permute-start.15) | collective-permute-done | bytes 262176 | tf_op jit(solution)/shard_map/ppermute | solution.py:23
  103.0 3.4 %weight_step.5 = (f32[1024,128]{1,0:T(8,128)}, f32[1024,128]{1,0:T(8,128)}) custom-call(s32[2]{0:T(128)S(1)} %pad_add_fusion.1.place, bf16[512,256]{1,0:T(8,128)(2,1)S(1)} %collective-permute-done.15.refs_0_, bf16[512,256]{1,0:T(8,128)(2,1)S(1)} %collective-permute-done.16.refs_1_, bf16[4,4,64,1024]{3,2,1,0:T(8,128)(2,1)S(1)} %bitcast.34, ...), custom_call_target="tpu_custom_call" | custom-call | tf_op jit(solution)/shard_map/weight_step/pallas_call | solution.py:186
  (37 shorter events, 1.1 us)
Async XLA Ops:
  1.4 11.0 %collective-permute-start = (bf16[1,128,256]{2,1,0:T(8,128)(2,1)S(1)}, bf16[1,128,256]{2,1,0:T(8,128)(2,1)S(1)}, u32[]{:S(2)}, u32[]{:S(2)}) collective-permute-start(bf16[1,128,256]{2,1,0:T(8,128)(2,1)S(1)} %pad_add_fusion), channel_id=1, source_target_pairs={{0,8},{2,10},{4,12},{6,14},{8,0},{10,2},{12,4},{14,6},{16,24},{18,... | collective-permute-start | bytes 196616 | tf_op jit(solution)/shard_map/ppermute | solution.py:23
  4.5 7.9 %collective-permute-start.1 = (bf16[1,128,256]{2,1,0:T(8,128)(2,1)S(1)}, bf16[1,128,256]{2,1,0:T(8,128)(2,1)S(1)}, u32[]{:S(2)}, u32[]{:S(2)}) collective-permute-start(bf16[1,128,256]{2,1,0:T(8,128)(2,1)S(1)} %pad_add_fusion), channel_id=1, source_target_pairs={{0,16},{2,18},{4,20},{6,22},{8,24},{10,26},{12,28},{14,30},{16,0},... | collective-permute-start | bytes 196616 | tf_op jit(solution)/shard_map/ppermute | solution.py:23
  7.1 6.1 %collective-permute-start.2 = (bf16[1,128,256]{2,1,0:T(8,128)(2,1)S(1)}, bf16[1,128,256]{2,1,0:T(8,128)(2,1)S(1)}, u32[]{:S(2)}, u32[]{:S(2)}) collective-permute-start(bf16[1,128,256]{2,1,0:T(8,128)(2,1)S(1)} %pad_add_fusion), channel_id=1, source_target_pairs={{0,24},{2,26},{4,28},{6,30},{8,16},{10,18},{12,20},{14,22},{16,8},... | collective-permute-start | bytes 196616 | tf_op jit(solution)/shard_map/ppermute | solution.py:23
  9.9 6.9 %copy-start = (bf16[1,128,2048]{2,1,0:T(8,128)(2,1)S(1)}, bf16[1,128,2048]{2,1,0:T(8,128)(2,1)}, u32[]{:S(2)}) copy-start(bf16[1,128,2048]{2,1,0:T(8,128)(2,1)} %param.12) | copy-start | bytes 1572868
  9.9 7.0 %copy-start.4 = (bf16[1,128,2048]{2,1,0:T(8,128)(2,1)S(1)}, bf16[1,128,2048]{2,1,0:T(8,128)(2,1)}, u32[]{:S(2)}) copy-start(bf16[1,128,2048]{2,1,0:T(8,128)(2,1)} %param.11) | copy-start | bytes 1572868
  13.2 10.8 %collective-permute-start.3 = (bf16[1,512,256]{2,1,0:T(8,128)(2,1)S(1)}, bf16[1,512,256]{2,1,0:T(8,128)(2,1)}, u32[]{:S(2)}, u32[]{:S(2)}) collective-permute-start(bf16[1,512,256]{2,1,0:T(8,128)(2,1)S(1)} %pad_maximum_fusion), channel_id=1, source_target_pairs={{0,2},{2,0},{4,6},{6,4},{8,10},{10,8},{12,14},{14,12},{16,18},{18,... | collective-permute-start | bytes 786440 | tf_op jit(solution)/shard_map/ppermute | solution.py:23
  14.7 18.4 %collective-permute-start.4 = (bf16[1,512,256]{2,1,0:T(8,128)(2,1)S(1)}, bf16[1,512,256]{2,1,0:T(8,128)(2,1)}, u32[]{:S(2)}, u32[]{:S(2)}) collective-permute-start(bf16[1,512,256]{2,1,0:T(8,128)(2,1)S(1)} %pad_maximum_fusion), channel_id=1, source_target_pairs={{0,4},{2,6},{4,0},{6,2},{8,12},{10,14},{12,8},{14,10},{16,20},{18,... | collective-permute-start | bytes 786440 | tf_op jit(solution)/shard_map/ppermute | solution.py:23
  16.3 16.9 %collective-permute-start.5 = (bf16[1,512,256]{2,1,0:T(8,128)(2,1)S(1)}, bf16[1,512,256]{2,1,0:T(8,128)(2,1)}, u32[]{:S(2)}, u32[]{:S(2)}) collective-permute-start(bf16[1,512,256]{2,1,0:T(8,128)(2,1)S(1)} %pad_maximum_fusion), channel_id=1, source_target_pairs={{0,6},{2,4},{4,2},{6,0},{8,14},{10,12},{12,10},{14,8},{16,22},{18,... | collective-permute-start | bytes 786440 | tf_op jit(solution)/shard_map/ppermute | solution.py:23
  17.5 15.6 %copy-start.1 = (bf16[1,128,2048]{2,1,0:T(8,128)(2,1)S(1)}, bf16[1,128,2048]{2,1,0:T(8,128)(2,1)}, u32[]{:S(2)}) copy-start(bf16[1,128,2048]{2,1,0:T(8,128)(2,1)} %param.8) | copy-start | bytes 1572868
  17.5 15.6 %copy-start.2 = (s32[32]{0:T(128)S(1)}, s32[32]{0:T(128)}, u32[]{:S(2)}) copy-start(s32[32]{0:T(128)} %slots.1) | copy-start | bytes 388
  17.5 15.6 %copy-start.3 = (s32[1,16]{1,0:T(1,128)S(1)}, s32[1,16]{1,0:T(1,128)}, u32[]{:S(2)}) copy-start(s32[1,16]{1,0:T(1,128)} %param.14) | copy-start | bytes 196
  17.5 70.1 %all-to-all-start = ((bf16[16,64,1024]{2,1,0:T(8,128)(2,1)}), bf16[16,64,1024]{2,1,0:T(8,128)(2,1)S(1)}, u32[]{:S(2)}, u32[]{:S(2)}) async-start(bf16[16,64,1024]{2,1,0:T(8,128)(2,1)} %bitcast.40), calls=%async_computation | async-start | bytes 4194304 | tf_op jit(solution)/shard_map/all_to_all | solution.py:223
  40.4 15.1 %collective-permute-start.6 = (bf16[512,256]{1,0:T(8,128)(2,1)S(1)}, bf16[512,256]{1,0:T(8,128)(2,1)S(1)}, u32[]{:S(2)}, u32[]{:S(2)}) collective-permute-start(bf16[512,256]{1,0:T(8,128)(2,1)S(1)} %get-tuple-element.16), channel_id=1, source_target_pairs={{0,2},{2,0},{4,6},{6,4},{8,10},{10,8},{12,14},{14,12},{16,18},{18,... | collective-permute-start | bytes 786440 | tf_op jit(solution)/shard_map/ppermute | solution.py:23
  40.4 15.1 %collective-permute-start.7 = (bf16[512,256]{1,0:T(8,128)(2,1)S(1)}, bf16[512,256]{1,0:T(8,128)(2,1)S(1)}, u32[]{:S(2)}, u32[]{:S(2)}) collective-permute-start(bf16[512,256]{1,0:T(8,128)(2,1)S(1)} %get-tuple-element.17), channel_id=1, source_target_pairs={{0,4},{2,6},{4,0},{6,2},{8,12},{10,14},{12,8},{14,10},{16,20},{18,... | collective-permute-start | bytes 786440 | tf_op jit(solution)/shard_map/ppermute | solution.py:23
  40.4 17.1 %collective-permute-start.8 = (bf16[512,256]{1,0:T(8,128)(2,1)S(1)}, bf16[512,256]{1,0:T(8,128)(2,1)S(1)}, u32[]{:S(2)}, u32[]{:S(2)}) collective-permute-start(bf16[512,256]{1,0:T(8,128)(2,1)S(1)} %get-tuple-element.18), channel_id=1, source_target_pairs={{0,6},{2,4},{4,2},{6,0},{8,14},{10,12},{12,10},{14,8},{16,22},{18,... | collective-permute-start | bytes 786440 | tf_op jit(solution)/shard_map/ppermute | solution.py:23
  57.7 17.1 %collective-permute-start.10 = (bf16[128,256]{1,0:T(8,128)(2,1)S(1)}, bf16[128,256]{1,0:T(8,128)(2,1)S(1)}, u32[]{:S(2)}, u32[]{:S(2)}) collective-permute-start(bf16[128,256]{1,0:T(8,128)(2,1)S(1)} %get-tuple-element.27), channel_id=1, source_target_pairs={{0,16},{2,18},{4,20},{6,22},{8,24},{10,26},{12,28},{14,30},{16,0},... | collective-permute-start | bytes 196616 | tf_op jit(solution)/shard_map/ppermute | solution.py:23
  72.0 6.6 %collective-permute-start.11 = (bf16[128,256]{1,0:T(8,128)(2,1)S(1)}, bf16[128,256]{1,0:T(8,128)(2,1)S(1)}, u32[]{:S(2)}, u32[]{:S(2)}) collective-permute-start(bf16[128,256]{1,0:T(8,128)(2,1)S(1)} %get-tuple-element.26), channel_id=1, source_target_pairs={{0,24},{2,26},{4,28},{6,30},{8,16},{10,18},{12,20},{14,22},{16,8},... | collective-permute-start | bytes 196616 | tf_op jit(solution)/shard_map/ppermute | solution.py:23
  72.0 6.6 %collective-permute-start.9 = (bf16[128,256]{1,0:T(8,128)(2,1)S(1)}, bf16[128,256]{1,0:T(8,128)(2,1)S(1)}, u32[]{:S(2)}, u32[]{:S(2)}) collective-permute-start(bf16[128,256]{1,0:T(8,128)(2,1)S(1)} %get-tuple-element.25), channel_id=1, source_target_pairs={{0,8},{2,10},{4,12},{6,14},{8,0},{10,2},{12,4},{14,6},{16,24},{18,... | collective-permute-start | bytes 196616 | tf_op jit(solution)/shard_map/ppermute | solution.py:23
  78.7 4.5 %collective-permute-start.12 = (bf16[128,256]{1,0:T(8,128)(2,1)S(1)}, bf16[128,256]{1,0:T(8,128)(2,1)S(1)}, u32[]{:S(2)}, u32[]{:S(2)}) collective-permute-start(bf16[128,256]{1,0:T(8,128)(2,1)S(1)} %fusion.3), channel_id=1, source_target_pairs={{0,8},{2,10},{4,12},{6,14},{8,0},{10,2},{12,4},{14,6},{16,24},{18,... | collective-permute-start | bytes 196616 | tf_op jit(solution)/shard_map/ppermute | solution.py:23
  78.7 5.2 %collective-permute-start.13 = (bf16[128,256]{1,0:T(8,128)(2,1)S(1)}, bf16[128,256]{1,0:T(8,128)(2,1)S(1)}, u32[]{:S(2)}, u32[]{:S(2)}) collective-permute-start(bf16[128,256]{1,0:T(8,128)(2,1)S(1)} %fusion.3), channel_id=1, source_target_pairs={{0,16},{2,18},{4,20},{6,22},{8,24},{10,26},{12,28},{14,30},{16,0},... | collective-permute-start | bytes 196616 | tf_op jit(solution)/shard_map/ppermute | solution.py:23
  81.6 6.1 %collective-permute-start.14 = (bf16[128,256]{1,0:T(8,128)(2,1)S(1)}, bf16[128,256]{1,0:T(8,128)(2,1)S(1)}, u32[]{:S(2)}, u32[]{:S(2)}) collective-permute-start(bf16[128,256]{1,0:T(8,128)(2,1)S(1)} %fusion.3), channel_id=1, source_target_pairs={{0,24},{2,26},{4,28},{6,30},{8,16},{10,18},{12,20},{14,22},{16,8},... | collective-permute-start | bytes 196616 | tf_op jit(solution)/shard_map/ppermute | solution.py:23
  87.7 4.4 %collective-permute-start.17 = (bf16[16,64,1024]{2,1,0:T(8,128)(2,1)S(1)}, bf16[16,64,1024]{2,1,0:T(8,128)(2,1)}, u32[]{:S(2)}, u32[]{:S(2)}) collective-permute-start(bf16[16,64,1024]{2,1,0:T(8,128)(2,1)S(1)} %all-to-all-done), channel_id=1, source_target_pairs={{0,1},{1,0},{2,3},{3,2},{4,5},{5,4},{6,7},{7,6},{8,9},{9,8},{10,11... | collective-permute-start | bytes 6291464 | tf_op jit(solution)/shard_map/ppermute | solution.py:250
  87.7 9.2 %collective-permute-start.18 = (bf16[512,256]{1,0:T(8,128)(2,1)S(1)}, bf16[512,256]{1,0:T(8,128)(2,1)S(1)}, u32[]{:S(2)}, u32[]{:S(2)}) collective-permute-start(bf16[512,256]{1,0:T(8,128)(2,1)S(1)} %pad_maximum_fusion.1.refs_0_), channel_id=1, source_target_pairs={{0,2},{2,0},{4,6},{6,4},{8,10},{10,8},{12,14},{14,12},{16,18},{18,... | collective-permute-start | bytes 786440 | tf_op jit(solution)/shard_map/ppermute | solution.py:23
  89.0 14.0 %collective-permute-start.15 = (bf16[512,256]{1,0:T(8,128)(2,1)S(1)}, bf16[512,256]{1,0:T(8,128)(2,1)S(1)}, u32[]{:S(2)}, u32[]{:S(2)}) collective-permute-start(bf16[512,256]{1,0:T(8,128)(2,1)S(1)} %pad_maximum_fusion.1.refs_0_), channel_id=1, source_target_pairs={{0,4},{2,6},{4,0},{6,2},{8,12},{10,14},{12,8},{14,10},{16,20},{18,... | collective-permute-start | bytes 786440 | tf_op jit(solution)/shard_map/ppermute | solution.py:23
  89.2 13.8 %collective-permute-start.16 = (bf16[512,256]{1,0:T(8,128)(2,1)S(1)}, bf16[512,256]{1,0:T(8,128)(2,1)S(1)}, u32[]{:S(2)}, u32[]{:S(2)}) collective-permute-start(bf16[512,256]{1,0:T(8,128)(2,1)S(1)} %pad_maximum_fusion.1.refs_0_), channel_id=1, source_target_pairs={{0,6},{2,4},{4,2},{6,0},{8,14},{10,12},{12,10},{14,8},{16,22},{18,... | collective-permute-start | bytes 786440 | tf_op jit(solution)/shard_map/ppermute | solution.py:23

commit v7 on v5

--- a/solution.py
+++ b/solution.py
@@ -243,7 +243,7 @@
         own_grads = sum(p.astype(jnp.float32) for p in arrived).astype(jnp.bfloat16)
         column = jnp.concatenate([own_grads] + [swap(own_grads, k * low, count) for k in range(1, high)], axis=0)
         columns = [column] + [swap(column, k, count) for k in range(1, low)]
-        held = after(mine.reshape(count, batch_count, -1, column_count)[:, b], own_grads)
+        held = after(mine.reshape(count, batch_count, -1, column_count)[:, b], column)
         held = [held] + [
             lax.ppermute(held, "tensor", [(i, i ^ k) for i in range(tensor_count)]) for k in range(1, tensor_count)
         ]

time: 104 us -> 104 us (level)
  starting transfers between devices: 35.4 us -> 39.2 us
  waiting for transfers between devices: 46.1 us -> 43.8 us
  Pallas kernels: 14.8 us -> 13.1 us
    ppermute x18, starting transfers between devices: 28.8 us -> 32.6 us  [swap(): lax.ppermute(value, 'context', [(i, i ^ offset) for i in range(count)])]
    ppermute x18, waiting for transfers between devices: 46.1 us -> 43.2 us  [swap(): lax.ppermute(value, 'context', [(i, i ^ offset) for i in range(count)])]
    pallas_call x1, Pallas kernels: 7.28 us -> 5.62 us  [attention_grads(): pl.pallas_call(body, out_shape=(jax.ShapeDtypeStruct((rows, width), jnp.b...]
  transfers between devices with their start and end apart: 20 -> 20, of which waited for: 12 -> 11; matrix products, arithmetic and copies ran while one was open for 6% -> 6% of each run, Pallas kernels for 11% -> 9%
where the time goes in v7:
time: 104 us
  waiting for transfers between devices  43.8 us (42%)
  starting transfers between devices  39.2 us (38%)
  Pallas kernels  13.1 us (13%)
  local copies, waits for them, and re-layouts  5.71 us (5%)
  other arithmetic  1.41 us (1%)
    ppermute x18, waiting for transfers between devices, swap(): lax.ppermute(value, 'context', [(i, i ^ offset) for i in range(count)])  43.2 us
    ppermute x18, starting transfers between devices, swap(): lax.ppermute(value, 'context', [(i, i ^ offset) for i in range(count)])  32.6 us
    pallas_call x3, Pallas kernels, weight_step(): pl.pallas_call(functools.partial(weight_kernel, low=low, parts=parts, dig...  7.53 us
    all_to_all x1, starting transfers between devices, on_device(): lax.all_to_all(sent, 'context', split_axis=0, concat_axis=0, tiled=True)  6.48 us
    pallas_call x1, Pallas kernels, attention_grads(): pl.pallas_call(body, out_shape=(jax.ShapeDtypeStruct((rows, width), jnp.b...  5.62 us
    unnamed x13, local copies, waits for them, and re-layouts  3.05 us
    reshape x1, local copies, waits for them, and re-layouts, on_device(): sent = jnp.moveaxis(inputs.reshape(-1, count, column_count), 1, 0)  2.48 us
  transfers between devices with their start and end apart: 20, of which 11 were waited for; matrix products, arithmetic and copies ran while one was open for 6% of the time, Pallas kernels for 9%

profile of v7, /device:TPU:0, one launch (start us, length us, event | category | flops | bytes accessed | tf_op | source)
XLA Modules:
  0.0 104.1 jit_solution(12035113148801065809)
XLA Ops:
  0.6 0.8 pad_add_fusion
  1.4 3.1 %collective-permute-start = (bf16[1,128,256]{2,1,0:T(8,128)(2,1)S(1)}, bf16[1,128,256]{2,1,0:T(8,128)(2,1)S(1)}, u32[]{:S(2)}, u32[]{:S(2)}) collective-permute-start(bf16[1,128,256]{2,1,0:T(8,128)(2,1)S(1)} %pad_add_fusion), channel_id=1, source_target_pairs={{0,8},{2,10},{4,12},{6,14},{8,0},{10,2},{12,4},{14,6},{16,24},{18,... | collective-permute-start | bytes 196616 | tf_op jit(solution)/shard_map/ppermute | solution.py:23
  4.5 2.6 %collective-permute-start.1 = (bf16[1,128,256]{2,1,0:T(8,128)(2,1)S(1)}, bf16[1,128,256]{2,1,0:T(8,128)(2,1)S(1)}, u32[]{:S(2)}, u32[]{:S(2)}) collective-permute-start(bf16[1,128,256]{2,1,0:T(8,128)(2,1)S(1)} %pad_add_fusion), channel_id=1, source_target_pairs={{0,16},{2,18},{4,20},{6,22},{8,24},{10,26},{12,28},{14,30},{16,0},... | collective-permute-start | bytes 196616 | tf_op jit(solution)/shard_map/ppermute | solution.py:23
  7.1 2.8 %copy.25 = bf16[8,8,16,1024]{3,2,1,0:T(8,128)(2,1)S(1)} copy(bf16[8,8,16,1024]{3,1,2,0:T(8,128)(2,1)} %bitcast.42) | data formatting | bytes 4194304
  9.9 2.5 %copy.27 = bf16[64,16,1024]{2,0,1:T(8,128)(2,1)} copy(bf16[64,16,1024]{2,1,0:T(8,128)(2,1)S(1)} %bitcast.41) | data formatting | bytes 4194304 | tf_op jit(solution)/shard_map/reshape | solution.py:219
  12.4 0.8 collective-permute-done.2
  13.2 1.6 %collective-permute-start.3 = (bf16[1,512,256]{2,1,0:T(8,128)(2,1)S(1)}, bf16[1,512,256]{2,1,0:T(8,128)(2,1)}, u32[]{:S(2)}, u32[]{:S(2)}) collective-permute-start(bf16[1,512,256]{2,1,0:T(8,128)(2,1)S(1)} %pad_maximum_fusion), channel_id=1, source_target_pairs={{0,2},{2,0},{4,6},{6,4},{8,10},{10,8},{12,14},{14,12},{16,18},{18,... | collective-permute-start | bytes 786440 | tf_op jit(solution)/shard_map/ppermute | solution.py:23
  14.7 1.5 %collective-permute-start.4 = (bf16[1,512,256]{2,1,0:T(8,128)(2,1)S(1)}, bf16[1,512,256]{2,1,0:T(8,128)(2,1)}, u32[]{:S(2)}, u32[]{:S(2)}) collective-permute-start(bf16[1,512,256]{2,1,0:T(8,128)(2,1)S(1)} %pad_maximum_fusion), channel_id=1, source_target_pairs={{0,4},{2,6},{4,0},{6,2},{8,12},{10,14},{12,8},{14,10},{16,20},{18,... | collective-permute-start | bytes 786440 | tf_op jit(solution)/shard_map/ppermute | solution.py:23
  17.5 6.5 %all-to-all-start = ((bf16[16,64,1024]{2,1,0:T(8,128)(2,1)}), bf16[16,64,1024]{2,1,0:T(8,128)(2,1)S(1)}, u32[]{:S(2)}, u32[]{:S(2)}) async-start(bf16[16,64,1024]{2,1,0:T(8,128)(2,1)} %bitcast.40), calls=%async_computation | async-start | bytes 4194304 | tf_op jit(solution)/shard_map/all_to_all | solution.py:221
  24.0 9.1 %collective-permute-done.4 = bf16[1,512,256]{2,1,0:T(8,128)(2,1)} collective-permute-done((bf16[1,512,256]{2,1,0:T(8,128)(2,1)S(1)}, bf16[1,512,256]{2,1,0:T(8,128)(2,1)}, u32[]{:S(2)}, u32[]{:S(2)}) %collective-permute-start.4) | collective-permute-done | bytes 262176 | tf_op jit(solution)/shard_map/ppermute | solution.py:23
  33.1 5.6 %attention_grads.1 = (bf16[128,2048]{1,0:T(8,128)(2,1)}, bf16[512,256]{1,0:T(8,128)(2,1)S(1)}, bf16[512,256]{1,0:T(8,128)(2,1)S(1)}, bf16[512,256]{1,0:T(8,128)(2,1)S(1)}, bf16[512,256]{1,0:T(8,128)(2,1)S(1)}) custom-call(s32[1]{0:T(128)} %bitcast.2.me, s32[32]{0:T(128)S(1)} %copy-done.2, s32[16]{0:T(128)S(1)} %bitcast.39, bf16[128,2048]{1,0:T(8,128)(2,1)S(1)} %bitcast.38, ...), custom_call_target="tpu_custom_call" | custom-call | flops 60000002048 | tf_op jit(solution)/shard_map/attention_grads/pallas_call | solution.py:131
  38.8 2.9 %collective-permute-start.6 = (bf16[512,256]{1,0:T(8,128)(2,1)S(1)}, bf16[512,256]{1,0:T(8,128)(2,1)S(1)}, u32[]{:S(2)}, u32[]{:S(2)}) collective-permute-start(bf16[512,256]{1,0:T(8,128)(2,1)S(1)} %get-tuple-element.16), channel_id=1, source_target_pairs={{0,2},{2,0},{4,6},{6,4},{8,10},{10,8},{12,14},{14,12},{16,18},{18,... | collective-permute-start | bytes 786440 | tf_op jit(solution)/shard_map/ppermute | solution.py:23
  42.1 1.5 %collective-permute-start.8 = (bf16[512,256]{1,0:T(8,128)(2,1)S(1)}, bf16[512,256]{1,0:T(8,128)(2,1)S(1)}, u32[]{:S(2)}, u32[]{:S(2)}) collective-permute-start(bf16[512,256]{1,0:T(8,128)(2,1)S(1)} %get-tuple-element.18), channel_id=1, source_target_pairs={{0,6},{2,4},{4,2},{6,0},{8,14},{10,12},{12,10},{14,8},{16,22},{18,... | collective-permute-start | bytes 786440 | tf_op jit(solution)/shard_map/ppermute | solution.py:23
  43.5 13.4 %collective-permute-done.6 = bf16[512,256]{1,0:T(8,128)(2,1)S(1)} collective-permute-done((bf16[512,256]{1,0:T(8,128)(2,1)S(1)}, bf16[512,256]{1,0:T(8,128)(2,1)S(1)}, u32[]{:S(2)}, u32[]{:S(2)}) %collective-permute-start.6) | collective-permute-done | bytes 262176 | tf_op jit(solution)/shard_map/ppermute | solution.py:23
  56.9 3.0 %collective-permute-done.8 = bf16[512,256]{1,0:T(8,128)(2,1)S(1)} collective-permute-done((bf16[512,256]{1,0:T(8,128)(2,1)S(1)}, bf16[512,256]{1,0:T(8,128)(2,1)S(1)}, u32[]{:S(2)}, u32[]{:S(2)}) %collective-permute-start.8) | collective-permute-done | bytes 262176 | tf_op jit(solution)/shard_map/ppermute | solution.py:23
  60.0 10.0 %collective-permute-start.10 = (bf16[128,256]{1,0:T(8,128)(2,1)S(1)}, bf16[128,256]{1,0:T(8,128)(2,1)S(1)}, u32[]{:S(2)}, u32[]{:S(2)}) collective-permute-start(bf16[128,256]{1,0:T(8,128)(2,1)S(1)} %get-tuple-element.27), channel_id=1, source_target_pairs={{0,16},{2,18},{4,20},{6,22},{8,24},{10,26},{12,28},{14,30},{16,0},... | collective-permute-start | bytes 196616 | tf_op jit(solution)/shard_map/ppermute | solution.py:23
  70.0 0.6 collective-permute-start.9
  70.7 4.2 %collective-permute-done.10 = bf16[128,256]{1,0:T(8,128)(2,1)S(1)} collective-permute-done((bf16[128,256]{1,0:T(8,128)(2,1)S(1)}, bf16[128,256]{1,0:T(8,128)(2,1)S(1)}, u32[]{:S(2)}, u32[]{:S(2)}) %collective-permute-start.10) | collective-permute-done | bytes 65568 | tf_op jit(solution)/shard_map/ppermute | solution.py:23
  74.8 1.3 %collective-permute-done.11 = bf16[128,256]{1,0:T(8,128)(2,1)S(1)} collective-permute-done((bf16[128,256]{1,0:T(8,128)(2,1)S(1)}, bf16[128,256]{1,0:T(8,128)(2,1)S(1)}, u32[]{:S(2)}, u32[]{:S(2)}) %collective-permute-start.11) | collective-permute-done | bytes 65568 | tf_op jit(solution)/shard_map/ppermute | solution.py:23
  76.3 2.9 %collective-permute-start.13 = (bf16[128,256]{1,0:T(8,128)(2,1)S(1)}, bf16[128,256]{1,0:T(8,128)(2,1)S(1)}, u32[]{:S(2)}, u32[]{:S(2)}) collective-permute-start(bf16[128,256]{1,0:T(8,128)(2,1)S(1)} %fusion.3), channel_id=1, source_target_pairs={{0,16},{2,18},{4,20},{6,22},{8,24},{10,26},{12,28},{14,30},{16,0},... | collective-permute-start | bytes 196616 | tf_op jit(solution)/shard_map/ppermute | solution.py:23
  79.2 1.5 %collective-permute-start.14 = (bf16[128,256]{1,0:T(8,128)(2,1)S(1)}, bf16[128,256]{1,0:T(8,128)(2,1)S(1)}, u32[]{:S(2)}, u32[]{:S(2)}) collective-permute-start(bf16[128,256]{1,0:T(8,128)(2,1)S(1)} %fusion.3), channel_id=1, source_target_pairs={{0,24},{2,26},{4,28},{6,30},{8,16},{10,18},{12,20},{14,22},{16,8},... | collective-permute-start | bytes 196616 | tf_op jit(solution)/shard_map/ppermute | solution.py:23
  80.7 0.9 collective-permute-done.13
  81.5 3.7 %collective-permute-done.14 = bf16[128,256]{1,0:T(8,128)(2,1)S(1)} collective-permute-done((bf16[128,256]{1,0:T(8,128)(2,1)S(1)}, bf16[128,256]{1,0:T(8,128)(2,1)S(1)}, u32[]{:S(2)}, u32[]{:S(2)}) %collective-permute-start.14) | collective-permute-done | bytes 65568 | tf_op jit(solution)/shard_map/ppermute | solution.py:23
  85.4 1.3 %collective-permute-start.18 = (bf16[512,256]{1,0:T(8,128)(2,1)S(1)}, bf16[512,256]{1,0:T(8,128)(2,1)S(1)}, u32[]{:S(2)}, u32[]{:S(2)}) collective-permute-start(bf16[512,256]{1,0:T(8,128)(2,1)S(1)} %pad_maximum_fusion.1.refs_0_), channel_id=1, source_target_pairs={{0,2},{2,0},{4,6},{6,4},{8,10},{10,8},{12,14},{14,12},{16,18},{18,... | collective-permute-start | bytes 786440 | tf_op jit(solution)/shard_map/ppermute | solution.py:23
  86.7 0.6 collective-permute-start.15
  87.2 1.7 %collective-permute-start.16 = (bf16[512,256]{1,0:T(8,128)(2,1)S(1)}, bf16[512,256]{1,0:T(8,128)(2,1)S(1)}, u32[]{:S(2)}, u32[]{:S(2)}) collective-permute-start(bf16[512,256]{1,0:T(8,128)(2,1)S(1)} %pad_maximum_fusion.1.refs_0_), channel_id=1, source_target_pairs={{0,6},{2,4},{4,2},{6,0},{8,14},{10,12},{12,10},{14,8},{16,22},{18,... | collective-permute-start | bytes 786440 | tf_op jit(solution)/shard_map/ppermute | solution.py:23
  89.0 0.6 collective-permute-done.17
  89.7 2.1 %weight_step.3.refs_3_ = f32[256,1024]{1,0:T(8,128)S(1)} custom-call(s32[2]{0:T(128)S(1)} %pad_add_fusion.1.place, bf16[512,256]{1,0:T(8,128)(2,1)S(1)} %pad_maximum_fusion.1.refs_0_, bf16[4,4,64,1024]{3,2,1,0:T(8,128)(2,1)S(1)} %bitcast.32, bf16[4,4,64,1024]{3,2,1,0:T(8,128)(2,1)} %bitcast.16.refs_2_.refs_3_), custom_call_target="tpu_custom_call" | custom-call | tf_op jit(solution)/shard_map/weight_step/pallas_call | solution.py:184
  91.7 2.8 %collective-permute-done.18.refs_0_ = bf16[512,256]{1,0:T(8,128)(2,1)S(1)} collective-permute-done((bf16[512,256]{1,0:T(8,128)(2,1)S(1)}, bf16[512,256]{1,0:T(8,128)(2,1)S(1)}, u32[]{:S(2)}, u32[]{:S(2)}) %collective-permute-start.18) | collective-permute-done | bytes 262176 | tf_op jit(solution)/shard_map/ppermute | solution.py:23
  94.6 2.1 %weight_step.4.refs_4_ = f32[256,1024]{1,0:T(8,128)S(1)} custom-call(s32[2]{0:T(128)S(1)} %pad_add_fusion.1.place, bf16[512,256]{1,0:T(8,128)(2,1)S(1)} %collective-permute-done.18.refs_0_, bf16[4,4,64,1024]{3,2,1,0:T(8,128)(2,1)S(1)} %bitcast.33, bf16[4,4,64,1024]{3,2,1,0:T(8,128)(2,1)} %bitcast.16.refs_2_.refs_3_, f32[256,1024]{1,0:T(8,128)S(1)} %weight_step.3.refs_3_), custom_call_target="tpu_custom_call" | custom-call | tf_op jit(solution)/shard_map/weight_step/pallas_call | solution.py:184
  96.6 4.0 %collective-permute-done.15.refs_0_ = bf16[512,256]{1,0:T(8,128)(2,1)S(1)} collective-permute-done((bf16[512,256]{1,0:T(8,128)(2,1)S(1)}, bf16[512,256]{1,0:T(8,128)(2,1)S(1)}, u32[]{:S(2)}, u32[]{:S(2)}) %collective-permute-start.15) | collective-permute-done | bytes 262176 | tf_op jit(solution)/shard_map/ppermute | solution.py:23
  100.7 3.4 %weight_step.5 = (f32[1024,128]{1,0:T(8,128)}, f32[1024,128]{1,0:T(8,128)}) custom-call(s32[2]{0:T(128)S(1)} %pad_add_fusion.1.place, bf16[512,256]{1,0:T(8,128)(2,1)S(1)} %collective-permute-done.15.refs_0_, bf16[512,256]{1,0:T(8,128)(2,1)S(1)} %collective-permute-done.16.refs_1_, bf16[4,4,64,1024]{3,2,1,0:T(8,128)(2,1)S(1)} %bitcast.34, ...), custom_call_target="tpu_custom_call" | custom-call | tf_op jit(solution)/shard_map/weight_step/pallas_call | solution.py:184
  (37 shorter events, 2.1 us)
Async XLA Ops:
  1.4 11.0 %collective-permute-start = (bf16[1,128,256]{2,1,0:T(8,128)(2,1)S(1)}, bf16[1,128,256]{2,1,0:T(8,128)(2,1)S(1)}, u32[]{:S(2)}, u32[]{:S(2)}) collective-permute-start(bf16[1,128,256]{2,1,0:T(8,128)(2,1)S(1)} %pad_add_fusion), channel_id=1, source_target_pairs={{0,8},{2,10},{4,12},{6,14},{8,0},{10,2},{12,4},{14,6},{16,24},{18,... | collective-permute-start | bytes 196616 | tf_op jit(solution)/shard_map/ppermute | solution.py:23
  4.5 7.9 %collective-permute-start.1 = (bf16[1,128,256]{2,1,0:T(8,128)(2,1)S(1)}, bf16[1,128,256]{2,1,0:T(8,128)(2,1)S(1)}, u32[]{:S(2)}, u32[]{:S(2)}) collective-permute-start(bf16[1,128,256]{2,1,0:T(8,128)(2,1)S(1)} %pad_add_fusion), channel_id=1, source_target_pairs={{0,16},{2,18},{4,20},{6,22},{8,24},{10,26},{12,28},{14,30},{16,0},... | collective-permute-start | bytes 196616 | tf_op jit(solution)/shard_map/ppermute | solution.py:23
  7.1 6.1 %collective-permute-start.2 = (bf16[1,128,256]{2,1,0:T(8,128)(2,1)S(1)}, bf16[1,128,256]{2,1,0:T(8,128)(2,1)S(1)}, u32[]{:S(2)}, u32[]{:S(2)}) collective-permute-start(bf16[1,128,256]{2,1,0:T(8,128)(2,1)S(1)} %pad_add_fusion), channel_id=1, source_target_pairs={{0,24},{2,26},{4,28},{6,30},{8,16},{10,18},{12,20},{14,22},{16,8},... | collective-permute-start | bytes 196616 | tf_op jit(solution)/shard_map/ppermute | solution.py:23
  9.9 6.9 %copy-start = (bf16[1,128,2048]{2,1,0:T(8,128)(2,1)S(1)}, bf16[1,128,2048]{2,1,0:T(8,128)(2,1)}, u32[]{:S(2)}) copy-start(bf16[1,128,2048]{2,1,0:T(8,128)(2,1)} %param.12) | copy-start | bytes 1572868
  9.9 7.0 %copy-start.4 = (bf16[1,128,2048]{2,1,0:T(8,128)(2,1)S(1)}, bf16[1,128,2048]{2,1,0:T(8,128)(2,1)}, u32[]{:S(2)}) copy-start(bf16[1,128,2048]{2,1,0:T(8,128)(2,1)} %param.11) | copy-start | bytes 1572868
  13.2 10.8 %collective-permute-start.3 = (bf16[1,512,256]{2,1,0:T(8,128)(2,1)S(1)}, bf16[1,512,256]{2,1,0:T(8,128)(2,1)}, u32[]{:S(2)}, u32[]{:S(2)}) collective-permute-start(bf16[1,512,256]{2,1,0:T(8,128)(2,1)S(1)} %pad_maximum_fusion), channel_id=1, source_target_pairs={{0,2},{2,0},{4,6},{6,4},{8,10},{10,8},{12,14},{14,12},{16,18},{18,... | collective-permute-start | bytes 786440 | tf_op jit(solution)/shard_map/ppermute | solution.py:23
  14.7 18.4 %collective-permute-start.4 = (bf16[1,512,256]{2,1,0:T(8,128)(2,1)S(1)}, bf16[1,512,256]{2,1,0:T(8,128)(2,1)}, u32[]{:S(2)}, u32[]{:S(2)}) collective-permute-start(bf16[1,512,256]{2,1,0:T(8,128)(2,1)S(1)} %pad_maximum_fusion), channel_id=1, source_target_pairs={{0,4},{2,6},{4,0},{6,2},{8,12},{10,14},{12,8},{14,10},{16,20},{18,... | collective-permute-start | bytes 786440 | tf_op jit(solution)/shard_map/ppermute | solution.py:23
  16.3 16.9 %collective-permute-start.5 = (bf16[1,512,256]{2,1,0:T(8,128)(2,1)S(1)}, bf16[1,512,256]{2,1,0:T(8,128)(2,1)}, u32[]{:S(2)}, u32[]{:S(2)}) collective-permute-start(bf16[1,512,256]{2,1,0:T(8,128)(2,1)S(1)} %pad_maximum_fusion), channel_id=1, source_target_pairs={{0,6},{2,4},{4,2},{6,0},{8,14},{10,12},{12,10},{14,8},{16,22},{18,... | collective-permute-start | bytes 786440 | tf_op jit(solution)/shard_map/ppermute | solution.py:23
  17.5 15.6 %copy-start.1 = (bf16[1,128,2048]{2,1,0:T(8,128)(2,1)S(1)}, bf16[1,128,2048]{2,1,0:T(8,128)(2,1)}, u32[]{:S(2)}) copy-start(bf16[1,128,2048]{2,1,0:T(8,128)(2,1)} %param.8) | copy-start | bytes 1572868
  17.5 15.6 %copy-start.2 = (s32[32]{0:T(128)S(1)}, s32[32]{0:T(128)}, u32[]{:S(2)}) copy-start(s32[32]{0:T(128)} %slots.1) | copy-start | bytes 388
  17.5 15.6 %copy-start.3 = (s32[1,16]{1,0:T(1,128)S(1)}, s32[1,16]{1,0:T(1,128)}, u32[]{:S(2)}) copy-start(s32[1,16]{1,0:T(1,128)} %param.14) | copy-start | bytes 196
  17.5 67.8 %all-to-all-start = ((bf16[16,64,1024]{2,1,0:T(8,128)(2,1)}), bf16[16,64,1024]{2,1,0:T(8,128)(2,1)S(1)}, u32[]{:S(2)}, u32[]{:S(2)}) async-start(bf16[16,64,1024]{2,1,0:T(8,128)(2,1)} %bitcast.40), calls=%async_computation | async-start | bytes 4194304 | tf_op jit(solution)/shard_map/all_to_all | solution.py:221
  38.8 18.1 %collective-permute-start.6 = (bf16[512,256]{1,0:T(8,128)(2,1)S(1)}, bf16[512,256]{1,0:T(8,128)(2,1)S(1)}, u32[]{:S(2)}, u32[]{:S(2)}) collective-permute-start(bf16[512,256]{1,0:T(8,128)(2,1)S(1)} %get-tuple-element.16), channel_id=1, source_target_pairs={{0,2},{2,0},{4,6},{6,4},{8,10},{10,8},{12,14},{14,12},{16,18},{18,... | collective-permute-start | bytes 786440 | tf_op jit(solution)/shard_map/ppermute | solution.py:23
  41.7 15.2 %collective-permute-start.7 = (bf16[512,256]{1,0:T(8,128)(2,1)S(1)}, bf16[512,256]{1,0:T(8,128)(2,1)S(1)}, u32[]{:S(2)}, u32[]{:S(2)}) collective-permute-start(bf16[512,256]{1,0:T(8,128)(2,1)S(1)} %get-tuple-element.17), channel_id=1, source_target_pairs={{0,4},{2,6},{4,0},{6,2},{8,12},{10,14},{12,8},{14,10},{16,20},{18,... | collective-permute-start | bytes 786440 | tf_op jit(solution)/shard_map/ppermute | solution.py:23
  42.1 17.8 %collective-permute-start.8 = (bf16[512,256]{1,0:T(8,128)(2,1)S(1)}, bf16[512,256]{1,0:T(8,128)(2,1)S(1)}, u32[]{:S(2)}, u32[]{:S(2)}) collective-permute-start(bf16[512,256]{1,0:T(8,128)(2,1)S(1)} %get-tuple-element.18), channel_id=1, source_target_pairs={{0,6},{2,4},{4,2},{6,0},{8,14},{10,12},{12,10},{14,8},{16,22},{18,... | collective-permute-start | bytes 786440 | tf_op jit(solution)/shard_map/ppermute | solution.py:23
  60.0 14.8 %collective-permute-start.10 = (bf16[128,256]{1,0:T(8,128)(2,1)S(1)}, bf16[128,256]{1,0:T(8,128)(2,1)S(1)}, u32[]{:S(2)}, u32[]{:S(2)}) collective-permute-start(bf16[128,256]{1,0:T(8,128)(2,1)S(1)} %get-tuple-element.27), channel_id=1, source_target_pairs={{0,16},{2,18},{4,20},{6,22},{8,24},{10,26},{12,28},{14,30},{16,0},... | collective-permute-start | bytes 196616 | tf_op jit(solution)/shard_map/ppermute | solution.py:23
  70.0 6.2 %collective-permute-start.11 = (bf16[128,256]{1,0:T(8,128)(2,1)S(1)}, bf16[128,256]{1,0:T(8,128)(2,1)S(1)}, u32[]{:S(2)}, u32[]{:S(2)}) collective-permute-start(bf16[128,256]{1,0:T(8,128)(2,1)S(1)} %get-tuple-element.26), channel_id=1, source_target_pairs={{0,24},{2,26},{4,28},{6,30},{8,16},{10,18},{12,20},{14,22},{16,8},... | collective-permute-start | bytes 196616 | tf_op jit(solution)/shard_map/ppermute | solution.py:23
  70.0 6.2 %collective-permute-start.9 = (bf16[128,256]{1,0:T(8,128)(2,1)S(1)}, bf16[128,256]{1,0:T(8,128)(2,1)S(1)}, u32[]{:S(2)}, u32[]{:S(2)}) collective-permute-start(bf16[128,256]{1,0:T(8,128)(2,1)S(1)} %get-tuple-element.25), channel_id=1, source_target_pairs={{0,8},{2,10},{4,12},{6,14},{8,0},{10,2},{12,4},{14,6},{16,24},{18,... | collective-permute-start | bytes 196616 | tf_op jit(solution)/shard_map/ppermute | solution.py:23
  76.2 4.5 %collective-permute-start.12 = (bf16[128,256]{1,0:T(8,128)(2,1)S(1)}, bf16[128,256]{1,0:T(8,128)(2,1)S(1)}, u32[]{:S(2)}, u32[]{:S(2)}) collective-permute-start(bf16[128,256]{1,0:T(8,128)(2,1)S(1)} %fusion.3), channel_id=1, source_target_pairs={{0,8},{2,10},{4,12},{6,14},{8,0},{10,2},{12,4},{14,6},{16,24},{18,... | collective-permute-start | bytes 196616 | tf_op jit(solution)/shard_map/ppermute | solution.py:23
  76.3 5.2 %collective-permute-start.13 = (bf16[128,256]{1,0:T(8,128)(2,1)S(1)}, bf16[128,256]{1,0:T(8,128)(2,1)S(1)}, u32[]{:S(2)}, u32[]{:S(2)}) collective-permute-start(bf16[128,256]{1,0:T(8,128)(2,1)S(1)} %fusion.3), channel_id=1, source_target_pairs={{0,16},{2,18},{4,20},{6,22},{8,24},{10,26},{12,28},{14,30},{16,0},... | collective-permute-start | bytes 196616 | tf_op jit(solution)/shard_map/ppermute | solution.py:23
  79.2 6.1 %collective-permute-start.14 = (bf16[128,256]{1,0:T(8,128)(2,1)S(1)}, bf16[128,256]{1,0:T(8,128)(2,1)S(1)}, u32[]{:S(2)}, u32[]{:S(2)}) collective-permute-start(bf16[128,256]{1,0:T(8,128)(2,1)S(1)} %fusion.3), channel_id=1, source_target_pairs={{0,24},{2,26},{4,28},{6,30},{8,16},{10,18},{12,20},{14,22},{16,8},... | collective-permute-start | bytes 196616 | tf_op jit(solution)/shard_map/ppermute | solution.py:23
  85.3 4.4 %collective-permute-start.17 = (bf16[16,64,1024]{2,1,0:T(8,128)(2,1)S(1)}, bf16[16,64,1024]{2,1,0:T(8,128)(2,1)}, u32[]{:S(2)}, u32[]{:S(2)}) collective-permute-start(bf16[16,64,1024]{2,1,0:T(8,128)(2,1)S(1)} %all-to-all-done), channel_id=1, source_target_pairs={{0,1},{1,0},{2,3},{3,2},{4,5},{5,4},{6,7},{7,6},{8,9},{9,8},{10,11... | collective-permute-start | bytes 6291464 | tf_op jit(solution)/shard_map/ppermute | solution.py:248
  85.4 9.2 %collective-permute-start.18 = (bf16[512,256]{1,0:T(8,128)(2,1)S(1)}, bf16[512,256]{1,0:T(8,128)(2,1)S(1)}, u32[]{:S(2)}, u32[]{:S(2)}) collective-permute-start(bf16[512,256]{1,0:T(8,128)(2,1)S(1)} %pad_maximum_fusion.1.refs_0_), channel_id=1, source_target_pairs={{0,2},{2,0},{4,6},{6,4},{8,10},{10,8},{12,14},{14,12},{16,18},{18,... | collective-permute-start | bytes 786440 | tf_op jit(solution)/shard_map/ppermute | solution.py:23
  86.7 14.0 %collective-permute-start.15 = (bf16[512,256]{1,0:T(8,128)(2,1)S(1)}, bf16[512,256]{1,0:T(8,128)(2,1)S(1)}, u32[]{:S(2)}, u32[]{:S(2)}) collective-permute-start(bf16[512,256]{1,0:T(8,128)(2,1)S(1)} %pad_maximum_fusion.1.refs_0_), channel_id=1, source_target_pairs={{0,4},{2,6},{4,0},{6,2},{8,12},{10,14},{12,8},{14,10},{16,20},{18,... | collective-permute-start | bytes 786440 | tf_op jit(solution)/shard_map/ppermute | solution.py:23
  87.2 13.4 %collective-permute-start.16 = (bf16[512,256]{1,0:T(8,128)(2,1)S(1)}, bf16[512,256]{1,0:T(8,128)(2,1)S(1)}, u32[]{:S(2)}, u32[]{:S(2)}) collective-permute-start(bf16[512,256]{1,0:T(8,128)(2,1)S(1)} %pad_maximum_fusion.1.refs_0_), channel_id=1, source_target_pairs={{0,6},{2,4},{4,2},{6,0},{8,14},{10,12},{12,10},{14,8},{16,22},{18,... | collective-permute-start | bytes 786440 | tf_op jit(solution)/shard_map/ppermute | solution.py:23
